TPU v7x, 128 devices: a whole 4x4x4 slice. The times are simulated.
128 devices in a mesh: dp: 32 (over x, z, y_lo), frame: 4 (over y_hi, core).
Axes of the slice: x: 4, y: 4 (y_hi: 2, y_lo: 2; y = y_hi * 2 + y_lo), z: 4, core: 2. Of those that a mesh axis runs over, the one named last changes fastest.
Arguments:
- hidden_in: bfloat16 [32768, 1280], P(('dp', 'frame')), may hold values from -24 to 24
- rec_lengths: int32 [32, 3], P('dp'), may hold values from 1 to 512, 1024 in all within a row
- token_positions: int32 [32768], P('dp'), may hold values from 0 to 1535, as said below
- thinker_grad: bfloat16 [49152, 1280], P(('dp', 'frame')), may hold values from -6 to 6
- norm_gain: float32 [1280], replicated, may hold values from 0.25 to 1.75
- norm_bias: float32 [1280], replicated, may hold values from -3 to 3
- qkv_weight: bfloat16 [1280, 3, 1280], P('dp', None, 'frame'), may hold values from -10 to 10
Outputs:
- hidden_grad: bfloat16 [32768, 1280], P(('dp', 'frame'))
- weight_grad: float32 [1280, 3, 1280], P('dp', None, 'frame')
Inputs may be any that keep to these rules, and one draw needn't show every extreme that they name: `token_positions`: within each block of 1024 entries the positions increase strictly; the first is 0 and the last is 1535.
All inputs are finite; a program needn't handle non-finite values.
Results may differ from a plain program's by a relative error of at most 0.025.
The roundings to bfloat16 on the way count: a program that leaves them out, or rounds other values in their place, can miss the bound.
Values may be sent and summed in bfloat16 or wider, within the bound.
No kernel may reach another device: no remote copies, remote signals or barrier semaphores. Data moves between devices by JAX's collectives and lax.ppermute only.
A program may use at most 128 MiB of HBM per device.

v0:
```python
import math

import jax
import jax.numpy as jnp
from jax import lax
from jax.sharding import PartitionSpec as P

HD = 64


norm_eps = 1e-05


def norm_forward(rows, gain, bias):
    rows_f32 = rows.astype(jnp.float32)
    mean_row = jnp.mean(rows_f32, axis=-1, keepdims=True)
    centered = rows_f32 - mean_row
    variance = jnp.mean(centered * centered, axis=-1, keepdims=True)
    inv_std = lax.rsqrt(variance + norm_eps)
    standard = centered * inv_std
    normalized = (standard * gain + bias).astype(jnp.bfloat16)
    return (normalized, standard, inv_std)


def norm_backward(norm_grad, standard, inv_std, gain):
    scaled = norm_grad * gain
    result = inv_std * (
        scaled
        - jnp.mean(scaled, axis=-1, keepdims=True)
        - standard * jnp.mean(scaled * standard, axis=-1, keepdims=True)
    )
    return result.astype(jnp.bfloat16)


def segment_ids(lengths, count):
    ends = jnp.cumsum(lengths)
    frame_ids = jnp.arange(count, dtype=jnp.int32)
    return jnp.sum((frame_ids[:, None] >= ends[None, :]).astype(jnp.int32), axis=1)


def head_pass(queries, keys_in, values, out_grad, segments, score_scale, block_rows):
    length = queries.shape[0]
    head_size = queries.shape[1]

    def step(totals, first_row):
        key_total, value_total = totals
        query_rows = lax.dynamic_slice_in_dim(queries, first_row, block_rows, 0)
        grad_rows = lax.dynamic_slice_in_dim(out_grad, first_row, block_rows, 0)
        seg_rows = lax.dynamic_slice_in_dim(segments, first_row, block_rows, 0)
        scores = jnp.einsum("qd,kd->qk", query_rows, keys_in, preferred_element_type=jnp.float32)
        same_rec = seg_rows[:, None] == segments[None, :]
        scores = jnp.where(same_rec, scores * score_scale, -1e30)
        row_max = jnp.max(scores, axis=-1, keepdims=True)
        expo = jnp.where(same_rec, jnp.exp(scores - row_max), 0.0)
        attn_weights = expo / jnp.sum(expo, axis=-1, keepdims=True)
        weight_grads = jnp.einsum(
            "qd,kd->qk", grad_rows, values, preferred_element_type=jnp.float32
        )
        row_dot = jnp.sum(attn_weights * weight_grads, axis=-1, keepdims=True)
        score_grad = (attn_weights * (weight_grads - row_dot)).astype(jnp.bfloat16)
        weights_low = attn_weights.astype(jnp.bfloat16)
        value_total = value_total + jnp.einsum(
            "qk,qd->kd", weights_low, grad_rows, preferred_element_type=jnp.float32
        )
        key_total = key_total + jnp.einsum(
            "qk,qd->kd", score_grad, query_rows, preferred_element_type=jnp.float32
        )
        query_grad = jnp.einsum(
            "qk,kd->qd", score_grad, keys_in, preferred_element_type=jnp.float32
        )
        return ((key_total, value_total), (query_grad * score_scale).astype(jnp.bfloat16))

    starts = jnp.arange(length // block_rows, dtype=jnp.int32) * block_rows
    zero_acc = jnp.zeros((length, head_size), jnp.float32)
    (key_total, value_total), query_grad = lax.scan(step, (zero_acc, zero_acc), starts)
    query_grad = query_grad.reshape(length, head_size)
    return (
        query_grad,
        (key_total * score_scale).astype(jnp.bfloat16),
        value_total.astype(jnp.bfloat16),
    )


def attention_grads(projected, out_grad, segments):
    length = projected.shape[0]
    head_cols = projected.shape[2]
    local_heads = head_cols // HD
    block_rows = math.gcd(length, 512)
    score_scale = HD ** (-0.5)

    def split_heads(block):
        return jnp.transpose(block.reshape(length, local_heads, HD), (1, 0, 2))

    def one_head(items):
        return head_pass(items[0], items[1], items[2], items[3], segments, score_scale, block_rows)

    grads = lax.map(
        one_head,
        (
            split_heads(projected[:, 0]),
            split_heads(projected[:, 1]),
            split_heads(projected[:, 2]),
            split_heads(out_grad),
        ),
    )
    merged = [jnp.transpose(item, (1, 0, 2)).reshape(length, head_cols) for item in grads]
    return jnp.stack(merged, axis=1)


def per_device(
    hidden_in, rec_lengths, token_positions, thinker_grad, norm_gain, norm_bias, qkv_weight
):
    frame_count = lax.axis_size("frame")
    local_rows = hidden_in.shape[0]
    width = hidden_in.shape[1]
    head_cols = qkv_weight.shape[2]
    group_frames = token_positions.shape[0]
    think_rows = thinker_grad.shape[0]
    normalized, standard, inv_std = norm_forward(hidden_in, norm_gain, norm_bias)
    segments = segment_ids(rec_lengths[0], group_frames)
    moved = lax.all_to_all(
        thinker_grad.reshape(think_rows, frame_count, head_cols),
        "frame",
        split_axis=1,
        concat_axis=0,
        tiled=True,
    )
    moved = moved.reshape(frame_count * think_rows, head_cols)
    out_grad = jnp.take(moved, token_positions, axis=0)
    wide_rows = lax.all_gather(qkv_weight, "frame", axis=2, tiled=True)
    piece = lax.all_gather(wide_rows, "dp", axis=0, tiled=True)
    count = piece.shape[0]
    columns = normalized
    projected = jnp.dot(
        columns, piece.reshape(count, 3 * width), preferred_element_type=jnp.float32
    )
    projected = projected.astype(jnp.bfloat16).reshape(local_rows, 3, frame_count, head_cols)
    by_heads = lax.all_to_all(projected, "frame", split_axis=2, concat_axis=0, tiled=True)
    by_heads = by_heads.reshape(group_frames, 3, head_cols)
    proj_grad = attention_grads(by_heads, out_grad, segments)
    proj_grad = lax.all_to_all(
        proj_grad.reshape(group_frames, 3, 1, head_cols),
        "frame",
        split_axis=0,
        concat_axis=2,
        tiled=True,
    )
    grad_flat = proj_grad.reshape(local_rows, 3 * width)
    piece = lax.all_gather(wide_rows, "dp", axis=0, tiled=True)
    count = piece.shape[0]
    norm_grad = lax.dot_general(
        grad_flat,
        piece.reshape(count, 3 * width),
        (((1,), (1,)), ((), ())),
        preferred_element_type=jnp.float32,
    )
    columns = normalized
    term = lax.dot_general(
        columns, grad_flat, (((0,), (0,)), ((), ())), preferred_element_type=jnp.float32
    )
    summed = lax.psum_scatter(
        term.reshape(qkv_weight.shape[0] * lax.axis_size("dp"), 3, width).astype(jnp.bfloat16),
        "dp",
        scatter_dimension=0,
        tiled=True,
    )
    weight_grad = lax.psum_scatter(summed, "frame", scatter_dimension=2, tiled=True).astype(
        jnp.float32
    )
    hidden_grad = norm_backward(norm_grad, standard, inv_std, norm_gain)
    return (hidden_grad, weight_grad)


def solution(mesh):
    placed = (
        P(("dp", "frame"), None),
        P("dp", None),
        P("dp"),
        P(("dp", "frame"), None),
        P(),
        P(),
        P("dp", None, "frame"),
    )
    return jax.shard_map(
        per_device,
        mesh=mesh,
        in_specs=placed,
        out_specs=(P(("dp", "frame"), None), P("dp", None, "frame")),
        check_vma=False,
    )
```

profile of v0, /device:TPU:1, one launch (start us, length us, event | category | flops | bytes accessed | tf_op | source)
XLA Modules:
  0.0 808.5 jit_solution(9008442061331394872)
XLA Ops:
  8.4 14.5 %all_gather.7 = bf16[40,3,1280]{0,1,2:T(4,128)(2,1)S(1)} all-gather(bf16[40,3,320]{0,1,2:T(4,128)(2,1)S(1)} %copy.71), channel_id=1, replica_groups=mesh['dp'=32,'frame'=4] {'frame'}, dimensions={2}, use_global_device_ids=true | all-gather | bytes 384000 | tf_op jit(solution)/shard_map/all_gather | solution.py:130
  25.6 4.0 all-to-all-start.1
  30.2 218.2 %all-gather.2.cloned.1.call-done = bf16[1280,3,1280]{2,0,1:T(8,128)(2,1)} async-done(((bf16[40,3,1280]{2,0,1:T(8,128)(2,1)}), bf16[1280,3,1280]{2,0,1:T(8,128)(2,1)}) %all-gather.2.cloned.1.call-update) | async-done | bytes 9830416 | tf_op jit(solution)/shard_map/all_gather | solution.py:131
  248.4 13.8 %copy.73 = bf16[1280,3,1280]{0,2,1:T(8,128)(2,1)} copy(bf16[1280,3,1280]{2,0,1:T(8,128)(2,1)} %all-gather.2.cloned.1.call-done) | data formatting | bytes 19660800 | tf_op jit(solution)/shard_map/all_gather | solution.py:131
  262.2 11.4 %convolution_convert_fusion.1 = bf16[256,3840]{1,0:T(8,128)(2,1)} fusion(bf16[1280,3840]{0,1:T(8,128)(2,1)} %bitcast.107, bf16[256,1280]{1,0:T(8,128)(2,1)S(1)} %copy-done, f32[1280]{0:T(1024)S(1)} %copy-done.12, f32[1280]{0:T(1024)S(1)} %copy-done.10, f32[256]{0:T(256)S(1)} %add_rsqrt_fusion, f32[256]{0:T(256)S(1)} %broadcast_multiply_fusion.2), kind=kOutput, calls=%fused_computation.37 | convolution fusion | flops 2519531520 | bytes 12464128 | tf_op jit(solution)/shard_map/dot_general | solution.py:134
  278.7 7.5 all-to-all-start
  288.2 5.0 gather_fusion
  295.5 15.5 %all-to-all-done = bf16[256,3,4,320]{0,3,1,2:T(8,128)(2,1)S(1)} async-done(((bf16[256,3,4,320]{0,3,1,2:T(8,128)(2,1)}), bf16[256,3,4,320]{0,3,1,2:T(8,128)(2,1)S(1)}, u32[]{:S(2)}, u32[]{:S(2)}) %all-to-all-start) | async-done | bytes 1966112 | tf_op jit(solution)/shard_map/all_to_all | solution.py:138
  313.8 3.5 reshape.98
  318.6 160.5 %while.30 = (s32[]{:T(128)}, bf16[5,1024,64]{1,2,0:T(8,128)(2,1)}, bf16[5,1024,64]{1,2,0:T(8,128)(2,1)}, bf16[5,1024,64]{1,2,0:T(8,128)(2,1)}, bf16[5,1024,64]{1...) while((s32[]{:T(128)}, bf16[5,1024,64]{1,2,0:T(8,128)(2,1)}, ...), condition=%wide.region_10.11_spmd, body=%wide.region_4.10_spmd.sunk | while | flops 347601408 | bytes 25924080 | solution.py:97
  325.0 23.0 %while.31 = (s32[]{:T(128)}, f32[1024,64]{0,1:T(8,128)}, f32[1024,64]{0,1:T(8,128)}, bf16[2,512,64]{1,2,0:T(8,128)(2,1)S(1)}, s32[2]{0:T(128)S(1)}, /*index=5*/s...) while((s32[]{:T(128)}, f32[1024,64]{0,1:T(8,128)}, ...), condition=%wide.region_9.9_spmd.clone, body=%wide.region_5.8_spmd.clone.sunk | while | flops 347404800 | bytes 22253780 | solution.py:75
  357.1 23.0 %while.31 = (s32[]{:T(128)}, f32[1024,64]{0,1:T(8,128)}, f32[1024,64]{0,1:T(8,128)}, bf16[2,512,64]{1,2,0:T(8,128)(2,1)S(1)}, s32[2]{0:T(128)S(1)}, /*index=5*/s...) while((s32[]{:T(128)}, f32[1024,64]{0,1:T(8,128)}, ...), condition=%wide.region_9.9_spmd.clone, body=%wide.region_5.8_spmd.clone.sunk | while | flops 347404800 | bytes 22253780 | solution.py:75
  389.2 23.0 %while.31 = (s32[]{:T(128)}, f32[1024,64]{0,1:T(8,128)}, f32[1024,64]{0,1:T(8,128)}, bf16[2,512,64]{1,2,0:T(8,128)(2,1)S(1)}, s32[2]{0:T(128)S(1)}, /*index=5*/s...) while((s32[]{:T(128)}, f32[1024,64]{0,1:T(8,128)}, ...), condition=%wide.region_9.9_spmd.clone, body=%wide.region_5.8_spmd.clone.sunk | while | flops 347404800 | bytes 22253780 | solution.py:75
  421.3 23.0 %while.31 = (s32[]{:T(128)}, f32[1024,64]{0,1:T(8,128)}, f32[1024,64]{0,1:T(8,128)}, bf16[2,512,64]{1,2,0:T(8,128)(2,1)S(1)}, s32[2]{0:T(128)S(1)}, /*index=5*/s...) while((s32[]{:T(128)}, f32[1024,64]{0,1:T(8,128)}, ...), condition=%wide.region_9.9_spmd.clone, body=%wide.region_5.8_spmd.clone.sunk | while | flops 347404800 | bytes 22253780 | solution.py:75
  453.4 23.0 %while.31 = (s32[]{:T(128)}, f32[1024,64]{0,1:T(8,128)}, f32[1024,64]{0,1:T(8,128)}, bf16[2,512,64]{1,2,0:T(8,128)(2,1)S(1)}, s32[2]{0:T(128)S(1)}, /*index=5*/s...) while((s32[]{:T(128)}, f32[1024,64]{0,1:T(8,128)}, ...), condition=%wide.region_9.9_spmd.clone, body=%wide.region_5.8_spmd.clone.sunk | while | flops 347404800 | bytes 22253780 | solution.py:75
  482.1 4.8 copy.87
  486.9 41.7 %all_to_all.45 = bf16[1024,3,1,320]{3,1,2,0:T(4,128)(2,1)} all-to-all(bf16[1024,3,1,320]{3,1,2,0:T(4,128)(2,1)S(1)} %copy.87), channel_id=1, replica_groups=mesh['dp'=32,'frame'=4] {'frame'}, dimensions={0} | all-to-all | bytes 3932160 | tf_op jit(solution)/shard_map/all_to_all | solution.py:141
  528.6 4.5 copy.88
  533.1 5.6 fusion.19
  538.7 8.2 %copy.103 = bf16[3,160,8,1280]{3,2,0,1:T(8,128)(2,1)} copy(bf16[3,160,8,1280]{3,2,1,0:T(8,128)(2,1)} %fusion.19) | data formatting | bytes 19660800
  547.2 7.7 fusion.36
  554.9 209.1 %reduce-scatter.7.cloned.1.call-done = bf16[40,3840]{1,0:T(8,128)(2,1)} async-done(((bf16[1280,3840]{1,0:T(8,128)(2,1)}), bf16[40,3840]{1,0:T(8,128)(2,1)}) %reduce-scatter.7.cloned.1.call-update) | async-done | bytes 307216
  767.3 3.2 reshape.117
  771.8 28.2 %reduce-scatter.9.cloned.1.call-done = bf16[320,120]{1,0:T(8,128)(2,1)} async-done(((bf16[1280,120]{1,0:T(8,128)(2,1)}), bf16[320,120]{1,0:T(8,128)(2,1)}) %reduce-scatter.9.cloned.1.call-update) | async-done | bytes 76816
  (236 shorter events, 168.6 us)
Async XLA Ops:
  7.2 17.1 %copy-start.4 = (bf16[384,1280]{1,0:T(8,128)(2,1)S(1)}, bf16[384,1280]{1,0:T(8,128)(2,1)}, u32[]{:S(2)}) copy-start(bf16[384,1280]{1,0:T(8,128)(2,1)} %param.14) | copy-start | bytes 2949124
  7.2 241.2 %all-gather.2.cloned.1.call-start = ((), (), s32[]{:S(2)}) async-start(), calls=%async_computation.5 | async-start | bytes 10137600 | tf_op jit(solution)/shard_map/all_gather | solution.py:131
  24.2 5.4 copy-start
  25.6 252.2 %all-to-all-start.1 = ((bf16[384,4,320]{0,2,1:T(8,128)(2,1)}), bf16[384,4,320]{0,2,1:T(8,128)(2,1)S(1)}, u32[]{:S(2)}, u32[]{:S(2)}) async-start(bf16[384,4,320]{0,2,1:T(8,128)(2,1)} %bitcast.13), calls=%async_computation.1 | async-start | bytes 1966080 | tf_op jit(solution)/shard_map/all_to_all | solution.py:121
  29.8 232.4 %copy-start.5 = (f32[256]{0:T(256)}, f32[256]{0:T(256)S(1)}, u32[]{:S(2)}) copy-start(f32[256]{0:T(256)S(1)} %broadcast_multiply_fusion.2) | copy-start | bytes 3076
  30.1 232.1 %copy-start.8 = (f32[256]{0:T(256)}, f32[256]{0:T(256)S(1)}, u32[]{:S(2)}) copy-start(f32[256]{0:T(256)S(1)} %add_rsqrt_fusion) | copy-start | bytes 3076
  30.1 232.1 %copy-start.10 = (f32[1280]{0:T(1024)S(1)}, f32[1280]{0:T(1024)}, u32[]{:S(2)}) copy-start(f32[1280]{0:T(1024)} %param.15) | copy-start | bytes 15364
  30.1 232.1 %copy-start.12 = (f32[1280]{0:T(1024)S(1)}, f32[1280]{0:T(1024)}, u32[]{:S(2)}) copy-start(f32[1280]{0:T(1024)} %param.16) | copy-start | bytes 15364
  277.7 8.5 %copy-start.14 = (s32[1,3]{1,0:T(1,128)S(1)}, s32[1,3]{1,0:T(1,128)}, u32[]{:S(2)}) copy-start(s32[1,3]{1,0:T(1,128)} %param.12) | copy-start | bytes 40
  277.7 8.7 %copy-start.7 = (s32[1024]{0:T(1024)S(1)}, s32[1024]{0:T(1024)}, u32[]{:S(2)}) copy-start(s32[1024]{0:T(1024)} %param.13) | copy-start | bytes 12292
  277.7 1.0 copy-start.3
  278.7 32.3 %all-to-all-start = ((bf16[256,3,4,320]{0,3,1,2:T(8,128)(2,1)}), bf16[256,3,4,320]{0,3,1,2:T(8,128)(2,1)S(1)}, u32[]{:S(2)}, u32[]{:S(2)}) async-start(bf16[256,3,4,320]{0,3,1,2:T(8,128)(2,1)} %copy.75), calls=%async_computation | async-start | bytes 3932160 | tf_op jit(solution)/shard_map/all_to_all | solution.py:138
  286.2 477.8 %reduce-scatter.7.cloned.1.call-start = ((), (), s32[]{:S(2)}) async-start(), calls=%async_computation.6 | async-start | bytes 10137600
  528.5 4.5 copy-start.1
  528.5 4.5 copy-start.6
  528.6 4.5 copy-start.9
  528.6 4.5 copy-start.11
  528.6 4.5 copy-start.13
  546.9 253.1 %reduce-scatter.9.cloned.1.call-start = ((), (), s32[]{:S(2)}) async-start(), calls=%async_computation.7 | async-start | bytes 409600
  765.1 5.5 copy-start.2
Sparse Core Ops, SparseCore 0:
  24.4 223.9 all-gather.1
  547.0 216.9 reduce-scatter.6
  770.7 29.2 reduce-scatter.8
where the time goes:
time: 811 us; the launch traced here: 808 us
  waiting for transfers between devices  471 us (58%)
  local copies, waits for them, and re-layouts  107 us (13%)
  matrix products  104 us (13%)
  blocking collectives  56.1 us (7%)
  other arithmetic  25.1 us (3%)
  loops' own time  19.5 us (2%)
  between operations  14 us (2%)
  starting transfers between devices  11.8 us (1%)
    unnamed x5, waiting for transfers between devices  237 us
    all_gather x1, waiting for transfers between devices, per_device(): piece = lax.all_gather(wide_rows, 'dp', axis=0, tiled=True)  218 us
    all_to_all x1, blocking collectives, per_device(): lax.all_to_all(proj_grad.reshape(group_frames, 3, 1, head_cols), 'frame',...  41.7 us
    dynamic_slice x40, local copies, waits for them, and re-layouts, attention_grads(): lax.map(one_head, (split_heads(projected[:, 0]), split_heads(projected[:,...  31.8 us
    dot_general x10, matrix products, step(): jnp.einsum('qk,qd->kd', score_grad, query_rows, preferred_element_type=jn...  20.2 us
    dot_general x10, matrix products, step(): jnp.einsum('qk,qd->kd', weights_low, grad_rows, preferred_element_type=jn...  20.2 us
    dot_general x10, matrix products, step(): jnp.einsum('qd,kd->qk', grad_rows, values, preferred_element_type=jnp.flo...  19.6 us
    unnamed x38, local copies, waits for them, and re-layouts  19.5 us
  transfers between devices with their start and end apart: 5, of which 4 were waited for; matrix products, arithmetic and copies ran while one was open for 6% of the time, Pallas kernels for 0%

commit v1 on v0

--- a/solution.py
+++ b/solution.py
@@ -107,16 +107,49 @@
     return jnp.stack(merged, axis=1)
 
 
+FRAME_SIDE = [(0, 2), (1, 3), (2, 0), (3, 1)]
+FRAME_CORE = [(0, 1), (1, 0), (2, 3), (3, 2)]
+
+
+def gather_frames(rows):
+    core = lax.axis_index("frame") % 2
+    side = lax.axis_index("frame") // 2
+    far = lax.ppermute(rows, "frame", FRAME_SIDE)
+    mine = jnp.where(side == 0, jnp.stack([rows, far]), jnp.stack([far, rows]))
+    other = lax.ppermute(mine, "frame", FRAME_CORE)
+    pair = jnp.where(core == 0, jnp.stack([mine, other], axis=1), jnp.stack([other, mine], axis=1))
+    return pair.reshape(4 * rows.shape[0], rows.shape[1])
+
+
+def scatter_frames(total):
+    core = lax.axis_index("frame") % 2
+    side = lax.axis_index("frame") // 2
+    quarter = total.shape[0] // 4
+    blocks = total.reshape(2, 2, quarter, total.shape[1])
+    keep = lax.dynamic_index_in_dim(blocks, core, 1, keepdims=False)
+    give = lax.dynamic_index_in_dim(blocks, 1 - core, 1, keepdims=False).astype(jnp.bfloat16)
+    half = keep + lax.ppermute(give, "frame", FRAME_CORE).astype(jnp.float32)
+    keep = lax.dynamic_index_in_dim(half, side, 0, keepdims=False)
+    give = lax.dynamic_index_in_dim(half, 1 - side, 0, keepdims=False).astype(jnp.bfloat16)
+    return keep + lax.ppermute(give, "frame", FRAME_SIDE).astype(jnp.float32)
+
+
 def per_device(
     hidden_in, rec_lengths, token_positions, thinker_grad, norm_gain, norm_bias, qkv_weight
 ):
     frame_count = lax.axis_size("frame")
-    local_rows = hidden_in.shape[0]
+    groups = lax.axis_size("dp")
     width = hidden_in.shape[1]
+    own_rows = qkv_weight.shape[0]
     head_cols = qkv_weight.shape[2]
     group_frames = token_positions.shape[0]
     think_rows = thinker_grad.shape[0]
+    flat_weight = qkv_weight.reshape(own_rows, 3 * head_cols)
+    weight = lax.all_to_all(
+        jnp.broadcast_to(flat_weight[None], (groups, own_rows, 3 * head_cols)), "dp", 0, 0, tiled=True
+    ).reshape(width, 3 * head_cols)
     normalized, standard, inv_std = norm_forward(hidden_in, norm_gain, norm_bias)
+    normalized = gather_frames(normalized)
     segments = segment_ids(rec_lengths[0], group_frames)
     moved = lax.all_to_all(
         thinker_grad.reshape(think_rows, frame_count, head_cols),
@@ -127,46 +160,21 @@
     )
     moved = moved.reshape(frame_count * think_rows, head_cols)
     out_grad = jnp.take(moved, token_positions, axis=0)
-    wide_rows = lax.all_gather(qkv_weight, "frame", axis=2, tiled=True)
-    piece = lax.all_gather(wide_rows, "dp", axis=0, tiled=True)
-    count = piece.shape[0]
-    columns = normalized
-    projected = jnp.dot(
-        columns, piece.reshape(count, 3 * width), preferred_element_type=jnp.float32
+    projected = jnp.dot(normalized, weight, preferred_element_type=jnp.float32)
+    projected = projected.astype(jnp.bfloat16).reshape(group_frames, 3, head_cols)
+    proj_grad = attention_grads(projected, out_grad, segments)
+    grad_flat = proj_grad.reshape(group_frames, 3 * head_cols)
+    partial = lax.dot_general(
+        grad_flat, weight, (((1,), (1,)), ((), ())), preferred_element_type=jnp.float32
     )
-    projected = projected.astype(jnp.bfloat16).reshape(local_rows, 3, frame_count, head_cols)
-    by_heads = lax.all_to_all(projected, "frame", split_axis=2, concat_axis=0, tiled=True)
-    by_heads = by_heads.reshape(group_frames, 3, head_cols)
-    proj_grad = attention_grads(by_heads, out_grad, segments)
-    proj_grad = lax.all_to_all(
-        proj_grad.reshape(group_frames, 3, 1, head_cols),
-        "frame",
-        split_axis=0,
-        concat_axis=2,
-        tiled=True,
+    norm_grad = scatter_frames(partial)
+    term = lax.dot_general(
+        normalized, grad_flat, (((0,), (0,)), ((), ())), preferred_element_type=jnp.float32
     )
-    grad_flat = proj_grad.reshape(local_rows, 3 * width)
-    piece = lax.all_gather(wide_rows, "dp", axis=0, tiled=True)
-    count = piece.shape[0]
-    norm_grad = lax.dot_general(
-        grad_flat,
-        piece.reshape(count, 3 * width),
-        (((1,), (1,)), ((), ())),
-        preferred_element_type=jnp.float32,
+    terms = lax.all_to_all(
+        term.astype(jnp.bfloat16).reshape(groups, own_rows, 3 * head_cols), "dp", 0, 0, tiled=True
     )
-    columns = normalized
-    term = lax.dot_general(
-        columns, grad_flat, (((0,), (0,)), ((), ())), preferred_element_type=jnp.float32
-    )
-    summed = lax.psum_scatter(
-        term.reshape(qkv_weight.shape[0] * lax.axis_size("dp"), 3, width).astype(jnp.bfloat16),
-        "dp",
-        scatter_dimension=0,
-        tiled=True,
-    )
-    weight_grad = lax.psum_scatter(summed, "frame", scatter_dimension=2, tiled=True).astype(
-        jnp.float32
-    )
+    weight_grad = jnp.sum(terms.astype(jnp.float32), axis=0).reshape(own_rows, 3, head_cols)
     hidden_grad = norm_backward(norm_grad, standard, inv_std, norm_gain)
     return (hidden_grad, weight_grad)
 

time: 811 us -> 312 us (0.38)
  waiting for transfers between devices: 471 us -> 66.7 us
  blocking collectives: 56.1 us -> 0 us
  local copies, waits for them, and re-layouts: 107 us -> 60.8 us
  starting transfers between devices: 11.8 us -> 36.4 us
  matrix products: 104 us -> 87.2 us
  between operations: 14 us -> 0.97 us
  other arithmetic: 25.1 us -> 35.9 us
    unnamed x5 -> x0, waiting for transfers between devices: 237 us -> none
    all_gather x1 -> x0, waiting for transfers between devices: 218 us -> none  [per_device(): piece = lax.all_gather(wide_rows, 'dp', axis=0, tiled=True)]
    ppermute x0 -> x4, waiting for transfers between devices: none -> 53.4 us  [the longest x1 42 us: scatter_frames(): return keep + lax.ppermute(give, 'frame', FRAME_SIDE).astype(jnp.float32)]
    all_to_all x1 -> x0, blocking collectives: 41.7 us -> none  [per_device(): lax.all_to_all(proj_grad.reshape(group_frames, 3, 1, head_cols), 'frame',...]
    unnamed x38 -> x31, local copies, waits for them, and re-layouts: 19.5 us -> 3.1 us
    all_gather x2 -> x0, local copies, waits for them, and re-layouts: 15.1 us -> none  [the longest x1 13.8 us: per_device(): piece = lax.all_gather(wide_rows, 'dp', axis=0, tiled=True)]
    ppermute x0 -> x4, starting transfers between devices: none -> 14.8 us  [the longest x1 5.1 us: gather_frames(): other = lax.ppermute(mine, 'frame', FRAME_CORE)]
    all_gather x1 -> x0, blocking collectives: 14.5 us -> none  [per_device(): wide_rows = lax.all_gather(qkv_weight, 'frame', axis=2, tiled=True)]
  transfers between devices with their start and end apart: 5 -> 7, of which waited for: 4 -> 4; matrix products, arithmetic and copies ran while one was open for 6% -> 11% of each run, Pallas kernels for 0% -> 0%
where the time goes in v1:
time: 312 us; the launch traced here: 309 us
  matrix products  87.2 us (28%)
  waiting for transfers between devices  66.7 us (21%)
  local copies, waits for them, and re-layouts  60.8 us (19%)
  starting transfers between devices  36.4 us (12%)
  other arithmetic  35.9 us (12%)
  loops' own time  21.3 us (7%)
    ppermute x1, waiting for transfers between devices, scatter_frames(): return keep + lax.ppermute(give, 'frame', FRAME_SIDE).astype(jnp.float32)  42 us
    dynamic_slice x40, local copies, waits for them, and re-layouts, attention_grads(): lax.map(one_head, (split_heads(projected[:, 0]), split_heads(projected[:,...  25.2 us
    another operation x5, loops' own time, head_pass(): lax.scan(step, (zero_acc, zero_acc), starts)  20.9 us
    dot_general x10, matrix products, step(): jnp.einsum('qk,qd->kd', weights_low, grad_rows, preferred_element_type=jn...  20.8 us
    dot_general x10, matrix products, step(): jnp.einsum('qk,qd->kd', score_grad, query_rows, preferred_element_type=jn...  20.2 us
    dot_general x10, matrix products, step(): jnp.einsum('qd,kd->qk', query_rows, keys_in, preferred_element_type=jnp.f...  14.5 us
    ppermute x1, waiting for transfers between devices, gather_frames(): far = lax.ppermute(rows, 'frame', FRAME_SIDE)  11.4 us
    all_to_all x1, waiting for transfers between devices, per_device(): lax.all_to_all(thinker_grad.reshape(think_rows, frame_count, head_cols),...  9.54 us
  transfers between devices with their start and end apart: 7, of which 4 were waited for; matrix products, arithmetic and copies ran while one was open for 11% of the time, Pallas kernels for 0%

profile of v1, /device:TPU:1, one launch (start us, length us, event | category | flops | bytes accessed | tf_op | source)
XLA Modules:
  0.0 309.2 jit_solution(8612541161747147691)
XLA Ops:
  3.0 6.1 %all-to-all-start.1 = ((bf16[384,4,320]{0,2,1:T(8,128)(2,1)}), bf16[384,4,320]{0,2,1:T(8,128)(2,1)S(1)}, u32[]{:S(2)}, u32[]{:S(2)}) async-start(bf16[384,4,320]{0,2,1:T(8,128)(2,1)} %bitcast.17), calls=%async_computation.1 | async-start | bytes 1966080 | tf_op jit(solution)/shard_map/all_to_all | solution.py:154
  10.7 2.9 collective-permute-start
  13.8 9.5 %all-to-all-done.1 = bf16[384,4,320]{0,2,1:T(8,128)(2,1)S(1)} async-done(((bf16[384,4,320]{0,2,1:T(8,128)(2,1)}), bf16[384,4,320]{0,2,1:T(8,128)(2,1)S(1)}, u32[]{:S(2)}, u32[]{:S(2)}) %all-to-all-start.1) | async-done | bytes 983072 | tf_op jit(solution)/shard_map/all_to_all | solution.py:154
  25.2 8.2 %all-to-all-start = ((bf16[32,40,960]{2,1,0:T(8,128)(2,1)}), bf16[32,40,960]{2,1,0:T(8,128)(2,1)}, u32[]{:S(2)}, u32[]{:S(2)}) async-start(bf16[32,40,960]{2,1,0:T(8,128)(2,1)} %broadcast_in_dim.55), calls=%async_computation | async-start | bytes 5242880 | tf_op jit(solution)/shard_map/all_to_all | solution.py:148
  34.0 11.4 %collective-permute-done = bf16[256,1280]{1,0:T(8,128)(2,1)S(1)} collective-permute-done((bf16[256,1280]{1,0:T(8,128)(2,1)}, bf16[256,1280]{1,0:T(8,128)(2,1)S(1)}, u32[]{:S(2)}, u32[]{:S(2)}) %collective-permute-start) | collective-permute-done | bytes 655392 | tf_op jit(solution)/shard_map/ppermute | solution.py:117
  46.6 5.1 %collective-permute-start.1 = (bf16[2,256,1280]{2,1,0:T(8,128)(2,1)}, bf16[2,256,1280]{2,1,0:T(8,128)(2,1)}, u32[]{:S(2)}, u32[]{:S(2)}) collective-permute-start(bf16[2,256,1280]{2,1,0:T(8,128)(2,1)} %maximum_select_fusion.2), channel_id=1, source_target_pairs={{0,1},{1,0},{2,3},{3,2},{4,5},{5,4},{6,7},{7,6},{8,9},{9,8},{10,11... | collective-permute-start | bytes 3932168 | tf_op jit(solution)/shard_map/ppermute | solution.py:119
  54.3 3.9 %gather_fusion = bf16[1024,320]{1,0:T(8,128)(2,1)S(1)} fusion(bf16[1536,320]{1,0:T(8,128)(2,1)S(1)} %bitcast.114, s32[1024]{0:T(1024)S(1)} %fusion.37), kind=kCustom, calls=%fused_computation | custom fusion | bytes 1314816 | tf_op jit(solution)/shard_map/jit(_take)/gather | solution.py:162
  61.7 3.7 %all-to-all-done = bf16[32,40,960]{2,1,0:T(8,128)(2,1)} async-done(((bf16[32,40,960]{2,1,0:T(8,128)(2,1)}), bf16[32,40,960]{2,1,0:T(8,128)(2,1)}, u32[]{:S(2)}, u32[]{:S(2)}) %all-to-all-start) | async-done | bytes 2457632 | tf_op jit(solution)/shard_map/all_to_all | solution.py:148
  65.4 4.5 %convolution_convert_fusion.1 = bf16[1024,960]{0,1:T(8,128)(2,1)S(1)} fusion(bf16[1024,1280]{1,0:T(8,128)(2,1)S(1)} %bitcast.119, bf16[1280,960]{1,0:T(8,128)(2,1)} %bitcast.13), kind=kOutput, calls=%fused_computation.43 | convolution fusion | flops 2517565440 | bytes 7045120 | tf_op jit(solution)/shard_map/dot_general | solution.py:163
  71.2 147.2 %while.30 = (s32[]{:T(128)}, bf16[5,1024,64]{1,2,0:T(8,128)(2,1)}, bf16[5,1024,64]{1,2,0:T(8,128)(2,1)}, bf16[5,1024,64]{1,2,0:T(8,128)(2,1)}, bf16[5,1024,64]{1...) while((s32[]{:T(128)}, bf16[5,1024,64]{1,2,0:T(8,128)(2,1)}, ...), condition=%wide.region_10.11_spmd, body=%wide.region_4.10_spmd.sunk | while | flops 347601408 | bytes 28022344 | solution.py:97
  76.3 21.6 %while.31 = (s32[]{:T(128)}, f32[1024,64]{0,1:T(8,128)}, f32[1024,64]{0,1:T(8,128)}, bf16[2,512,64]{1,2,0:T(8,128)(2,1)S(1)}, s32[2]{0:T(128)S(1)}, /*index=5*/s...) while((s32[]{:T(128)}, f32[1024,64]{0,1:T(8,128)}, ...), condition=%wide.region_9.9_spmd.clone, body=%wide.region_5.8_spmd.clone.sunk | while | flops 347404800 | bytes 24351036 | solution.py:75
  105.8 21.6 %while.31 = (s32[]{:T(128)}, f32[1024,64]{0,1:T(8,128)}, f32[1024,64]{0,1:T(8,128)}, bf16[2,512,64]{1,2,0:T(8,128)(2,1)S(1)}, s32[2]{0:T(128)S(1)}, /*index=5*/s...) while((s32[]{:T(128)}, f32[1024,64]{0,1:T(8,128)}, ...), condition=%wide.region_9.9_spmd.clone, body=%wide.region_5.8_spmd.clone.sunk | while | flops 347404800 | bytes 24351036 | solution.py:75
  135.2 21.6 %while.31 = (s32[]{:T(128)}, f32[1024,64]{0,1:T(8,128)}, f32[1024,64]{0,1:T(8,128)}, bf16[2,512,64]{1,2,0:T(8,128)(2,1)S(1)}, s32[2]{0:T(128)S(1)}, /*index=5*/s...) while((s32[]{:T(128)}, f32[1024,64]{0,1:T(8,128)}, ...), condition=%wide.region_9.9_spmd.clone, body=%wide.region_5.8_spmd.clone.sunk | while | flops 347404800 | bytes 24351036 | solution.py:75
  164.7 21.6 %while.31 = (s32[]{:T(128)}, f32[1024,64]{0,1:T(8,128)}, f32[1024,64]{0,1:T(8,128)}, bf16[2,512,64]{1,2,0:T(8,128)(2,1)S(1)}, s32[2]{0:T(128)S(1)}, /*index=5*/s...) while((s32[]{:T(128)}, f32[1024,64]{0,1:T(8,128)}, ...), condition=%wide.region_9.9_spmd.clone, body=%wide.region_5.8_spmd.clone.sunk | while | flops 347404800 | bytes 24351036 | solution.py:75
  194.1 21.6 %while.31 = (s32[]{:T(128)}, f32[1024,64]{0,1:T(8,128)}, f32[1024,64]{0,1:T(8,128)}, bf16[2,512,64]{1,2,0:T(8,128)(2,1)S(1)}, s32[2]{0:T(128)S(1)}, /*index=5*/s...) while((s32[]{:T(128)}, f32[1024,64]{0,1:T(8,128)}, ...), condition=%wide.region_9.9_spmd.clone, body=%wide.region_5.8_spmd.clone.sunk | while | flops 347404800 | bytes 24351036 | solution.py:75
  220.2 2.7 dot_general.27
  222.8 7.7 %fusion.19 = f32[2,2,256,1280]{3,2,1,0:T(8,128)} fusion(bf16[1280,960,1,1]{1,0,3,2:T(8,128)(2,1)} %bitcast.35, bf16[2,2,256,960]{2,1,0,3:T(2,128)(2,1)} %dot_general.27), kind=kOutput, calls=%fused_computation.41 | convolution fusion | flops 2516582400 | bytes 9666560 | tf_op jit(solution)/shard_map/dot_general | solution.py:167
  232.4 3.5 %collective-permute-start.2 = (bf16[2,256,1280]{2,1,0:T(8,128)(2,1)S(1)}, bf16[2,256,1280]{2,1,0:T(8,128)(2,1)}, u32[]{:S(2)}, u32[]{:S(2)}) collective-permute-start(bf16[2,256,1280]{2,1,0:T(8,128)(2,1)S(1)} %fusion.33), channel_id=1, source_target_pairs={{0,1},{1,0},{2,3},{3,2},{4,5},{5,4},{6,7},{7,6},{8,9},{9,8},{10,11... | collective-permute-start | bytes 3932168 | tf_op jit(solution)/shard_map/ppermute | solution.py:131
  235.9 5.7 %convolution_convert_fusion = bf16[1280,960]{0,1:T(8,128)(2,1)} fusion(bf16[1024,960]{0,1:T(8,128)(2,1)S(1)} %bitcast.116, bf16[1024,1280]{1,0:T(8,128)(2,1)} %bitcast.120), kind=kOutput, calls=%fused_computation.36 | convolution fusion | flops 2517811200 | bytes 7045120 | tf_op jit(solution)/shard_map/dot_general | solution.py:171
  241.6 4.5 %copy.46 = bf16[1280,960]{1,0:T(8,128)(2,1)} copy(bf16[1280,960]{0,1:T(8,128)(2,1)} %convolution_convert_fusion) | data formatting | bytes 4915200 | tf_op jit(solution)/shard_map/convert_element_type | solution.py:175
  246.1 7.3 %all-to-all-start.2 = ((bf16[32,40,960]{2,1,0:T(8,128)(2,1)}), bf16[32,40,960]{2,1,0:T(8,128)(2,1)}, u32[]{:S(2)}, u32[]{:S(2)}) async-start(bf16[32,40,960]{2,1,0:T(8,128)(2,1)} %bitcast.41), calls=%async_computation.2 | async-start | bytes 5242880 | tf_op jit(solution)/shard_map/all_to_all | solution.py:174
  253.4 2.4 bitcast_add_fusion
  256.8 3.4 %collective-permute-start.3 = (bf16[256,1280]{1,0:T(8,128)(2,1)}, bf16[256,1280]{1,0:T(8,128)(2,1)}, u32[]{:S(2)}, u32[]{:S(2)}) collective-permute-start(bf16[256,1280]{1,0:T(8,128)(2,1)} %fusion.35), channel_id=1, source_target_pairs={{0,2},{1,3},{2,0},{3,1},{4,6},{5,7},{6,4},{7,5},{8,10},{9,11},{10,... | collective-permute-start | bytes 1966088 | tf_op jit(solution)/shard_map/ppermute | solution.py:134
  260.1 42.0 %collective-permute-done.3 = bf16[256,1280]{1,0:T(8,128)(2,1)} collective-permute-done((bf16[256,1280]{1,0:T(8,128)(2,1)}, bf16[256,1280]{1,0:T(8,128)(2,1)}, u32[]{:S(2)}, u32[]{:S(2)}) %collective-permute-start.3) | collective-permute-done | bytes 655392 | tf_op jit(solution)/shard_map/ppermute | solution.py:134
  (316 shorter events, 152.4 us)
Async XLA Ops:
  0.6 8.4 %copy-start.2 = (bf16[256,1280]{1,0:T(8,128)(2,1)S(1)}, bf16[256,1280]{1,0:T(8,128)(2,1)}, u32[]{:S(2)}) copy-start(bf16[256,1280]{1,0:T(8,128)(2,1)} %param.11) | copy-start | bytes 1966084
  2.9 6.6 %copy-start.8 = (f32[1280]{0:T(1024)S(1)}, f32[1280]{0:T(1024)}, u32[]{:S(2)}) copy-start(f32[1280]{0:T(1024)} %param.15) | copy-start | bytes 15364
  2.9 6.6 %copy-start.11 = (f32[1280]{0:T(1024)S(1)}, f32[1280]{0:T(1024)}, u32[]{:S(2)}) copy-start(f32[1280]{0:T(1024)} %param.16) | copy-start | bytes 15364
  2.9 10.7 %copy-start.10 = (bf16[40,3,320]{2,0,1:T(8,128)(2,1)S(1)}, bf16[40,3,320]{2,0,1:T(8,128)(2,1)}, u32[]{:S(2)}) copy-start(bf16[40,3,320]{2,0,1:T(8,128)(2,1)} %param.17) | copy-start | bytes 230404
  3.0 20.4 %all-to-all-start.1 = ((bf16[384,4,320]{0,2,1:T(8,128)(2,1)}), bf16[384,4,320]{0,2,1:T(8,128)(2,1)S(1)}, u32[]{:S(2)}, u32[]{:S(2)}) async-start(bf16[384,4,320]{0,2,1:T(8,128)(2,1)} %bitcast.17), calls=%async_computation.1 | async-start | bytes 1966080 | tf_op jit(solution)/shard_map/all_to_all | solution.py:154
  9.2 42.7 %copy-start.12 = (f32[256]{0:T(256)}, f32[256]{0:T(256)S(1)}, u32[]{:S(2)}) copy-start(f32[256]{0:T(256)S(1)} %broadcast_multiply_fusion.2) | copy-start | bytes 3076
  9.6 42.3 %copy-start.14 = (f32[256]{0:T(256)}, f32[256]{0:T(256)S(1)}, u32[]{:S(2)}) copy-start(f32[256]{0:T(256)S(1)} %add_rsqrt_fusion) | copy-start | bytes 3076
  10.7 34.6 %collective-permute-start = (bf16[256,1280]{1,0:T(8,128)(2,1)}, bf16[256,1280]{1,0:T(8,128)(2,1)S(1)}, u32[]{:S(2)}, u32[]{:S(2)}) collective-permute-start(bf16[256,1280]{1,0:T(8,128)(2,1)} %fusion.27), channel_id=1, source_target_pairs={{0,2},{1,3},{2,0},{3,1},{4,6},{5,7},{6,4},{7,5},{8,10},{9,11},{10,... | collective-permute-start | bytes 1966088 | tf_op jit(solution)/shard_map/ppermute | solution.py:117
  23.3 23.3 %copy-start.6 = (bf16[384,4,320]{0,2,1:T(8,128)(2,1)}, bf16[384,4,320]{0,2,1:T(8,128)(2,1)S(1)}, u32[]{:S(2)}) copy-start(bf16[384,4,320]{0,2,1:T(8,128)(2,1)S(1)} %all-to-all-done.1) | copy-start | bytes 2949124
  25.2 8.6 %copy-start.17 = (s32[1,3]{1,0:T(1,128)S(1)}, s32[1,3]{1,0:T(1,128)}, u32[]{:S(2)}) copy-start(s32[1,3]{1,0:T(1,128)} %param.12) | copy-start | bytes 40
  25.2 8.8 %copy-start.16 = (s32[1024]{0:T(1024)S(1)}, s32[1024]{0:T(1024)}, u32[]{:S(2)}) copy-start(s32[1024]{0:T(1024)} %param.13) | copy-start | bytes 12292
  25.2 40.2 %all-to-all-start = ((bf16[32,40,960]{2,1,0:T(8,128)(2,1)}), bf16[32,40,960]{2,1,0:T(8,128)(2,1)}, u32[]{:S(2)}, u32[]{:S(2)}) async-start(bf16[32,40,960]{2,1,0:T(8,128)(2,1)} %broadcast_in_dim.55), calls=%async_computation | async-start | bytes 5242880 | tf_op jit(solution)/shard_map/all_to_all | solution.py:148
  46.6 12.8 %collective-permute-start.1 = (bf16[2,256,1280]{2,1,0:T(8,128)(2,1)}, bf16[2,256,1280]{2,1,0:T(8,128)(2,1)}, u32[]{:S(2)}, u32[]{:S(2)}) collective-permute-start(bf16[2,256,1280]{2,1,0:T(8,128)(2,1)} %maximum_select_fusion.2), channel_id=1, source_target_pairs={{0,1},{1,0},{2,3},{3,2},{4,5},{5,4},{6,7},{7,6},{8,9},{9,8},{10,11... | collective-permute-start | bytes 3932168 | tf_op jit(solution)/shard_map/ppermute | solution.py:119
  61.7 8.2 %copy-start.7 = (bf16[2,2,256,1280]{3,2,1,0:T(8,128)(2,1)}, bf16[2,2,256,1280]{3,2,1,0:T(8,128)(2,1)S(1)}, u32[]{:S(2)}) copy-start(bf16[2,2,256,1280]{3,2,1,0:T(8,128)(2,1)S(1)} %copy.32) | copy-start | bytes 7864324
  76.3 5.0 %copy-start = (bf16[1024,64]{1,0:T(8,128)(2,1)}, bf16[1024,64]{1,0:T(8,128)(2,1)S(1)}, u32[]{:S(2)}) copy-start(bf16[1024,64]{1,0:T(8,128)(2,1)S(1)} %get-tuple-element.415) | copy-start | bytes 393220 | tf_op jit(solution)/shard_map/while/body/eval_jaxpr/while
  105.8 5.0 %copy-start = (bf16[1024,64]{1,0:T(8,128)(2,1)}, bf16[1024,64]{1,0:T(8,128)(2,1)S(1)}, u32[]{:S(2)}) copy-start(bf16[1024,64]{1,0:T(8,128)(2,1)S(1)} %get-tuple-element.415) | copy-start | bytes 393220 | tf_op jit(solution)/shard_map/while/body/eval_jaxpr/while
  194.1 5.0 %copy-start = (bf16[1024,64]{1,0:T(8,128)(2,1)}, bf16[1024,64]{1,0:T(8,128)(2,1)S(1)}, u32[]{:S(2)}) copy-start(bf16[1024,64]{1,0:T(8,128)(2,1)S(1)} %get-tuple-element.415) | copy-start | bytes 393220 | tf_op jit(solution)/shard_map/while/body/eval_jaxpr/while
  232.4 21.0 %collective-permute-start.2 = (bf16[2,256,1280]{2,1,0:T(8,128)(2,1)S(1)}, bf16[2,256,1280]{2,1,0:T(8,128)(2,1)}, u32[]{:S(2)}, u32[]{:S(2)}) collective-permute-start(bf16[2,256,1280]{2,1,0:T(8,128)(2,1)S(1)} %fusion.33), channel_id=1, source_target_pairs={{0,1},{1,0},{2,3},{3,2},{4,5},{5,4},{6,7},{7,6},{8,9},{9,8},{10,11... | collective-permute-start | bytes 3932168 | tf_op jit(solution)/shard_map/ppermute | solution.py:131
  246.1 60.1 %all-to-all-start.2 = ((bf16[32,40,960]{2,1,0:T(8,128)(2,1)}), bf16[32,40,960]{2,1,0:T(8,128)(2,1)}, u32[]{:S(2)}, u32[]{:S(2)}) async-start(bf16[32,40,960]{2,1,0:T(8,128)(2,1)} %bitcast.41), calls=%async_computation.2 | async-start | bytes 5242880 | tf_op jit(solution)/shard_map/all_to_all | solution.py:174
  253.4 48.8 %copy-start.3 = (bf16[256,1280]{1,0:T(8,128)(2,1)S(1)}, bf16[256,1280]{1,0:T(8,128)(2,1)}, u32[]{:S(2)}) copy-start(bf16[256,1280]{1,0:T(8,128)(2,1)} %param.11) | copy-start | bytes 1966084
  253.4 48.8 %copy-start.9 = (f32[1280]{0:T(1024)S(1)}, f32[1280]{0:T(1024)}, u32[]{:S(2)}) copy-start(f32[1280]{0:T(1024)} %param.15) | copy-start | bytes 15364
  253.4 48.8 %copy-start.13 = (f32[256]{0:T(256)S(1)}, f32[256]{0:T(256)}, u32[]{:S(2)}) copy-start(f32[256]{0:T(256)} %copy-done.12) | copy-start | bytes 3076
  253.4 48.8 %copy-start.15 = (f32[256]{0:T(256)S(1)}, f32[256]{0:T(256)}, u32[]{:S(2)}) copy-start(f32[256]{0:T(256)} %copy-done.14) | copy-start | bytes 3076
  256.8 45.4 %collective-permute-start.3 = (bf16[256,1280]{1,0:T(8,128)(2,1)}, bf16[256,1280]{1,0:T(8,128)(2,1)}, u32[]{:S(2)}, u32[]{:S(2)}) collective-permute-start(bf16[256,1280]{1,0:T(8,128)(2,1)} %fusion.35), channel_id=1, source_target_pairs={{0,2},{1,3},{2,0},{3,1},{4,6},{5,7},{6,4},{7,5},{8,10},{9,11},{10,... | collective-permute-start | bytes 1966088 | tf_op jit(solution)/shard_map/ppermute | solution.py:134
  (37 other events, 126.9 us)

commit v2 on v1

v2 whole, which is shorter than its diff:
```python
import jax
import jax.numpy as jnp
from jax import lax
from jax.experimental import pallas as pl
from jax.experimental.pallas import tpu as pltpu
from jax.sharding import PartitionSpec as P

HD = 64


norm_eps = 1e-05


def norm_forward(rows, gain, bias):
    rows_f32 = rows.astype(jnp.float32)
    mean_row = jnp.mean(rows_f32, axis=-1, keepdims=True)
    centered = rows_f32 - mean_row
    variance = jnp.mean(centered * centered, axis=-1, keepdims=True)
    inv_std = lax.rsqrt(variance + norm_eps)
    standard = centered * inv_std
    normalized = (standard * gain + bias).astype(jnp.bfloat16)
    return (normalized, standard, inv_std)


def norm_backward(norm_grad, standard, inv_std, gain):
    scaled = norm_grad * gain
    result = inv_std * (
        scaled
        - jnp.mean(scaled, axis=-1, keepdims=True)
        - standard * jnp.mean(scaled * standard, axis=-1, keepdims=True)
    )
    return result.astype(jnp.bfloat16)


def segment_ids(lengths, count):
    ends = jnp.cumsum(lengths)
    frame_ids = jnp.arange(count, dtype=jnp.int32)
    return jnp.sum((frame_ids[:, None] >= ends[None, :]).astype(jnp.int32), axis=1)


NEG = -1e30
F32 = jnp.float32
BF16 = jnp.bfloat16
QB = 256
KT = 256

KEY_UPPER = (True, False, True, False, False)
NT = (((1,), (1,)), ((), ()))
TN = (((0,), (0,)), ((), ()))


def attention_kernel(
    bounds, proj_ref, grad_ref, seg_ref, out_ref,
    q_aug, q_pad, k_aug, k_pad, v_pad, g_pad, score, dprob, kv_acc, dq_acc,
):
    rows = proj_ref.shape[0]
    heads = len(KEY_UPPER)
    scale = HD ** (-0.5)
    step_rows = 256

    def prepare(i, carry):
        r = pl.ds(pl.multiple_of(i * step_rows, step_rows), step_rows)
        lane = lax.broadcasted_iota(jnp.int32, (step_rows, 128), 1)
        seg = seg_ref[r, :]
        for h in range(heads):
            upper = KEY_UPPER[h]
            own = (lane >= 64) if upper else (lane < 64)
            slot = lane if upper else lane - 64
            kv = proj_ref[r, 128 * h:128 * (h + 1)].astype(F32)
            if h < 4:
                q = proj_ref[r, 640 + 128 * (h // 2):768 + 128 * (h // 2)].astype(F32)
            else:
                q = jnp.concatenate([proj_ref[r, 896:960].astype(F32), jnp.zeros((step_rows, 64), F32)], axis=1)
            q = q * scale
            g = grad_ref[r, 128 * (h // 2):128 * (h // 2) + 128].astype(F32)
            hit = slot == seg
            q_aug[h, r, :] = jnp.where(own, q, jnp.where(hit, 1.0, 0.0)).astype(BF16)
            q_pad[h, r, :] = jnp.where(own, q, 0.0).astype(BF16)
            miss = jnp.logical_and(jnp.logical_and(slot >= 0, slot < 3), jnp.logical_not(hit))
            k_aug[h, r, :] = jnp.where(own, kv, jnp.where(miss, NEG, 0.0)).astype(BF16)
            k_pad[h, r, :] = jnp.where(own, kv, 0.0).astype(BF16)
            v_pad[h, r, :] = jnp.where(own, 0.0, kv).astype(BF16)
            g_pad[h, r, :] = jnp.where(own, 0.0, g).astype(BF16)
            kv_acc[h, r, :] = jnp.zeros((step_rows, 128), F32)
        return carry

    lax.fori_loop(0, rows // step_rows, prepare, 0)

    def fold(x, op):
        y = x[0:8]
        for i in range(1, x.shape[0] // 8):
            y = op(y, x[8 * i:8 * i + 8])
        return y

    def query_block(qb, carry):
        q0 = pl.multiple_of(qb * QB, QB)
        qr = pl.ds(q0, QB)
        lo, hi = bounds[0, qb], bounds[1, qb]

        def first(t, tops):
            kr = pl.ds(pl.multiple_of(t * KT, KT), KT)
            new = []
            for h in range(heads):
                s = lax.dot_general(k_aug[h, kr, :], q_aug[h, qr, :], NT, preferred_element_type=F32)
                score[h, kr, :] = s
                new.append(jnp.maximum(tops[h], jnp.max(s.reshape(KT // 8, 8, QB), axis=0)))
            return tuple(new)

        tops = lax.fori_loop(lo, hi, first, tuple(jnp.full((8, QB), -3e38, F32) for _ in range(heads)))
        tops = [jnp.max(x, axis=0, keepdims=True) for x in tops]

        def second(t, sums):
            kr = pl.ds(pl.multiple_of(t * KT, KT), KT)
            new = []
            for h in range(heads):
                e = jnp.exp(score[h, kr, :] - tops[h])
                d = lax.dot_general(v_pad[h, kr, :], g_pad[h, qr, :], NT, preferred_element_type=F32)
                score[h, kr, :] = e
                dprob[h, kr, :] = d
                total, dotted = sums[h]
                new.append((
                    total + jnp.sum(e.reshape(KT // 8, 8, QB), axis=0),
                    dotted + jnp.sum((e * d).reshape(KT // 8, 8, QB), axis=0),
                ))
            return tuple(new)

        zero = jnp.zeros((8, QB), F32)
        sums = lax.fori_loop(lo, hi, second, tuple((zero, zero) for _ in range(heads)))
        inv, dot = [], []
        for total, dotted in sums:
            one = 1.0 / jnp.sum(total, axis=0, keepdims=True)
            inv.append(one)
            dot.append(jnp.sum(dotted, axis=0, keepdims=True) * one)
        dq_acc[...] = jnp.zeros(dq_acc.shape, F32)

        def third(t, carry):
            kr = pl.ds(pl.multiple_of(t * KT, KT), KT)
            for h in range(heads):
                a = score[h, kr, :] * inv[h]
                ds = (a * (dprob[h, kr, :] - dot[h])).astype(BF16)
                w = a.astype(BF16)
                kv_acc[h, kr, :] += (
                    jnp.dot(ds, q_pad[h, qr, :], preferred_element_type=F32)
                    + jnp.dot(w, g_pad[h, qr, :], preferred_element_type=F32)
                )
                dq_acc[h // 2] += lax.dot_general(ds, k_pad[h, kr, :], TN, preferred_element_type=F32)
            return carry

        lax.fori_loop(lo, hi, third, 0)
        out_ref[qr, 640:768] = (dq_acc[0] * scale).astype(BF16)
        out_ref[qr, 768:896] = (dq_acc[1] * scale).astype(BF16)
        out_ref[qr, 896:960] = (dq_acc[2] * scale).astype(BF16)[:, :64]
        return carry

    lax.fori_loop(0, rows // QB, query_block, 0)

    def finish(i, carry):
        r = pl.ds(pl.multiple_of(i * step_rows, step_rows), step_rows)
        for h in range(heads):
            out_ref[r, 128 * h:128 * (h + 1)] = kv_acc[h, r, :].astype(BF16)
        return carry

    lax.fori_loop(0, rows // step_rows, finish, 0)


def attention(projected, out_grad, segments, lengths):
    rows = projected.shape[0]
    heads = len(KEY_UPPER)
    ends = jnp.cumsum(lengths)
    starts = ends - lengths
    first_row = jnp.arange(rows // QB, dtype=jnp.int32) * QB
    lo = starts[segments[first_row]] // KT
    hi = (ends[segments[first_row + (QB - 1)]] + KT - 1) // KT
    bounds = jnp.stack([lo, hi]).astype(jnp.int32)
    vm = pl.BlockSpec(memory_space=pltpu.VMEM)
    tall = lambda: pltpu.VMEM((heads, rows, 128), BF16)
    return pl.pallas_call(
        attention_kernel,
        out_shape=jax.ShapeDtypeStruct((rows, projected.shape[1]), BF16),
        in_specs=[pl.BlockSpec(memory_space=pltpu.SMEM), vm, vm, vm],
        out_specs=vm,
        scratch_shapes=[tall() for _ in range(6)] + [
            pltpu.VMEM((heads, rows, QB), F32),
            pltpu.VMEM((heads, rows, QB), F32),
            pltpu.VMEM((heads, rows, 128), F32),
            pltpu.VMEM((3, QB, 128), F32),
        ],
        compiler_params=pltpu.CompilerParams(vmem_limit_bytes=60 << 20),
        cost_estimate=pl.CostEstimate(flops=20_000_000_000, bytes_accessed=6_000_000, transcendentals=5_000_000),
        name="attention_backward",
    )(bounds, projected, out_grad, segments.reshape(rows, 1))


PACK = ((2, 0), (1, 0), (1, 1), (2, 1), (2, 2), (1, 2), (1, 3), (2, 3), (1, 4), (2, 4), (0, 1), (0, 0), (0, 3), (0, 2), (0, 4))


def pack_columns(weight):
    return jnp.concatenate([weight[:, c, HD * h:HD * h + HD] for c, h in PACK], axis=1)


def unpack_columns(packed):
    place = {block: i for i, block in enumerate(PACK)}
    parts = [
        jnp.concatenate([packed[:, HD * place[c, h]:HD * place[c, h] + HD] for h in range(len(KEY_UPPER))], axis=1)
        for c in range(3)
    ]
    return jnp.stack(parts, axis=1)


def grad_tiles(out_grad):
    empty = jnp.zeros((out_grad.shape[0], HD), out_grad.dtype)
    return jnp.concatenate([out_grad[:, :256], empty, out_grad[:, 256:]], axis=1)


FRAME_SIDE = [(0, 2), (1, 3), (2, 0), (3, 1)]
FRAME_CORE = [(0, 1), (1, 0), (2, 3), (3, 2)]


def gather_frames(rows):
    core = lax.axis_index("frame") % 2
    side = lax.axis_index("frame") // 2
    far = lax.ppermute(rows, "frame", FRAME_SIDE)
    mine = jnp.where(side == 0, jnp.stack([rows, far]), jnp.stack([far, rows]))
    other = lax.ppermute(mine, "frame", FRAME_CORE)
    pair = jnp.where(core == 0, jnp.stack([mine, other], axis=1), jnp.stack([other, mine], axis=1))
    return pair.reshape(4 * rows.shape[0], rows.shape[1])


def scatter_frames(total):
    core = lax.axis_index("frame") % 2
    side = lax.axis_index("frame") // 2
    quarter = total.shape[0] // 4
    blocks = total.reshape(2, 2, quarter, total.shape[1])
    keep = lax.dynamic_index_in_dim(blocks, core, 1, keepdims=False)
    give = lax.dynamic_index_in_dim(blocks, 1 - core, 1, keepdims=False).astype(jnp.bfloat16)
    half = keep + lax.ppermute(give, "frame", FRAME_CORE).astype(jnp.float32)
    keep = lax.dynamic_index_in_dim(half, side, 0, keepdims=False)
    give = lax.dynamic_index_in_dim(half, 1 - side, 0, keepdims=False).astype(jnp.bfloat16)
    return keep + lax.ppermute(give, "frame", FRAME_SIDE).astype(jnp.float32)


def per_device(
    hidden_in, rec_lengths, token_positions, thinker_grad, norm_gain, norm_bias, qkv_weight
):
    frame_count = lax.axis_size("frame")
    groups = lax.axis_size("dp")
    width = hidden_in.shape[1]
    own_rows = qkv_weight.shape[0]
    head_cols = qkv_weight.shape[2]
    group_frames = token_positions.shape[0]
    think_rows = thinker_grad.shape[0]
    flat_weight = pack_columns(qkv_weight)
    weight = lax.all_to_all(
        jnp.broadcast_to(flat_weight[None], (groups, own_rows, 3 * head_cols)), "dp", 0, 0, tiled=True
    ).reshape(width, 3 * head_cols)
    normalized, standard, inv_std = norm_forward(hidden_in, norm_gain, norm_bias)
    normalized = gather_frames(normalized)
    segments = segment_ids(rec_lengths[0], group_frames)
    moved = lax.all_to_all(
        thinker_grad.reshape(think_rows, frame_count, head_cols),
        "frame",
        split_axis=1,
        concat_axis=0,
        tiled=True,
    )
    moved = moved.reshape(frame_count * think_rows, head_cols)
    out_grad = jnp.take(moved, token_positions, axis=0)
    projected = jnp.dot(normalized, weight, preferred_element_type=jnp.float32)
    projected = projected.astype(jnp.bfloat16)
    grad_flat = attention(projected, grad_tiles(out_grad), segments, rec_lengths[0])
    partial = lax.dot_general(
        grad_flat, weight, (((1,), (1,)), ((), ())), preferred_element_type=jnp.float32
    )
    norm_grad = scatter_frames(partial)
    term = lax.dot_general(
        normalized, grad_flat, (((0,), (0,)), ((), ())), preferred_element_type=jnp.float32
    )
    terms = lax.all_to_all(
        term.astype(jnp.bfloat16).reshape(groups, own_rows, 3 * head_cols), "dp", 0, 0, tiled=True
    )
    weight_grad = unpack_columns(jnp.sum(terms.astype(jnp.float32), axis=0))
    hidden_grad = norm_backward(norm_grad, standard, inv_std, norm_gain)
    return (hidden_grad, weight_grad)


def solution(mesh):
    placed = (
        P(("dp", "frame"), None),
        P("dp", None),
        P("dp"),
        P(("dp", "frame"), None),
        P(),
        P(),
        P("dp", None, "frame"),
    )
    return jax.shard_map(
        per_device,
        mesh=mesh,
        in_specs=placed,
        out_specs=(P(("dp", "frame"), None), P("dp", None, "frame")),
        check_vma=False,
    )
```

time: 312 us -> 194 us (0.62)
  matrix products: 87.2 us -> 16.9 us
  local copies, waits for them, and re-layouts: 60.8 us -> 27 us
  loops' own time: 21.3 us -> 0 us
  Pallas kernels: 0 us -> 17 us
  other arithmetic: 35.9 us -> 21.1 us
  waiting for transfers between devices: 66.7 us -> 73 us
    dot_general x50 -> x0, matrix products: 69.3 us -> none  [the longest x10 20.8 us: step(): jnp.einsum('qk,qd->kd', weights_low, grad_rows, preferred_element_type=jn...]
    dynamic_slice x60 -> x0, local copies, waits for them, and re-layouts: 33.1 us -> none  [the longest x40 25.2 us: attention_grads(): lax.map(one_head, (split_heads(projected[:, 0]), split_heads(projected[:,...]
    another operation x6 -> x0, loops' own time: 21.3 us -> none  [the longest x5 20.9 us: head_pass(): lax.scan(step, (zero_acc, zero_acc), starts)]
    pallas_call x0 -> x1, Pallas kernels: none -> 17 us  [attention(): pl.pallas_call(attention_kernel, out_shape=jax.ShapeDtypeStruct((rows, pr...]
    ppermute x1, waiting for transfers between devices: 11.4 us -> 0.01 us  [gather_frames(): far = lax.ppermute(rows, 'frame', FRAME_SIDE)]
    all_to_all x1, waiting for transfers between devices: 3.7 us -> 15 us  [per_device(): lax.all_to_all(jnp.broadcast_to(flat_weight[None], (groups, own_rows, 3 *...]
    dynamic_update_slice x5 -> x0, other arithmetic: 8.85 us -> none  [attention_grads(): lax.map(one_head, (split_heads(projected[:, 0]), split_heads(projected[:,...]
    reduce_sum x11 -> x1, other arithmetic: 9.24 us -> 2.22 us  [per_device(): weight_grad = unpack_columns(jnp.sum(terms.astype(jnp.float32), axis=0))]
  transfers between devices with their start and end apart: 7 -> 7, of which waited for: 4 -> 3; matrix products, arithmetic and copies ran while one was open for 11% -> 20% of each run, Pallas kernels for 0% -> 0%
where the time goes in v2:
time: 194 us
  waiting for transfers between devices  73 us (38%)
  starting transfers between devices  38 us (20%)
  local copies, waits for them, and re-layouts  27 us (14%)
  other arithmetic  21.1 us (11%)
  Pallas kernels  17 us (9%)
  matrix products  16.9 us (9%)
    ppermute x1, waiting for transfers between devices, scatter_frames(): return keep + lax.ppermute(give, 'frame', FRAME_SIDE).astype(jnp.float32)  42.4 us
    pallas_call x1, Pallas kernels, attention(): pl.pallas_call(attention_kernel, out_shape=jax.ShapeDtypeStruct((rows, pr...  17 us
    all_to_all x1, waiting for transfers between devices, per_device(): lax.all_to_all(thinker_grad.reshape(think_rows, frame_count, head_cols),...  15.6 us
    all_to_all x1, waiting for transfers between devices, per_device(): lax.all_to_all(jnp.broadcast_to(flat_weight[None], (groups, own_rows, 3 *...  15 us
    all_to_all x1, starting transfers between devices, per_device(): lax.all_to_all(term.astype(jnp.bfloat16).reshape(groups, own_rows, 3 * he...  13.2 us
    all_to_all x1, starting transfers between devices, per_device(): lax.all_to_all(jnp.broadcast_to(flat_weight[None], (groups, own_rows, 3 *...  9.01 us
    dot_general x1, matrix products, per_device(): lax.dot_general(normalized, grad_flat, (((0,), (0,)), ((), ())), preferre...  5.84 us
    dot_general x1, matrix products, per_device(): projected = jnp.dot(normalized, weight, preferred_element_type=jnp.float32)  5.77 us
  transfers between devices with their start and end apart: 7, of which 3 were waited for; matrix products, arithmetic and copies ran while one was open for 20% of the time, Pallas kernels for 0%

profile of v2, /device:TPU:1, one launch (start us, length us, event | category | flops | bytes accessed | tf_op | source)
XLA Modules:
  0.0 193.9 jit_solution(2477192792456154874)
XLA Ops:
  4.6 3.7 %collective-permute-start = (bf16[256,1280]{1,0:T(8,128)(2,1)}, bf16[256,1280]{1,0:T(8,128)(2,1)S(1)}, u32[]{:S(2)}, u32[]{:S(2)}) collective-permute-start(bf16[256,1280]{1,0:T(8,128)(2,1)} %fusion.6), channel_id=1, source_target_pairs={{0,2},{1,3},{2,0},{3,1},{4,6},{5,7},{6,4},{7,5},{8,10},{9,11},{10,... | collective-permute-start | bytes 1966088 | tf_op jit(solution)/shard_map/ppermute | solution.py:222
  9.7 4.6 %all-to-all-start.1 = ((bf16[384,4,320]{0,2,1:T(8,128)(2,1)}), bf16[384,4,320]{0,2,1:T(8,128)(2,1)S(1)}, u32[]{:S(2)}, u32[]{:S(2)}) async-start(bf16[384,4,320]{0,2,1:T(8,128)(2,1)} %bitcast.33), calls=%async_computation.1 | async-start | bytes 1966080 | tf_op jit(solution)/shard_map/all_to_all | solution.py:259
  17.7 15.6 %all-to-all-done.1 = bf16[384,4,320]{0,2,1:T(8,128)(2,1)S(1)} async-done(((bf16[384,4,320]{0,2,1:T(8,128)(2,1)}), bf16[384,4,320]{0,2,1:T(8,128)(2,1)S(1)}, u32[]{:S(2)}, u32[]{:S(2)}) %all-to-all-start.1) | async-done | bytes 983072 | tf_op jit(solution)/shard_map/all_to_all | solution.py:259
  33.3 1.9 broadcast_in_dim.13
  35.2 9.0 %all-to-all-start = ((bf16[32,40,960]{2,1,0:T(8,128)(2,1)}), bf16[32,40,960]{2,1,0:T(8,128)(2,1)}, u32[]{:S(2)}, u32[]{:S(2)}) async-start(bf16[32,40,960]{2,1,0:T(8,128)(2,1)} %broadcast_in_dim.13), calls=%async_computation | async-start | bytes 5242880 | tf_op jit(solution)/shard_map/all_to_all | solution.py:253
  45.6 1.8 collective-permute-start.1
  49.6 1.7 copy.31
  51.3 5.0 %gather_fusion.4 = bf16[1024,320]{1,0:T(8,128)(2,1)} fusion(bf16[1536,320]{1,0:T(8,128)(2,1)S(1)} %bitcast.112, s32[1024]{0:T(1024)S(1)} %fusion.16), kind=kCustom, calls=%fused_computation.4 | custom fusion | bytes 1314816 | tf_op jit(solution)/shard_map/jit(_take)/gather | solution.py:267
  58.9 2.1 %maximum_select_fusion = bf16[2,2,256,1280]{3,2,0,1:T(8,128)(2,1)S(1)} fusion(bf16[2,1,256,1280]{3,2,0,1:T(8,128)(2,1)} %bitcast.15, bf16[2,1,256,1280]{3,2,0,1:T(8,128)(2,1)S(1)} %maximum_select_fusion.1, pred[]{:T(512)S(6)} %eq.9), kind=kLoop, calls=%fused_computation.7 | loop fusion | flops 3932160 | bytes 5242881 | tf_op jit(solution)/shard_map/jit(_where)/select_n | solution.py:225
  61.2 15.0 %all-to-all-done = bf16[32,40,960]{2,1,0:T(8,128)(2,1)} async-done(((bf16[32,40,960]{2,1,0:T(8,128)(2,1)}), bf16[32,40,960]{2,1,0:T(8,128)(2,1)}, u32[]{:S(2)}, u32[]{:S(2)}) %all-to-all-start) | async-done | bytes 2457632 | tf_op jit(solution)/shard_map/all_to_all | solution.py:253
  76.1 5.8 %convolution_convert_fusion.1 = bf16[1024,960]{0,1:T(8,128)(2,1)} fusion(bf16[1024,1280]{1,0:T(8,128)(2,1)S(1)} %bitcast.114, bf16[1280,960]{1,0:T(8,128)(2,1)} %bitcast.32), kind=kOutput, calls=%fused_computation.10 | convolution fusion | flops 2517565440 | bytes 7045120 | tf_op jit(solution)/shard_map/dot_general | solution.py:268
  81.9 3.9 %copy.32.proj_ref = bf16[1024,960]{1,0:T(8,128)(2,1)} copy(bf16[1024,960]{0,1:T(8,128)(2,1)} %convolution_convert_fusion.1) | data formatting | bytes 3932160 | tf_op jit(solution)/shard_map/convert_element_type | solution.py:269
  85.8 17.0 %attention_backward.1 = bf16[1024,960]{1,0:T(8,128)(2,1)} custom-call(s32[2,4]{1,0:T(2,128)} %pad_add_fusion.bounds, bf16[1024,960]{1,0:T(8,128)(2,1)} %copy.32.proj_ref, bf16[1024,384]{1,0:T(8,128)(2,1)} %pad_maximum_fusion.grad_ref, s32[1024,1]{1,0:T(8,128)} %copy.33.seg_ref), custom_call_target="tpu_custom_call" | custom-call | flops 20000000000 | bytes 6000000 | tf_op jit(solution)/shard_map/attention_backward/pallas_call | solution.py:177
  102.8 5.3 %fusion.23 = f32[2,2,256,1280]{3,2,1,0:T(8,128)S(1)} fusion(bf16[2,2,256,960]{3,2,1,0:T(8,128)(2,1)} %bitcast.120, bf16[1280,960,1,1]{1,0,3,2:T(8,128)(2,1)} %bitcast.39), kind=kOutput, calls=%fused_computation.89 | convolution fusion | flops 2516582400 | bytes 9666560 | tf_op jit(solution)/shard_map/dot_general | solution.py:271
  108.1 2.3 %copy-done.2 = f32[2,2,256,1280]{3,2,1,0:T(8,128)} copy-done((f32[2,2,256,1280]{3,2,1,0:T(8,128)}, f32[2,2,256,1280]{3,2,1,0:T(8,128)S(1)}, u32[]{:S(2)}) %copy-start.2) | copy-done | bytes 5242904
  111.6 3.0 %collective-permute-start.2 = (bf16[2,256,1280]{2,1,0:T(8,128)(2,1)}, bf16[2,256,1280]{2,1,0:T(8,128)(2,1)}, u32[]{:S(2)}, u32[]{:S(2)}) collective-permute-start(bf16[2,256,1280]{2,1,0:T(8,128)(2,1)} %fusion.12), channel_id=1, source_target_pairs={{0,1},{1,0},{2,3},{3,2},{4,5},{5,4},{6,7},{7,6},{8,9},{9,8},{10,11... | collective-permute-start | bytes 3932168 | tf_op jit(solution)/shard_map/ppermute | solution.py:236
  114.7 5.8 %convolution_convert_fusion = bf16[1280,960]{0,1:T(8,128)(2,1)} fusion(bf16[1024,1280]{1,0:T(8,128)(2,1)S(1)} %bitcast.115, bf16[1024,960]{1,0:T(8,128)(2,1)} %attention_backward.1), kind=kOutput, calls=%fused_computation.6 | convolution fusion | flops 2517811200 | bytes 7045120 | tf_op jit(solution)/shard_map/dot_general | solution.py:275
  120.5 4.5 %copy.36 = bf16[1280,960]{1,0:T(8,128)(2,1)} copy(bf16[1280,960]{0,1:T(8,128)(2,1)} %convolution_convert_fusion) | data formatting | bytes 4915200 | tf_op jit(solution)/shard_map/convert_element_type | solution.py:279
  125.0 13.2 %all-to-all-start.2 = ((bf16[32,40,960]{2,1,0:T(8,128)(2,1)}), bf16[32,40,960]{2,1,0:T(8,128)(2,1)}, u32[]{:S(2)}, u32[]{:S(2)}) async-start(bf16[32,40,960]{2,1,0:T(8,128)(2,1)} %bitcast.44), calls=%async_computation.2 | async-start | bytes 5242880 | tf_op jit(solution)/shard_map/all_to_all | solution.py:278
  138.2 2.4 %bitcast_add_fusion = f32[2,256,1280]{2,1,0:T(8,128)S(1)} fusion(bf16[2,256,1280]{2,1,0:T(8,128)(2,1)} %collective-permute-done.2, f32[2,2,256,1280]{3,2,1,0:T(8,128)} %copy-done.2, s32[]{:T(128)S(6)} %select_n.154), kind=kLoop, calls=%fused_computation.8 | loop fusion | flops 1310720 | bytes 6553604 | tf_op jit(solution)/shard_map/add | solution.py:236
  141.6 2.6 %collective-permute-start.3 = (bf16[256,1280]{1,0:T(8,128)(2,1)}, bf16[256,1280]{1,0:T(8,128)(2,1)}, u32[]{:S(2)}, u32[]{:S(2)}) collective-permute-start(bf16[256,1280]{1,0:T(8,128)(2,1)} %fusion.14), channel_id=1, source_target_pairs={{0,2},{1,3},{2,0},{3,1},{4,6},{5,7},{6,4},{7,5},{8,10},{9,11},{10,... | collective-permute-start | bytes 1966088 | tf_op jit(solution)/shard_map/ppermute | solution.py:239
  144.2 42.4 %collective-permute-done.3 = bf16[256,1280]{1,0:T(8,128)(2,1)} collective-permute-done((bf16[256,1280]{1,0:T(8,128)(2,1)}, bf16[256,1280]{1,0:T(8,128)(2,1)}, u32[]{:S(2)}, u32[]{:S(2)}) %collective-permute-start.3) | collective-permute-done | bytes 655392 | tf_op jit(solution)/shard_map/ppermute | solution.py:239
  188.2 2.4 %fusion.10 = bf16[256,1280]{1,0:T(8,128)(2,1)} fusion(bf16[256,1280]{1,0:T(8,128)(2,1)S(1)} %copy-done, f32[256]{0:T(256)S(1)} %broadcast_multiply_fusion, f32[256]{0:T(256)S(1)} %broadcast_multiply_fusion.1, f32[256]{0:T(256)S(1)} %add_rsqrt_fusion, f32[256]{0:T(256)S(1)} %broadcast_multiply_fusion.2, f32[1280]{0:T(1024)S(1)} %copy-done.5, ...), kind=kLoop, calls=%fused_computation.23 | loop fusion | flops 3604480 | bytes 3286020 | tf_op jit(solution)/shard_map/convert_element_type | solution.py:32
  190.6 2.2 %convert_reduce_fusion = f32[40,960]{1,0:T(8,128)S(1)} fusion(bf16[32,40,960]{2,1,0:T(8,128)(2,1)} %all-to-all-done.2), kind=kLoop, calls=%fused_computation.5 | loop fusion | flops 2419200 | bytes 2611200 | tf_op jit(solution)/shard_map/reduce_sum | solution.py:281
  (71 shorter events, 19.7 us)
Async XLA Ops:
  0.6 2.8 %copy-start = (bf16[256,1280]{1,0:T(8,128)(2,1)S(1)}, bf16[256,1280]{1,0:T(8,128)(2,1)}, u32[]{:S(2)}) copy-start(bf16[256,1280]{1,0:T(8,128)(2,1)} %param.7) | copy-start | bytes 1966084
  0.6 2.8 %copy-start.5 = (f32[1280]{0:T(1024)S(1)}, f32[1280]{0:T(1024)}, u32[]{:S(2)}) copy-start(f32[1280]{0:T(1024)} %param.11) | copy-start | bytes 15364
  0.7 2.8 %copy-start.6 = (f32[1280]{0:T(1024)S(1)}, f32[1280]{0:T(1024)}, u32[]{:S(2)}) copy-start(f32[1280]{0:T(1024)} %param.12) | copy-start | bytes 15364
  0.7 7.7 %copy-start.3 = (bf16[384,1280]{1,0:T(8,128)(2,1)S(1)}, bf16[384,1280]{1,0:T(8,128)(2,1)}, u32[]{:S(2)}) copy-start(bf16[384,1280]{1,0:T(8,128)(2,1)} %param.10) | copy-start | bytes 2949124
  4.6 39.6 %collective-permute-start = (bf16[256,1280]{1,0:T(8,128)(2,1)}, bf16[256,1280]{1,0:T(8,128)(2,1)S(1)}, u32[]{:S(2)}, u32[]{:S(2)}) collective-permute-start(bf16[256,1280]{1,0:T(8,128)(2,1)} %fusion.6), channel_id=1, source_target_pairs={{0,2},{1,3},{2,0},{3,1},{4,6},{5,7},{6,4},{7,5},{8,10},{9,11},{10,... | collective-permute-start | bytes 1966088 | tf_op jit(solution)/shard_map/ppermute | solution.py:222
  9.7 4.6 %copy-start.4 = (bf16[40,3,320]{2,0,1:T(8,128)(2,1)S(1)}, bf16[40,3,320]{2,0,1:T(8,128)(2,1)}, u32[]{:S(2)}) copy-start(bf16[40,3,320]{2,0,1:T(8,128)(2,1)} %param.13) | copy-start | bytes 230404
  9.7 4.7 %copy-start.8 = (s32[1,3]{1,0:T(1,128)S(1)}, s32[1,3]{1,0:T(1,128)}, u32[]{:S(2)}) copy-start(s32[1,3]{1,0:T(1,128)} %param.8) | copy-start | bytes 40
  9.7 23.6 %all-to-all-start.1 = ((bf16[384,4,320]{0,2,1:T(8,128)(2,1)}), bf16[384,4,320]{0,2,1:T(8,128)(2,1)S(1)}, u32[]{:S(2)}, u32[]{:S(2)}) async-start(bf16[384,4,320]{0,2,1:T(8,128)(2,1)} %bitcast.33), calls=%async_computation.1 | async-start | bytes 1966080 | tf_op jit(solution)/shard_map/all_to_all | solution.py:259
  16.0 1.7 copy-start.7
  33.3 1.9 copy-start.1
  35.2 40.9 %all-to-all-start = ((bf16[32,40,960]{2,1,0:T(8,128)(2,1)}), bf16[32,40,960]{2,1,0:T(8,128)(2,1)}, u32[]{:S(2)}, u32[]{:S(2)}) async-start(bf16[32,40,960]{2,1,0:T(8,128)(2,1)} %broadcast_in_dim.13), calls=%async_computation | async-start | bytes 5242880 | tf_op jit(solution)/shard_map/all_to_all | solution.py:253
  45.6 13.3 %collective-permute-start.1 = (bf16[2,256,1280]{2,1,0:T(8,128)(2,1)}, bf16[2,256,1280]{2,1,0:T(8,128)(2,1)}, u32[]{:S(2)}, u32[]{:S(2)}) collective-permute-start(bf16[2,256,1280]{2,1,0:T(8,128)(2,1)} %maximum_select_fusion.2), channel_id=1, source_target_pairs={{0,1},{1,0},{2,3},{3,2},{4,5},{5,4},{6,7},{7,6},{8,9},{9,8},{10,11... | collective-permute-start | bytes 3932168 | tf_op jit(solution)/shard_map/ppermute | solution.py:224
  108.1 2.3 %copy-start.2 = (f32[2,2,256,1280]{3,2,1,0:T(8,128)}, f32[2,2,256,1280]{3,2,1,0:T(8,128)S(1)}, u32[]{:S(2)}) copy-start(f32[2,2,256,1280]{3,2,1,0:T(8,128)S(1)} %fusion.23) | copy-start | bytes 15728644
  111.6 26.6 %collective-permute-start.2 = (bf16[2,256,1280]{2,1,0:T(8,128)(2,1)}, bf16[2,256,1280]{2,1,0:T(8,128)(2,1)}, u32[]{:S(2)}, u32[]{:S(2)}) collective-permute-start(bf16[2,256,1280]{2,1,0:T(8,128)(2,1)} %fusion.12), channel_id=1, source_target_pairs={{0,1},{1,0},{2,3},{3,2},{4,5},{5,4},{6,7},{7,6},{8,9},{9,8},{10,11... | collective-permute-start | bytes 3932168 | tf_op jit(solution)/shard_map/ppermute | solution.py:236
  125.0 65.6 %all-to-all-start.2 = ((bf16[32,40,960]{2,1,0:T(8,128)(2,1)}), bf16[32,40,960]{2,1,0:T(8,128)(2,1)}, u32[]{:S(2)}, u32[]{:S(2)}) async-start(bf16[32,40,960]{2,1,0:T(8,128)(2,1)} %bitcast.44), calls=%async_computation.2 | async-start | bytes 5242880 | tf_op jit(solution)/shard_map/all_to_all | solution.py:278
  141.6 45.0 %collective-permute-start.3 = (bf16[256,1280]{1,0:T(8,128)(2,1)}, bf16[256,1280]{1,0:T(8,128)(2,1)}, u32[]{:S(2)}, u32[]{:S(2)}) collective-permute-start(bf16[256,1280]{1,0:T(8,128)(2,1)} %fusion.14), channel_id=1, source_target_pairs={{0,2},{1,3},{2,0},{3,1},{4,6},{5,7},{6,4},{7,5},{8,10},{9,11},{10,... | collective-permute-start | bytes 1966088 | tf_op jit(solution)/shard_map/ppermute | solution.py:239

commit v3 on v2

v3 whole, which is shorter than its diff:
```python
import jax
import jax.numpy as jnp
from jax import lax
from jax.experimental import pallas as pl
from jax.experimental.pallas import tpu as pltpu
from jax.sharding import PartitionSpec as P


HD = 64


norm_eps = 1e-05


def norm_forward(rows, gain, bias):
    rows_f32 = rows.astype(jnp.float32)
    mean_row = jnp.mean(rows_f32, axis=-1, keepdims=True)
    centered = rows_f32 - mean_row
    variance = jnp.mean(centered * centered, axis=-1, keepdims=True)
    inv_std = lax.rsqrt(variance + norm_eps)
    standard = centered * inv_std
    normalized = (standard * gain + bias).astype(jnp.bfloat16)
    return (normalized, standard, inv_std)


def norm_backward(norm_grad, standard, inv_std, gain):
    scaled = norm_grad * gain
    result = inv_std * (
        scaled
        - jnp.mean(scaled, axis=-1, keepdims=True)
        - standard * jnp.mean(scaled * standard, axis=-1, keepdims=True)
    )
    return result.astype(jnp.bfloat16)


def segment_ids(lengths, count):
    ends = jnp.cumsum(lengths)
    frame_ids = jnp.arange(count, dtype=jnp.int32)
    return jnp.sum((frame_ids[:, None] >= ends[None, :]).astype(jnp.int32), axis=1)


NEG = -1e30
F32 = jnp.float32
BF16 = jnp.bfloat16
QB = 256
KT = 256
ROWS = 256

KEY_UPPER = (True, False, True, False, False)
NT = (((1,), (1,)), ((), ()))
TN = (((0,), (0,)), ((), ()))


def chunk_blocks(heads):
    blocks = []
    for h in heads:
        blocks += [(2, h), (1, h)] if KEY_UPPER[h] else [(1, h), (2, h)]
    for h in heads:
        if h % 2 == 0:
            blocks += [(0, h + 1), (0, h)] if h + 1 in heads else [(0, h)]
    return tuple(blocks)


def attention_kernel(
    heads, bounds, norm_ref, weight_ref, grad_ref, seg_ref, out_ref, term_ref,
    q_aug, q_pad, k_aug, k_pad, v_pad, g_pad, score, dprob, kv_acc, dq_acc,
):
    rows = norm_ref.shape[0]
    count = len(heads)
    width = weight_ref.shape[1]
    scale = HD ** (-0.5)

    def prepare(i, carry):
        r = pl.ds(pl.multiple_of(i * ROWS, ROWS), ROWS)
        lane = lax.broadcasted_iota(jnp.int32, (ROWS, 128), 1)
        seg = seg_ref[r, :]
        proj = jnp.dot(norm_ref[r, :], weight_ref[...], preferred_element_type=F32)
        proj = proj.astype(BF16).astype(F32)
        for n, h in enumerate(heads):
            upper = KEY_UPPER[h]
            own = (lane >= 64) if upper else (lane < 64)
            slot = lane if upper else lane - 64
            kv = proj[:, 128 * n:128 * (n + 1)]
            at = 128 * (count + n // 2)
            if at + 128 <= width:
                q = proj[:, at:at + 128]
            else:
                q = jnp.concatenate([proj[:, at:at + 64], jnp.zeros((ROWS, 64), F32)], axis=1)
            q = q * scale
            g = grad_ref[r, 128 * (h // 2):128 * (h // 2) + 128].astype(F32)
            hit = slot == seg
            q_aug[n, r, :] = jnp.where(own, q, jnp.where(hit, 1.0, 0.0)).astype(BF16)
            q_pad[n, r, :] = jnp.where(own, q, 0.0).astype(BF16)
            miss = jnp.logical_and(jnp.logical_and(slot >= 0, slot < 3), jnp.logical_not(hit))
            k_aug[n, r, :] = jnp.where(own, kv, jnp.where(miss, NEG, 0.0)).astype(BF16)
            k_pad[n, r, :] = jnp.where(own, kv, 0.0).astype(BF16)
            v_pad[n, r, :] = jnp.where(own, 0.0, kv).astype(BF16)
            g_pad[n, r, :] = jnp.where(own, 0.0, g).astype(BF16)
            kv_acc[n, r, :] = jnp.zeros((ROWS, 128), F32)
        return carry

    lax.fori_loop(0, rows // ROWS, prepare, 0)

    def query_block(qb, carry):
        qr = pl.ds(pl.multiple_of(qb * QB, QB), QB)
        lo, hi = bounds[0, qb], bounds[1, qb]

        def first(t, tops):
            kr = pl.ds(pl.multiple_of(t * KT, KT), KT)
            new = []
            for h in range(count):
                s = lax.dot_general(k_aug[h, kr, :], q_aug[h, qr, :], NT, preferred_element_type=F32)
                score[h, kr, :] = s
                new.append(jnp.maximum(tops[h], jnp.max(s.reshape(KT // 8, 8, QB), axis=0)))
            return tuple(new)

        tops = lax.fori_loop(lo, hi, first, tuple(jnp.full((8, QB), -3e38, F32) for _ in range(count)))
        tops = [jnp.max(x, axis=0, keepdims=True) for x in tops]

        def second(t, sums):
            kr = pl.ds(pl.multiple_of(t * KT, KT), KT)
            new = []
            for h in range(count):
                e = jnp.exp(score[h, kr, :] - tops[h])
                d = lax.dot_general(v_pad[h, kr, :], g_pad[h, qr, :], NT, preferred_element_type=F32)
                score[h, kr, :] = e
                dprob[h, kr, :] = d
                total, dotted = sums[h]
                new.append((
                    total + jnp.sum(e.reshape(KT // 8, 8, QB), axis=0),
                    dotted + jnp.sum((e * d).reshape(KT // 8, 8, QB), axis=0),
                ))
            return tuple(new)

        zero = jnp.zeros((8, QB), F32)
        sums = lax.fori_loop(lo, hi, second, tuple((zero, zero) for _ in range(count)))
        inv, dot = [], []
        for total, dotted in sums:
            one = 1.0 / jnp.sum(total, axis=0, keepdims=True)
            inv.append(one)
            dot.append(jnp.sum(dotted, axis=0, keepdims=True) * one)
        dq_acc[...] = jnp.zeros(dq_acc.shape, F32)

        def third(t, carry):
            kr = pl.ds(pl.multiple_of(t * KT, KT), KT)
            for h in range(count):
                a = score[h, kr, :] * inv[h]
                ds = (a * (dprob[h, kr, :] - dot[h])).astype(BF16)
                w = a.astype(BF16)
                kv_acc[h, kr, :] += (
                    jnp.dot(ds, q_pad[h, qr, :], preferred_element_type=F32)
                    + jnp.dot(w, g_pad[h, qr, :], preferred_element_type=F32)
                )
                dq_acc[h // 2] += lax.dot_general(ds, k_pad[h, kr, :], TN, preferred_element_type=F32)
            return carry

        lax.fori_loop(lo, hi, third, 0)
        for p in range((count + 1) // 2):
            at = 128 * (count + p)
            span = min(128, width - at)
            out_ref[qr, at:at + span] = (dq_acc[p] * scale).astype(BF16)[:, :span]
        return carry

    lax.fori_loop(0, rows // QB, query_block, 0)

    def finish(i, carry):
        r = pl.ds(pl.multiple_of(i * ROWS, ROWS), ROWS)
        for h in range(count):
            out_ref[r, 128 * h:128 * (h + 1)] = kv_acc[h, r, :].astype(BF16)
        return carry

    lax.fori_loop(0, rows // ROWS, finish, 0)

    for i in range(norm_ref.shape[1] // 256):
        part = lax.dot_general(norm_ref[:, 256 * i:256 * i + 256], out_ref[...], TN, preferred_element_type=F32)
        term_ref[256 * i:256 * i + 256, :] = part.astype(BF16)


def key_bounds(segments, lengths):
    rows = segments.shape[0]
    ends = jnp.cumsum(lengths)
    starts = ends - lengths
    first_row = jnp.arange(rows // QB, dtype=jnp.int32) * QB
    lo = starts[segments[first_row]] // KT
    hi = (ends[segments[first_row + (QB - 1)]] + KT - 1) // KT
    return jnp.stack([lo, hi]).astype(jnp.int32)


def attention(heads, normalized, weight, out_grad, segments, bounds):
    rows, features = normalized.shape
    columns = weight.shape[1]
    count = len(heads)
    vm = pl.BlockSpec(memory_space=pltpu.VMEM)
    tall = pltpu.VMEM((count, rows, 128), BF16)
    wide = pltpu.VMEM((count, rows, QB), F32)
    body = lambda *refs: attention_kernel(heads, *refs)
    return pl.pallas_call(
        body,
        out_shape=(
            jax.ShapeDtypeStruct((rows, columns), BF16),
            jax.ShapeDtypeStruct((features, columns), BF16),
        ),
        in_specs=[pl.BlockSpec(memory_space=pltpu.SMEM), vm, vm, vm, vm],
        out_specs=(vm, vm),
        scratch_shapes=[tall] * 6 + [wide, wide, pltpu.VMEM((count, rows, 128), F32), pltpu.VMEM(((count + 1) // 2, QB, 128), F32)],
        compiler_params=pltpu.CompilerParams(vmem_limit_bytes=40 << 20),
        cost_estimate=pl.CostEstimate(
            flops=5_000_000_000 * count, bytes_accessed=8_000_000, transcendentals=1_000_000 * count
        ),
        name="attention_backward",
    )(bounds, normalized, weight, out_grad, segments)


CHUNKS = ((0, 1), (2, 3, 4))


def pack_columns(weight, heads):
    return jnp.concatenate([weight[:, c, HD * h:HD * h + HD] for c, h in chunk_blocks(heads)], axis=1)


def unpack_columns(chunks):
    place = {}
    for heads, packed in zip(CHUNKS, chunks):
        for i, block in enumerate(chunk_blocks(heads)):
            place[block] = packed[:, HD * i:HD * i + HD]
    parts = [jnp.concatenate([place[c, h] for h in range(len(KEY_UPPER))], axis=1) for c in range(3)]
    return jnp.stack(parts, axis=1)


def gather_weight(shard):
    groups = lax.axis_size("dp")
    spread = lax.all_to_all(jnp.broadcast_to(shard[None], (groups,) + shard.shape), "dp", 0, 0, tiled=True)
    return spread.reshape(groups * shard.shape[0], shard.shape[1])


def exchange_terms(term):
    groups = lax.axis_size("dp")
    return lax.all_to_all(
        term.reshape(groups, term.shape[0] // groups, term.shape[1]), "dp", 0, 0, tiled=True
    )


def grad_tiles(out_grad):
    empty = jnp.zeros((out_grad.shape[0], HD), out_grad.dtype)
    return jnp.concatenate([out_grad[:, :256], empty, out_grad[:, 256:]], axis=1)


FRAME_SIDE = [(0, 2), (1, 3), (2, 0), (3, 1)]
FRAME_CORE = [(0, 1), (1, 0), (2, 3), (3, 2)]


def gather_frames(rows):
    core = lax.axis_index("frame") % 2
    side = lax.axis_index("frame") // 2
    far = lax.ppermute(rows, "frame", FRAME_SIDE)
    mine = jnp.where(side == 0, jnp.stack([rows, far]), jnp.stack([far, rows]))
    other = lax.ppermute(mine, "frame", FRAME_CORE)
    pair = jnp.where(core == 0, jnp.stack([mine, other], axis=1), jnp.stack([other, mine], axis=1))
    return pair.reshape(4 * rows.shape[0], rows.shape[1])


def scatter_frames(total):
    core = lax.axis_index("frame") % 2
    side = lax.axis_index("frame") // 2
    quarter = total.shape[0] // 4
    blocks = total.reshape(2, 2, quarter, total.shape[1])
    keep = lax.dynamic_index_in_dim(blocks, core, 1, keepdims=False)
    give = lax.dynamic_index_in_dim(blocks, 1 - core, 1, keepdims=False).astype(jnp.bfloat16)
    half = keep + lax.ppermute(give, "frame", FRAME_CORE).astype(jnp.float32)
    keep = lax.dynamic_index_in_dim(half, side, 0, keepdims=False)
    give = lax.dynamic_index_in_dim(half, 1 - side, 0, keepdims=False).astype(jnp.bfloat16)
    return keep + lax.ppermute(give, "frame", FRAME_SIDE).astype(jnp.float32)


def per_device(
    hidden_in, rec_lengths, token_positions, thinker_grad, norm_gain, norm_bias, qkv_weight
):
    frame_count = lax.axis_size("frame")
    head_cols = qkv_weight.shape[2]
    group_frames = token_positions.shape[0]
    think_rows = thinker_grad.shape[0]
    shards = [pack_columns(qkv_weight, heads) for heads in CHUNKS]
    normalized, standard, inv_std = norm_forward(hidden_in, norm_gain, norm_bias)
    weights = [gather_weight(shards[0])]
    normalized = gather_frames(normalized)
    thinker, weights[0] = lax.optimization_barrier((thinker_grad, weights[0]))
    moved = lax.all_to_all(
        thinker.reshape(think_rows, frame_count, head_cols),
        "frame",
        split_axis=1,
        concat_axis=0,
        tiled=True,
    )
    shard, moved = lax.optimization_barrier((shards[1], moved))
    weights.append(gather_weight(shard))
    moved = moved.reshape(frame_count * think_rows, head_cols)
    out_grad = grad_tiles(jnp.take(moved, token_positions, axis=0))
    segments = segment_ids(rec_lengths[0], group_frames)
    bounds = key_bounds(segments, rec_lengths[0])
    segments = segments.reshape(group_frames, 1)
    grads, terms = [], []
    for heads, weight in zip(CHUNKS, weights):
        grad, term = attention(heads, normalized, weight, out_grad, segments, bounds)
        grads.append(grad)
        terms.append(exchange_terms(term))
    partial = sum(lax.dot_general(grad, weight, NT, preferred_element_type=F32) for grad, weight in zip(grads, weights))
    norm_grad = scatter_frames(partial)
    weight_grad = unpack_columns([jnp.sum(term.astype(F32), axis=0) for term in terms])
    hidden_grad = norm_backward(norm_grad, standard, inv_std, norm_gain)
    return (hidden_grad, weight_grad)


def solution(mesh):
    placed = (
        P(("dp", "frame"), None),
        P("dp", None),
        P("dp"),
        P(("dp", "frame"), None),
        P(),
        P(),
        P("dp", None, "frame"),
    )

    return jax.shard_map(
        per_device,
        mesh=mesh,
        in_specs=placed,
        out_specs=(P(("dp", "frame"), None), P("dp", None, "frame")),
        check_vma=False,
    )
```

time: 194 us -> 199 us (1.026); the launches traced: 194 us -> 197 us
  blocking collectives: 0 us -> 26.2 us
  waiting for transfers between devices: 73 us -> 58.7 us
  matrix products: 16.9 us -> 6.11 us
  Pallas kernels: 17 us -> 27.2 us
  starting transfers between devices: 38 us -> 33.1 us
  other arithmetic: 21.1 us -> 16.6 us
    ppermute x1, waiting for transfers between devices: 42.4 us -> 6.47 us  [scatter_frames(): return keep + lax.ppermute(give, 'frame', FRAME_SIDE).astype(jnp.float32)]
    all_to_all x0 -> x1, blocking collectives: none -> 26.2 us  [exchange_terms(): lax.all_to_all(term.reshape(groups, term.shape[0] // groups, term.shape[1...]
    ppermute x1, waiting for transfers between devices: 0.01 us -> 20.4 us  [gather_frames(): far = lax.ppermute(rows, 'frame', FRAME_SIDE)]
    dot_general x3 -> x2, matrix products: 16.9 us -> 6.11 us  [per_device(): lax.dot_general(grad, weight, NT, preferred_element_type=F32)]
    pallas_call x1 -> x2, Pallas kernels: 17 us -> 27.2 us  [attention(): pl.pallas_call(body, out_shape=(jax.ShapeDtypeStruct((rows, columns), BF1...]
    convert_element_type x2 -> x0, local copies, waits for them, and re-layouts: 8.37 us -> none  [the longest x1 4.48 us: per_device(): term.astype(jnp.bfloat16).reshape(groups, own_rows, 3 * head_cols)]
    unnamed x19 -> x44, local copies, waits for them, and re-layouts: 3.64 us -> 9.37 us
    all_to_all x3 -> x4, waiting for transfers between devices: 30.6 us -> 31.7 us  [the longest x1 16.7 us: exchange_terms(): lax.all_to_all(term.reshape(groups, term.shape[0] // groups, term.shape[1...]
  transfers between devices with their start and end apart: 7 -> 8, of which waited for: 3 -> 5; matrix products, arithmetic and copies ran while one was open for 20% -> 14% of each run, Pallas kernels for 0% -> 6%
where the time goes in v3:
time: 199 us; the launch traced here: 197 us
  waiting for transfers between devices  58.7 us (29%)
  starting transfers between devices  33.1 us (17%)
  local copies, waits for them, and re-layouts  27.8 us (14%)
  Pallas kernels  27.2 us (14%)
  blocking collectives  26.2 us (13%)
  other arithmetic  16.6 us (8%)
  matrix products  6.11 us (3%)
    pallas_call x2, Pallas kernels, attention(): pl.pallas_call(body, out_shape=(jax.ShapeDtypeStruct((rows, columns), BF1...  27.2 us
    all_to_all x1, blocking collectives, exchange_terms(): lax.all_to_all(term.reshape(groups, term.shape[0] // groups, term.shape[1...  26.2 us
    ppermute x1, waiting for transfers between devices, gather_frames(): far = lax.ppermute(rows, 'frame', FRAME_SIDE)  20.4 us
    all_to_all x2, starting transfers between devices, gather_weight(): lax.all_to_all(jnp.broadcast_to(shard[None], (groups,) + shard.shape), 'd...  17.4 us
    all_to_all x1, waiting for transfers between devices, exchange_terms(): lax.all_to_all(term.reshape(groups, term.shape[0] // groups, term.shape[1...  16.7 us
    all_to_all x1, waiting for transfers between devices, per_device(): lax.all_to_all(thinker.reshape(think_rows, frame_count, head_cols), 'fram...  11.8 us
    unnamed x44, local copies, waits for them, and re-layouts  9.37 us
    ppermute x1, waiting for transfers between devices, scatter_frames(): return keep + lax.ppermute(give, 'frame', FRAME_SIDE).astype(jnp.float32)  6.47 us
  transfers between devices with their start and end apart: 8, of which 5 were waited for; matrix products, arithmetic and copies ran while one was open for 14% of the time, Pallas kernels for 6%

profile of v3, /device:TPU:1, one launch (start us, length us, event | category | flops | bytes accessed | tf_op | source)
XLA Modules:
  0.0 196.8 jit_solution(16954906573300232909)
XLA Ops:
  2.8 9.8 %all-to-all-start = ((bf16[32,40,384]{2,1,0:T(8,128)(2,1)}), bf16[32,40,384]{2,1,0:T(8,128)(2,1)S(1)}, u32[]{:S(2)}, u32[]{:S(2)}) async-start(bf16[32,40,384]{2,1,0:T(8,128)(2,1)} %broadcast_in_dim.15), calls=%async_computation | async-start | bytes 1966080 | tf_op jit(solution)/shard_map/all_to_all | solution.py:232
  13.5 2.7 %collective-permute-start = (bf16[256,1280]{1,0:T(8,128)(2,1)S(1)}, bf16[256,1280]{1,0:T(8,128)(2,1)S(1)}, u32[]{:S(2)}, u32[]{:S(2)}) collective-permute-start(bf16[256,1280]{1,0:T(8,128)(2,1)S(1)} %fusion.6), channel_id=1, source_target_pairs={{0,2},{1,3},{2,0},{3,1},{4,6},{5,7},{6,4},{7,5},{8,10},{9,11},{10,... | collective-permute-start | bytes 1966088 | tf_op jit(solution)/shard_map/ppermute | solution.py:255
  19.5 20.4 %collective-permute-done = bf16[256,1280]{1,0:T(8,128)(2,1)S(1)} collective-permute-done((bf16[256,1280]{1,0:T(8,128)(2,1)S(1)}, bf16[256,1280]{1,0:T(8,128)(2,1)S(1)}, u32[]{:S(2)}, u32[]{:S(2)}) %collective-permute-start) | collective-permute-done | bytes 655392 | tf_op jit(solution)/shard_map/ppermute | solution.py:255
  45.3 3.5 %all-to-all-start.1 = ((bf16[384,4,320]{0,2,1:T(8,128)(2,1)}), bf16[384,4,320]{0,2,1:T(8,128)(2,1)S(1)}, u32[]{:S(2)}, u32[]{:S(2)}) async-start(bf16[384,4,320]{0,2,1:T(8,128)(2,1)} %bitcast.123), calls=%async_computation.1 | async-start | bytes 1966080 | tf_op jit(solution)/shard_map/all_to_all | solution.py:287
  51.2 11.8 %all-to-all-done.1 = bf16[384,4,320]{0,2,1:T(8,128)(2,1)S(1)} async-done(((bf16[384,4,320]{0,2,1:T(8,128)(2,1)}), bf16[384,4,320]{0,2,1:T(8,128)(2,1)S(1)}, u32[]{:S(2)}, u32[]{:S(2)}) %all-to-all-start.1) | async-done | bytes 983072 | tf_op jit(solution)/shard_map/all_to_all | solution.py:287
  63.8 3.9 %gather_fusion.4 = bf16[1024,320]{1,0:T(8,128)(2,1)S(1)} fusion(bf16[1536,320]{1,0:T(8,128)(2,1)S(1)} %bitcast.121, s32[1024]{0:T(1024)S(1)} %fusion.16), kind=kCustom, calls=%fused_computation.4 | custom fusion | bytes 1314816 | tf_op jit(solution)/shard_map/jit(_take)/gather | solution.py:297
  69.3 7.6 %all-to-all-start.2 = ((bf16[32,40,576]{2,1,0:T(8,128)(2,1)}), bf16[32,40,576]{2,1,0:T(8,128)(2,1)S(1)}, u32[]{:S(2)}, u32[]{:S(2)}) async-start(bf16[32,40,576]{2,1,0:T(8,128)(2,1)} %broadcast_in_dim.23), calls=%async_computation.2 | async-start | bytes 3276800 | tf_op jit(solution)/shard_map/all_to_all | solution.py:232
  78.5 2.1 %maximum_select_fusion = bf16[2,2,256,1280]{3,2,0,1:T(8,128)(2,1)S(1)} fusion(bf16[2,1,256,1280]{3,2,0,1:T(8,128)(2,1)} %bitcast.15, bf16[2,1,256,1280]{3,2,0,1:T(8,128)(2,1)S(1)} %copy-done.10, pred[]{:T(512)S(6)} %eq.9), kind=kLoop, calls=%fused_computation.7 | loop fusion | flops 3932160 | bytes 5242881 | tf_op jit(solution)/shard_map/jit(_where)/select_n | solution.py:258
  81.7 11.4 %attention_backward.2 = (bf16[1024,384]{1,0:T(8,128)(2,1)S(1)}, bf16[1280,384]{1,0:T(8,128)(2,1)S(1)}) custom-call(s32[2,4]{1,0:T(2,128)S(1)} %pad_add_fusion.refs_0_, bf16[1024,1280]{1,0:T(8,128)(2,1)S(1)} %bitcast.113, bf16[1280,384]{1,0:T(8,128)(2,1)S(1)} %bitcast.111, bf16[1024,384]{1,0:T(8,128)(2,1)S(1)} %pad_maximum_fusion.refs_3_, s32[1024,1]{1,0:T(8,128)S(1)} %copy-done.6), custom_call_target="tpu_custom_call" | custom-call | flops 10000000000 | bytes 8000000 | tf_op jit(solution)/shard_map/attention_backward/pallas_call | solution.py:197
  95.6 3.2 %all-to-all-done.2 = bf16[32,40,576]{2,1,0:T(8,128)(2,1)S(1)} async-done(((bf16[32,40,576]{2,1,0:T(8,128)(2,1)}), bf16[32,40,576]{2,1,0:T(8,128)(2,1)S(1)}, u32[]{:S(2)}, u32[]{:S(2)}) %all-to-all-start.2) | async-done | bytes 1474592 | tf_op jit(solution)/shard_map/all_to_all | solution.py:232
  98.8 1.7 copy-done.1
  102.7 15.7 %attention_backward.3 = (bf16[1024,576]{1,0:T(8,128)(2,1)S(1)}, bf16[1280,576]{1,0:T(8,128)(2,1)}) custom-call(s32[2,4]{1,0:T(2,128)S(1)} %pad_add_fusion.refs_0_, bf16[1024,1280]{1,0:T(8,128)(2,1)S(1)} %bitcast.114, bf16[1280,576]{1,0:T(8,128)(2,1)S(1)} %bitcast.115, bf16[1024,384]{1,0:T(8,128)(2,1)S(1)} %copy-done.5, s32[1024,1]{1,0:T(8,128)S(1)} %copy-done.7), custom_call_target="tpu_custom_call" | custom-call | flops 15000000512 | bytes 8000000 | tf_op jit(solution)/shard_map/attention_backward/pallas_call | solution.py:197
  118.5 2.2 %fusion.23 = f32[1024,1280]{1,0:T(8,128)S(1)} fusion(bf16[1024,576]{1,0:T(8,128)(2,1)S(1)} %get-tuple-element.15, bf16[1280,576]{1,0:T(8,128)(2,1)S(1)} %bitcast.116), kind=kOutput, calls=%fused_computation.88 | convolution fusion | flops 1509949440 | bytes 7897088 | tf_op jit(solution)/shard_map/dot_general | solution.py:306
  120.7 3.9 %convolution_add_fusion = f32[1024,1280]{1,0:T(8,128)} fusion(f32[1024,1280]{1,0:T(8,128)S(1)} %fusion.23, bf16[1024,384]{1,0:T(8,128)(2,1)S(1)} %get-tuple-element.13, bf16[1280,384]{1,0:T(8,128)(2,1)S(1)} %bitcast.112), kind=kOutput, calls=%fused_computation.5 | convolution fusion | flops 1007943680 | bytes 12255232 | tf_op jit(solution)/shard_map/dot_general | solution.py:306
  124.6 2.0 fusion.12
  126.5 2.6 %collective-permute-start.2 = (bf16[2,256,1280]{2,1,0:T(8,128)(2,1)S(1)}, bf16[2,256,1280]{2,1,0:T(8,128)(2,1)}, u32[]{:S(2)}, u32[]{:S(2)}) collective-permute-start(bf16[2,256,1280]{2,1,0:T(8,128)(2,1)S(1)} %fusion.12), channel_id=1, source_target_pairs={{0,1},{1,0},{2,3},{3,2},{4,5},{5,4},{6,7},{7,6},{8,9},{9,8},{10,11... | collective-permute-start | bytes 3932168 | tf_op jit(solution)/shard_map/ppermute | solution.py:269
  129.1 26.2 %all_to_all.38 = bf16[32,40,384]{2,1,0:T(8,128)(2,1)S(1)} all-to-all(bf16[32,40,384]{2,1,0:T(8,128)(2,1)S(1)} %bitcast.117), channel_id=1, replica_groups=mesh['dp'=32,'frame'=4] {'dp'}, dimensions={0} | all-to-all | bytes 1966080 | tf_op jit(solution)/shard_map/all_to_all | solution.py:238
  155.4 4.7 %all-to-all-start.4 = ((bf16[32,40,576]{2,1,0:T(8,128)(2,1)}), bf16[32,40,576]{2,1,0:T(8,128)(2,1)}, u32[]{:S(2)}, u32[]{:S(2)}) async-start(bf16[32,40,576]{2,1,0:T(8,128)(2,1)} %bitcast.46), calls=%async_computation.4 | async-start | bytes 3276800 | tf_op jit(solution)/shard_map/all_to_all | solution.py:238
  160.3 2.4 %bitcast_add_fusion = f32[2,256,1280]{2,1,0:T(8,128)S(1)} fusion(bf16[2,256,1280]{2,1,0:T(8,128)(2,1)} %collective-permute-done.2, f32[2,2,256,1280]{3,2,1,0:T(8,128)} %bitcast.40, s32[]{:T(128)S(6)} %select_n.147), kind=kLoop, calls=%fused_computation.9 | loop fusion | flops 1310720 | bytes 6553604 | tf_op jit(solution)/shard_map/add | solution.py:269
  165.0 16.7 %all-to-all-done.4 = bf16[32,40,576]{2,1,0:T(8,128)(2,1)} async-done(((bf16[32,40,576]{2,1,0:T(8,128)(2,1)}), bf16[32,40,576]{2,1,0:T(8,128)(2,1)}, u32[]{:S(2)}, u32[]{:S(2)}) %all-to-all-start.4) | async-done | bytes 1474592 | tf_op jit(solution)/shard_map/all_to_all | solution.py:238
  181.7 1.7 convert_reduce_fusion
  186.3 6.5 %collective-permute-done.3 = bf16[256,1280]{1,0:T(8,128)(2,1)} collective-permute-done((bf16[256,1280]{1,0:T(8,128)(2,1)}, bf16[256,1280]{1,0:T(8,128)(2,1)}, u32[]{:S(2)}, u32[]{:S(2)}) %collective-permute-start.3) | collective-permute-done | bytes 655392 | tf_op jit(solution)/shard_map/ppermute | solution.py:272
  192.8 1.6 fusion.15
  194.4 2.4 %fusion.10 = bf16[256,1280]{1,0:T(8,128)(2,1)} fusion(bf16[256,1280]{1,0:T(8,128)(2,1)S(1)} %copy-done.9, f32[256]{0:T(256)S(1)} %broadcast_multiply_fusion, f32[256]{0:T(256)S(1)} %broadcast_multiply_fusion.1, f32[256]{0:T(256)S(1)} %copy-done.19, f32[256]{0:T(256)S(1)} %copy-done.17, f32[1280]{0:T(1024)S(1)} %copy-done.14, ...), kind=kLoop, calls=%fused_computation.23 | loop fusion | flops 3604480 | bytes 3286020 | tf_op jit(solution)/shard_map/convert_element_type | solution.py:33
  (103 shorter events, 28.8 us)
Async XLA Ops:
  1.7 10.9 %copy-start.8 = (bf16[256,1280]{1,0:T(8,128)(2,1)S(1)}, bf16[256,1280]{1,0:T(8,128)(2,1)}, u32[]{:S(2)}) copy-start(bf16[256,1280]{1,0:T(8,128)(2,1)} %param.7) | copy-start | bytes 1966084
  2.8 10.4 %copy-start.14 = (f32[1280]{0:T(1024)S(1)}, f32[1280]{0:T(1024)}, u32[]{:S(2)}) copy-start(f32[1280]{0:T(1024)} %param.11) | copy-start | bytes 15364
  2.8 10.4 %copy-start.15 = (f32[1280]{0:T(1024)S(1)}, f32[1280]{0:T(1024)}, u32[]{:S(2)}) copy-start(f32[1280]{0:T(1024)} %param.12) | copy-start | bytes 15364
  2.8 41.1 %all-to-all-start = ((bf16[32,40,384]{2,1,0:T(8,128)(2,1)}), bf16[32,40,384]{2,1,0:T(8,128)(2,1)S(1)}, u32[]{:S(2)}, u32[]{:S(2)}) async-start(bf16[32,40,384]{2,1,0:T(8,128)(2,1)} %broadcast_in_dim.15), calls=%async_computation | async-start | bytes 1966080 | tf_op jit(solution)/shard_map/all_to_all | solution.py:232
  12.6 3.6 %copy-start.20 = (s32[1024]{0:T(1024)S(1)}, s32[1024]{0:T(1024)}, u32[]{:S(2)}) copy-start(s32[1024]{0:T(1024)} %param.9) | copy-start | bytes 12292
  12.6 3.6 %copy-start.21 = (s32[1,3]{1,0:T(1,128)S(1)}, s32[1,3]{1,0:T(1,128)}, u32[]{:S(2)}) copy-start(s32[1,3]{1,0:T(1,128)} %param.8) | copy-start | bytes 40
  12.8 35.9 %copy-start.16 = (f32[256]{0:T(256)}, f32[256]{0:T(256)S(1)}, u32[]{:S(2)}) copy-start(f32[256]{0:T(256)S(1)} %broadcast_multiply_fusion.2) | copy-start | bytes 3076
  13.2 35.6 %copy-start.18 = (f32[256]{0:T(256)}, f32[256]{0:T(256)S(1)}, u32[]{:S(2)}) copy-start(f32[256]{0:T(256)S(1)} %add_rsqrt_fusion) | copy-start | bytes 3076
  13.5 26.4 %collective-permute-start = (bf16[256,1280]{1,0:T(8,128)(2,1)S(1)}, bf16[256,1280]{1,0:T(8,128)(2,1)S(1)}, u32[]{:S(2)}, u32[]{:S(2)}) collective-permute-start(bf16[256,1280]{1,0:T(8,128)(2,1)S(1)} %fusion.6), channel_id=1, source_target_pairs={{0,2},{1,3},{2,0},{3,1},{4,6},{5,7},{6,4},{7,5},{8,10},{9,11},{10,... | collective-permute-start | bytes 1966088 | tf_op jit(solution)/shard_map/ppermute | solution.py:255
  39.9 4.0 %copy-start.13 = (bf16[384,1280]{1,0:T(8,128)(2,1)S(1)}, bf16[384,1280]{1,0:T(8,128)(2,1)}, u32[]{:S(2)}) copy-start(bf16[384,1280]{1,0:T(8,128)(2,1)} %param.10) | copy-start | bytes 2949124
  41.2 35.9 %collective-permute-start.1 = (bf16[2,256,1280]{2,1,0:T(8,128)(2,1)}, bf16[2,256,1280]{2,1,0:T(8,128)(2,1)}, u32[]{:S(2)}, u32[]{:S(2)}) collective-permute-start(bf16[2,256,1280]{2,1,0:T(8,128)(2,1)} %maximum_select_fusion.2), channel_id=1, source_target_pairs={{0,1},{1,0},{2,3},{3,2},{4,5},{5,4},{6,7},{7,6},{8,9},{9,8},{10,11... | collective-permute-start | bytes 3932168 | tf_op jit(solution)/shard_map/ppermute | solution.py:257
  45.3 17.8 %all-to-all-start.1 = ((bf16[384,4,320]{0,2,1:T(8,128)(2,1)}), bf16[384,4,320]{0,2,1:T(8,128)(2,1)S(1)}, u32[]{:S(2)}, u32[]{:S(2)}) async-start(bf16[384,4,320]{0,2,1:T(8,128)(2,1)} %bitcast.123), calls=%async_computation.1 | async-start | bytes 1966080 | tf_op jit(solution)/shard_map/all_to_all | solution.py:287
  69.3 29.5 %all-to-all-start.2 = ((bf16[32,40,576]{2,1,0:T(8,128)(2,1)}), bf16[32,40,576]{2,1,0:T(8,128)(2,1)S(1)}, u32[]{:S(2)}, u32[]{:S(2)}) async-start(bf16[32,40,576]{2,1,0:T(8,128)(2,1)} %broadcast_in_dim.23), calls=%async_computation.2 | async-start | bytes 3276800 | tf_op jit(solution)/shard_map/all_to_all | solution.py:232
  76.9 1.6 copy-start.10
  77.1 3.7 %copy-start.4 = (bf16[1024,384]{1,0:T(8,128)(2,1)}, bf16[1024,384]{1,0:T(8,128)(2,1)S(1)}, u32[]{:S(2)}) copy-start(bf16[1024,384]{1,0:T(8,128)(2,1)S(1)} %pad_maximum_fusion.refs_3_) | copy-start | bytes 2359300
  93.1 1.5 copy-start
  98.8 1.7 copy-start.1
  124.6 4.5 %copy-start.3 = (bf16[1280,384]{1,0:T(8,128)(2,1)S(1)}, bf16[1280,384]{1,0:T(8,128)(2,1)}, u32[]{:S(2)}) copy-start(bf16[1280,384]{1,0:T(8,128)(2,1)} %copy-done.2) | copy-start | bytes 2949124
  126.5 33.7 %collective-permute-start.2 = (bf16[2,256,1280]{2,1,0:T(8,128)(2,1)S(1)}, bf16[2,256,1280]{2,1,0:T(8,128)(2,1)}, u32[]{:S(2)}, u32[]{:S(2)}) collective-permute-start(bf16[2,256,1280]{2,1,0:T(8,128)(2,1)S(1)} %fusion.12), channel_id=1, source_target_pairs={{0,1},{1,0},{2,3},{3,2},{4,5},{5,4},{6,7},{7,6},{8,9},{9,8},{10,11... | collective-permute-start | bytes 3932168 | tf_op jit(solution)/shard_map/ppermute | solution.py:269
  155.4 26.3 %all-to-all-start.4 = ((bf16[32,40,576]{2,1,0:T(8,128)(2,1)}), bf16[32,40,576]{2,1,0:T(8,128)(2,1)}, u32[]{:S(2)}, u32[]{:S(2)}) async-start(bf16[32,40,576]{2,1,0:T(8,128)(2,1)} %bitcast.46), calls=%async_computation.4 | async-start | bytes 3276800 | tf_op jit(solution)/shard_map/all_to_all | solution.py:238
  163.6 29.2 %collective-permute-start.3 = (bf16[256,1280]{1,0:T(8,128)(2,1)}, bf16[256,1280]{1,0:T(8,128)(2,1)}, u32[]{:S(2)}, u32[]{:S(2)}) collective-permute-start(bf16[256,1280]{1,0:T(8,128)(2,1)} %fusion.14), channel_id=1, source_target_pairs={{0,2},{1,3},{2,0},{3,1},{4,6},{5,7},{6,4},{7,5},{8,10},{9,11},{10,... | collective-permute-start | bytes 1966088 | tf_op jit(solution)/shard_map/ppermute | solution.py:272
  165.0 27.8 %copy-start.9 = (bf16[256,1280]{1,0:T(8,128)(2,1)S(1)}, bf16[256,1280]{1,0:T(8,128)(2,1)}, u32[]{:S(2)}) copy-start(bf16[256,1280]{1,0:T(8,128)(2,1)} %param.7) | copy-start | bytes 1966084
  165.0 27.8 %copy-start.17 = (f32[256]{0:T(256)S(1)}, f32[256]{0:T(256)}, u32[]{:S(2)}) copy-start(f32[256]{0:T(256)} %copy-done.16) | copy-start | bytes 3076
  186.3 8.1 %copy-start.19 = (f32[256]{0:T(256)S(1)}, f32[256]{0:T(256)}, u32[]{:S(2)}) copy-start(f32[256]{0:T(256)} %copy-done.18) | copy-start | bytes 3076
  (6 other events, 6.5 us)

commit v4 on v3

--- a/solution.py
+++ b/solution.py
@@ -33,12 +33,6 @@
     return result.astype(jnp.bfloat16)
 
 
-def segment_ids(lengths, count):
-    ends = jnp.cumsum(lengths)
-    frame_ids = jnp.arange(count, dtype=jnp.int32)
-    return jnp.sum((frame_ids[:, None] >= ends[None, :]).astype(jnp.int32), axis=1)
-
-
 NEG = -1e30
 F32 = jnp.float32
 BF16 = jnp.bfloat16
@@ -61,11 +55,19 @@
     return tuple(blocks)
 
 
+def block_rows(place, j):
+    return pl.ds(pl.multiple_of((place ^ j) * ROWS, ROWS), ROWS)
+
+
 def attention_kernel(
-    heads, bounds, norm_ref, weight_ref, grad_ref, seg_ref, out_ref, term_ref,
-    q_aug, q_pad, k_aug, k_pad, v_pad, g_pad, score, dprob, kv_acc, dq_acc,
+    heads, lengths, place, own, near, far, far_near, weight_ref, grad_ref, out_ref, term_ref,
+    norm_ref, q_aug, q_pad, k_aug, k_pad, v_pad, g_pad, score, dprob, kv_acc, dq_acc,
 ):
     rows = norm_ref.shape[0]
+    first_end = lengths[0]
+    second_end = first_end + lengths[1]
+    for j, piece in enumerate((own, near, far, far_near)):
+        norm_ref[block_rows(place[0], j), :] = piece[...]
     count = len(heads)
     width = weight_ref.shape[1]
     scale = HD ** (-0.5)
@@ -73,7 +75,8 @@
     def prepare(i, carry):
         r = pl.ds(pl.multiple_of(i * ROWS, ROWS), ROWS)
         lane = lax.broadcasted_iota(jnp.int32, (ROWS, 128), 1)
-        seg = seg_ref[r, :]
+        frame = i * ROWS + lax.broadcasted_iota(jnp.int32, (ROWS, 128), 0)
+        seg = (frame >= first_end).astype(jnp.int32) + (frame >= second_end).astype(jnp.int32)
         proj = jnp.dot(norm_ref[r, :], weight_ref[...], preferred_element_type=F32)
         proj = proj.astype(BF16).astype(F32)
         for n, h in enumerate(heads):
@@ -103,7 +106,10 @@
 
     def query_block(qb, carry):
         qr = pl.ds(pl.multiple_of(qb * QB, QB), QB)
-        lo, hi = bounds[0, qb], bounds[1, qb]
+        head_row, tail_row = qb * QB, qb * QB + (QB - 1)
+        start = jnp.where(head_row >= second_end, second_end, jnp.where(head_row >= first_end, first_end, 0))
+        end = jnp.where(tail_row >= second_end, rows, jnp.where(tail_row >= first_end, second_end, first_end))
+        lo, hi = start // KT, (end + (KT - 1)) // KT
 
         def first(t, tops):
             kr = pl.ds(pl.multiple_of(t * KT, KT), KT)
@@ -176,21 +182,14 @@
         term_ref[256 * i:256 * i + 256, :] = part.astype(BF16)
 
 
-def key_bounds(segments, lengths):
-    rows = segments.shape[0]
-    ends = jnp.cumsum(lengths)
-    starts = ends - lengths
-    first_row = jnp.arange(rows // QB, dtype=jnp.int32) * QB
-    lo = starts[segments[first_row]] // KT
-    hi = (ends[segments[first_row + (QB - 1)]] + KT - 1) // KT
-    return jnp.stack([lo, hi]).astype(jnp.int32)
-
-
-def attention(heads, normalized, weight, out_grad, segments, bounds):
-    rows, features = normalized.shape
-    columns = weight.shape[1]
+VM = pl.BlockSpec(memory_space=pltpu.VMEM)
+SM = pl.BlockSpec(memory_space=pltpu.SMEM)
+
+
+def attention(heads, lengths, place, pieces, weight, out_grad):
+    features, columns = weight.shape
+    rows = out_grad.shape[0]
     count = len(heads)
-    vm = pl.BlockSpec(memory_space=pltpu.VMEM)
     tall = pltpu.VMEM((count, rows, 128), BF16)
     wide = pltpu.VMEM((count, rows, QB), F32)
     body = lambda *refs: attention_kernel(heads, *refs)
@@ -200,15 +199,39 @@
             jax.ShapeDtypeStruct((rows, columns), BF16),
             jax.ShapeDtypeStruct((features, columns), BF16),
         ),
-        in_specs=[pl.BlockSpec(memory_space=pltpu.SMEM), vm, vm, vm, vm],
-        out_specs=(vm, vm),
-        scratch_shapes=[tall] * 6 + [wide, wide, pltpu.VMEM((count, rows, 128), F32), pltpu.VMEM(((count + 1) // 2, QB, 128), F32)],
+        in_specs=[SM, SM] + [VM] * 6,
+        out_specs=(VM, VM),
+        scratch_shapes=[pltpu.VMEM((rows, features), BF16)] + [tall] * 6 + [
+            wide, wide, pltpu.VMEM((count, rows, 128), F32), pltpu.VMEM(((count + 1) // 2, QB, 128), F32)
+        ],
         compiler_params=pltpu.CompilerParams(vmem_limit_bytes=40 << 20),
         cost_estimate=pl.CostEstimate(
             flops=5_000_000_000 * count, bytes_accessed=8_000_000, transcendentals=1_000_000 * count
         ),
         name="attention_backward",
-    )(bounds, normalized, weight, out_grad, segments)
+    )(lengths, place, *pieces, weight, out_grad)
+
+
+def norm_grad_kernel(keep_at, give_at, place, grad_0, grad_1, weight_0, weight_1, keep_ref, give_ref):
+    for at, ref in ((give_at, give_ref), (keep_at, keep_ref)):
+        r = block_rows(place[0], at)
+        total = lax.dot_general(grad_0[r, :], weight_0[...], NT, preferred_element_type=F32)
+        total += lax.dot_general(grad_1[r, :], weight_1[...], NT, preferred_element_type=F32)
+        ref[...] = total.astype(ref.dtype)
+
+
+def norm_grad_blocks(keep_at, give_at, place, grads, weights):
+    shape = (ROWS, weights[0].shape[0])
+    body = lambda *refs: norm_grad_kernel(keep_at, give_at, *refs)
+    return pl.pallas_call(
+        body,
+        out_shape=(jax.ShapeDtypeStruct(shape, F32), jax.ShapeDtypeStruct(shape, BF16)),
+        in_specs=[SM] + [VM] * 4,
+        out_specs=(VM, VM),
+        compiler_params=pltpu.CompilerParams(vmem_limit_bytes=24 << 20),
+        cost_estimate=pl.CostEstimate(flops=1_300_000_000, bytes_accessed=6_000_000, transcendentals=0),
+        name="norm_grad",
+    )(place, *grads, *weights)
 
 
 CHUNKS = ((0, 1), (2, 3, 4))
@@ -249,62 +272,50 @@
 FRAME_CORE = [(0, 1), (1, 0), (2, 3), (3, 2)]
 
 
-def gather_frames(rows):
-    core = lax.axis_index("frame") % 2
-    side = lax.axis_index("frame") // 2
-    far = lax.ppermute(rows, "frame", FRAME_SIDE)
-    mine = jnp.where(side == 0, jnp.stack([rows, far]), jnp.stack([far, rows]))
-    other = lax.ppermute(mine, "frame", FRAME_CORE)
-    pair = jnp.where(core == 0, jnp.stack([mine, other], axis=1), jnp.stack([other, mine], axis=1))
-    return pair.reshape(4 * rows.shape[0], rows.shape[1])
-
-
-def scatter_frames(total):
-    core = lax.axis_index("frame") % 2
-    side = lax.axis_index("frame") // 2
-    quarter = total.shape[0] // 4
-    blocks = total.reshape(2, 2, quarter, total.shape[1])
-    keep = lax.dynamic_index_in_dim(blocks, core, 1, keepdims=False)
-    give = lax.dynamic_index_in_dim(blocks, 1 - core, 1, keepdims=False).astype(jnp.bfloat16)
-    half = keep + lax.ppermute(give, "frame", FRAME_CORE).astype(jnp.float32)
-    keep = lax.dynamic_index_in_dim(half, side, 0, keepdims=False)
-    give = lax.dynamic_index_in_dim(half, 1 - side, 0, keepdims=False).astype(jnp.bfloat16)
-    return keep + lax.ppermute(give, "frame", FRAME_SIDE).astype(jnp.float32)
+def swap_side(block):
+    return lax.ppermute(block, "frame", FRAME_SIDE)
+
+
+def swap_core(block):
+    return lax.ppermute(block, "frame", FRAME_CORE)
 
 
 def per_device(
     hidden_in, rec_lengths, token_positions, thinker_grad, norm_gain, norm_bias, qkv_weight
 ):
-    frame_count = lax.axis_size("frame")
     head_cols = qkv_weight.shape[2]
-    group_frames = token_positions.shape[0]
     think_rows = thinker_grad.shape[0]
+    place = lax.axis_index("frame")
+    side, core = place // 2, place % 2
     shards = [pack_columns(qkv_weight, heads) for heads in CHUNKS]
-    normalized, standard, inv_std = norm_forward(hidden_in, norm_gain, norm_bias)
     weights = [gather_weight(shards[0])]
-    normalized = gather_frames(normalized)
-    thinker, weights[0] = lax.optimization_barrier((thinker_grad, weights[0]))
-    moved = lax.all_to_all(
-        thinker.reshape(think_rows, frame_count, head_cols),
-        "frame",
-        split_axis=1,
-        concat_axis=0,
-        tiled=True,
-    )
-    shard, moved = lax.optimization_barrier((shards[1], moved))
+    own, standard, inv_std = norm_forward(hidden_in, norm_gain, norm_bias)
+    far = swap_side(own)
+    near = swap_core(own)
+    sides = [lax.dynamic_slice_in_dim(thinker_grad, 2 * head_cols * at, 2 * head_cols, 1) for at in (side, 1 - side)]
+    far_think = swap_side(sides[1])
+    cols = lambda block, at: lax.dynamic_slice_in_dim(block, head_cols * at, head_cols, 1)
+    near_think = swap_core(cols(sides[0], 1 - core))
+    far_near = swap_core(far)
+    far_near_think = swap_core(cols(far_think, 1 - core))
+    shard, weights[0] = lax.optimization_barrier((shards[1], weights[0]))
     weights.append(gather_weight(shard))
-    moved = moved.reshape(frame_count * think_rows, head_cols)
-    out_grad = grad_tiles(jnp.take(moved, token_positions, axis=0))
-    segments = segment_ids(rec_lengths[0], group_frames)
-    bounds = key_bounds(segments, rec_lengths[0])
-    segments = segments.reshape(group_frames, 1)
+    moved = jnp.concatenate([cols(sides[0], core), near_think, cols(far_think, core), far_near_think], axis=0)
+    rows_at = ((token_positions // think_rows) ^ place) * think_rows + token_positions % think_rows
+    out_grad = grad_tiles(jnp.take(moved, rows_at, axis=0))
+    pieces = (own, near, far, far_near)
+    at = place.reshape(1)
     grads, terms = [], []
     for heads, weight in zip(CHUNKS, weights):
-        grad, term = attention(heads, normalized, weight, out_grad, segments, bounds)
+        grad, term = attention(heads, rec_lengths[0], at, pieces, weight, out_grad)
         grads.append(grad)
         terms.append(exchange_terms(term))
-    partial = sum(lax.dot_general(grad, weight, NT, preferred_element_type=F32) for grad, weight in zip(grads, weights))
-    norm_grad = scatter_frames(partial)
+    keep, give = norm_grad_blocks(2, 3, at, grads, weights)
+    got = swap_core(give)
+    side_sum = swap_side((keep + got.astype(F32)).astype(BF16))
+    keep, give = norm_grad_blocks(0, 1, at, grads, weights)
+    core_sum = swap_core(give)
+    norm_grad = keep + core_sum.astype(F32) + side_sum.astype(F32)
     weight_grad = unpack_columns([jnp.sum(term.astype(F32), axis=0) for term in terms])
     hidden_grad = norm_backward(norm_grad, standard, inv_std, norm_gain)
     return (hidden_grad, weight_grad)

time: 199 us -> 160 us (0.80)
  blocking collectives: 26.2 us -> 0 us
  local copies, waits for them, and re-layouts: 27.8 us -> 16.4 us
  starting transfers between devices: 33.1 us -> 42.9 us
  Pallas kernels: 27.2 us -> 34.5 us
  matrix products: 6.11 us -> 0 us
  other arithmetic: 16.6 us -> 10.9 us
  waiting for transfers between devices: 58.7 us -> 53.1 us
    all_to_all x1 -> x0, blocking collectives: 26.2 us -> none  [exchange_terms(): lax.all_to_all(term.reshape(groups, term.shape[0] // groups, term.shape[1...]
    all_to_all x1 -> x0, waiting for transfers between devices: 11.8 us -> none  [per_device(): lax.all_to_all(thinker.reshape(think_rows, frame_count, head_cols), 'fram...]
    all_to_all x1 -> x2, starting transfers between devices: 4.71 us -> 12.7 us  [exchange_terms(): lax.all_to_all(term.reshape(groups, term.shape[0] // groups, term.shape[1...]
    ppermute x4 -> x9, waiting for transfers between devices: 26.9 us -> 34.2 us  [the longest x3 34.2 us: swap_side(): return lax.ppermute(block, 'frame', FRAME_SIDE)]
    dot_general x2 -> x0, matrix products: 6.11 us -> none  [per_device(): lax.dot_general(grad, weight, NT, preferred_element_type=F32)]
    all_to_all x1 -> x2, waiting for transfers between devices: 16.7 us -> 11.2 us  [exchange_terms(): lax.all_to_all(term.reshape(groups, term.shape[0] // groups, term.shape[1...]
    select_n x9 -> x1, other arithmetic: 4.97 us -> 0.21 us  [per_device(): out_grad = grad_tiles(jnp.take(moved, rows_at, axis=0))]
    ppermute x4 -> x9, starting transfers between devices: 7.48 us -> 12 us  [the longest x3 6.36 us: swap_side(): return lax.ppermute(block, 'frame', FRAME_SIDE)]
  transfers between devices with their start and end apart: 8 -> 13, of which waited for: 5 -> 5; matrix products, arithmetic and copies ran while one was open for 14% -> 11% of each run, Pallas kernels for 6% -> 9%
where the time goes in v4:
time: 160 us; the launch traced here: 159 us
  waiting for transfers between devices  53.1 us (33%)
  starting transfers between devices  42.9 us (27%)
  Pallas kernels  34.5 us (22%)
  local copies, waits for them, and re-layouts  16.4 us (10%)
  other arithmetic  10.9 us (7%)
    ppermute x3, waiting for transfers between devices, swap_side(): return lax.ppermute(block, 'frame', FRAME_SIDE)  34.2 us
    pallas_call x2, Pallas kernels, attention(): pl.pallas_call(body, out_shape=(jax.ShapeDtypeStruct((rows, columns), BF1...  29.9 us
    all_to_all x2, starting transfers between devices, gather_weight(): lax.all_to_all(jnp.broadcast_to(shard[None], (groups,) + shard.shape), 'd...  18.2 us
    all_to_all x2, starting transfers between devices, exchange_terms(): lax.all_to_all(term.reshape(groups, term.shape[0] // groups, term.shape[1...  12.7 us
    all_to_all x2, waiting for transfers between devices, exchange_terms(): lax.all_to_all(term.reshape(groups, term.shape[0] // groups, term.shape[1...  11.2 us
    all_to_all x2, waiting for transfers between devices, gather_weight(): lax.all_to_all(jnp.broadcast_to(shard[None], (groups,) + shard.shape), 'd...  7.7 us
    ppermute x3, starting transfers between devices, swap_side(): return lax.ppermute(block, 'frame', FRAME_SIDE)  6.36 us
    unnamed x38, local copies, waits for them, and re-layouts  5.91 us
  transfers between devices with their start and end apart: 13, of which 5 were waited for; matrix products, arithmetic and copies ran while one was open for 11% of the time, Pallas kernels for 9%

profile of v4, /device:TPU:1, one launch (start us, length us, event | category | flops | bytes accessed | tf_op | source)
XLA Modules:
  0.0 158.7 jit_solution(1110680120225930941)
XLA Ops:
  0.7 1.9 %constant_dynamic-slice_fusion.2 = bf16[384,640]{1,0:T(8,128)(2,1)} fusion(bf16[384,1280]{1,0:T(8,128)(2,1)} %param.10, s32[]{:T(128)S(6)} %select_n.61), kind=kLoop, calls=%fused_computation.52 | loop fusion | bytes 983044 | tf_op jit(solution)/shard_map/dynamic_slice | solution.py:295
  2.6 3.7 %collective-permute-start.4 = (bf16[384,640]{1,0:T(8,128)(2,1)}, bf16[384,640]{1,0:T(8,128)(2,1)S(1)}, u32[]{:S(2)}, u32[]{:S(2)}) collective-permute-start(bf16[384,640]{1,0:T(8,128)(2,1)} %constant_dynamic-slice_fusion.2), channel_id=1, source_target_pairs={{0,2},{1,3},{2,0},{3,1},{4,6},{5,7},{6,4},{7,5},{8,10},{9,11},{10,... | collective-permute-start | bytes 1474568 | tf_op jit(solution)/shard_map/ppermute | solution.py:276
  10.5 9.0 %all-to-all-start = ((bf16[32,40,384]{2,1,0:T(8,128)(2,1)}), bf16[32,40,384]{2,1,0:T(8,128)(2,1)S(1)}, u32[]{:S(2)}, u32[]{:S(2)}) async-start(bf16[32,40,384]{2,1,0:T(8,128)(2,1)} %broadcast_in_dim.15), calls=%async_computation | async-start | bytes 1966080 | tf_op jit(solution)/shard_map/all_to_all | solution.py:255
  21.6 17.7 %collective-permute-done.1.refs_4_ = bf16[256,1280]{1,0:T(8,128)(2,1)} collective-permute-done((bf16[256,1280]{1,0:T(8,128)(2,1)}, bf16[256,1280]{1,0:T(8,128)(2,1)}, u32[]{:S(2)}, u32[]{:S(2)}) %collective-permute-start.1) | collective-permute-done | bytes 655392 | tf_op jit(solution)/shard_map/ppermute | solution.py:276
  39.3 2.6 %collective-permute-start.2 = (bf16[256,1280]{1,0:T(8,128)(2,1)}, bf16[256,1280]{1,0:T(8,128)(2,1)}, u32[]{:S(2)}, u32[]{:S(2)}) collective-permute-start(bf16[256,1280]{1,0:T(8,128)(2,1)} %collective-permute-done.1.refs_4_), channel_id=1, source_target_pairs={{0,1},{1,0},{2,3},{3,2},{4,5},{5,4},{6,7},{7,6},{8,9},{9,8},{10,11... | collective-permute-start | bytes 1966088 | tf_op jit(solution)/shard_map/ppermute | solution.py:280
  42.9 3.9 %gather_fusion = bf16[1024,320]{1,0:T(8,128)(2,1)S(1)} fusion(bf16[1536,320]{1,0:T(8,128)(2,1)S(1)} %pad_maximum_fusion, s32[1024]{0:T(1024)S(1)} %broadcast_clamp_fusion), kind=kCustom, calls=%fused_computation | custom fusion | bytes 1314816 | tf_op jit(solution)/shard_map/jit(_take)/gather | solution.py:305
  46.9 1.4 broadcast_in_dim.39
  48.3 9.2 %all-to-all-start.1 = ((bf16[32,40,576]{2,1,0:T(8,128)(2,1)}), bf16[32,40,576]{2,1,0:T(8,128)(2,1)S(1)}, u32[]{:S(2)}, u32[]{:S(2)}) async-start(bf16[32,40,576]{2,1,0:T(8,128)(2,1)} %broadcast_in_dim.39), calls=%async_computation.1 | async-start | bytes 3276800 | tf_op jit(solution)/shard_map/all_to_all | solution.py:255
  58.4 12.8 %attention_backward.2 = (bf16[1024,384]{1,0:T(8,128)(2,1)S(1)}, bf16[1280,384]{1,0:T(8,128)(2,1)S(1)}) custom-call(s32[3]{0:T(128)S(1)} %bitcast.47, s32[1]{0:T(128)} %bitcast.refs_1_.refs_0_, bf16[256,1280]{1,0:T(8,128)(2,1)} %fusion.6.refs_2_, bf16[256,1280]{1,0:T(8,128)(2,1)} %collective-permute-done.refs_3_, ...), custom_call_target="tpu_custom_call" | custom-call | flops 10000000000 | bytes 8000000 | tf_op jit(solution)/shard_map/attention_backward/pallas_call | solution.py:196
  73.1 7.7 %all-to-all-done.1 = bf16[32,40,576]{2,1,0:T(8,128)(2,1)S(1)} async-done(((bf16[32,40,576]{2,1,0:T(8,128)(2,1)}), bf16[32,40,576]{2,1,0:T(8,128)(2,1)S(1)}, u32[]{:S(2)}, u32[]{:S(2)}) %all-to-all-start.1) | async-done | bytes 1474592 | tf_op jit(solution)/shard_map/all_to_all | solution.py:255
  80.8 17.2 %attention_backward.3 = (bf16[1024,576]{1,0:T(8,128)(2,1)S(1)}, bf16[1280,576]{1,0:T(8,128)(2,1)}) custom-call(s32[3]{0:T(128)S(1)} %bitcast.48, s32[1]{0:T(128)} %bitcast.refs_1_.refs_0_, bf16[256,1280]{1,0:T(8,128)(2,1)} %fusion.6.refs_2_, bf16[256,1280]{1,0:T(8,128)(2,1)} %collective-permute-done.refs_3_, ...), custom_call_target="tpu_custom_call" | custom-call | flops 15000000512 | bytes 8000000 | tf_op jit(solution)/shard_map/attention_backward/pallas_call | solution.py:196
  97.9 2.3 %norm_grad.3 = (f32[256,1280]{1,0:T(8,128)S(1)}, bf16[256,1280]{1,0:T(8,128)(2,1)}) custom-call(s32[1]{0:T(128)} %bitcast.refs_1_.refs_0_, bf16[1024,384]{1,0:T(8,128)(2,1)S(1)} %copy-done.10, bf16[1024,576]{1,0:T(8,128)(2,1)S(1)} %get-tuple-element.15.refs_2_, bf16[1280,384]{1,0:T(8,128)(2,1)S(1)} %bitcast.44, bf16[1280,576]{1,0:T(8,128)(2,1)S(1)} %bitcast.41), custom_call_target="tpu_custom_call" | custom-call | flops 1300000000 | bytes 6000000 | tf_op jit(solution)/shard_map/norm_grad/pallas_call | solution.py:226
  101.3 8.3 %all-to-all-start.2 = ((bf16[32,40,384]{2,1,0:T(8,128)(2,1)}), bf16[32,40,384]{2,1,0:T(8,128)(2,1)}, u32[]{:S(2)}, u32[]{:S(2)}) async-start(bf16[32,40,384]{2,1,0:T(8,128)(2,1)} %bitcast.46), calls=%async_computation.2 | async-start | bytes 1966080 | tf_op jit(solution)/shard_map/all_to_all | solution.py:261
  110.8 1.3 copy-done.8
  113.3 2.3 %norm_grad.2 = (f32[256,1280]{1,0:T(8,128)S(1)}, bf16[256,1280]{1,0:T(8,128)(2,1)}) custom-call(s32[1]{0:T(128)} %bitcast.refs_1_.refs_0_, bf16[1024,384]{1,0:T(8,128)(2,1)S(1)} %copy-done.11, bf16[1024,576]{1,0:T(8,128)(2,1)S(1)} %copy-done.8, bf16[1280,384]{1,0:T(8,128)(2,1)S(1)} %bitcast.45, bf16[1280,576]{1,0:T(8,128)(2,1)S(1)} %bitcast.42), custom_call_target="tpu_custom_call" | custom-call | flops 1300000000 | bytes 6000000 | tf_op jit(solution)/shard_map/norm_grad/pallas_call | solution.py:226
  115.8 2.2 %add_convert_fusion = bf16[256,1280]{1,0:T(8,128)(2,1)} fusion(f32[256,1280]{1,0:T(8,128)S(1)} %get-tuple-element.18, bf16[256,1280]{1,0:T(8,128)(2,1)} %collective-permute-done.7), kind=kLoop, calls=%fused_computation.18 | loop fusion | flops 983040 | bytes 2621440 | tf_op jit(solution)/shard_map/convert_element_type | solution.py:315
  118.0 2.6 %collective-permute-start.8 = (bf16[256,1280]{1,0:T(8,128)(2,1)}, bf16[256,1280]{1,0:T(8,128)(2,1)}, u32[]{:S(2)}, u32[]{:S(2)}) collective-permute-start(bf16[256,1280]{1,0:T(8,128)(2,1)} %add_convert_fusion), channel_id=1, source_target_pairs={{0,2},{1,3},{2,0},{3,1},{4,6},{5,7},{6,4},{7,5},{8,10},{9,11},{10,... | collective-permute-start | bytes 1966088 | tf_op jit(solution)/shard_map/ppermute | solution.py:276
  120.7 5.2 %all-to-all-done.2 = bf16[32,40,384]{2,1,0:T(8,128)(2,1)} async-done(((bf16[32,40,384]{2,1,0:T(8,128)(2,1)}), bf16[32,40,384]{2,1,0:T(8,128)(2,1)}, u32[]{:S(2)}, u32[]{:S(2)}) %all-to-all-start.2) | async-done | bytes 983072 | tf_op jit(solution)/shard_map/all_to_all | solution.py:261
  125.8 4.4 %all-to-all-start.3 = ((bf16[32,40,576]{2,1,0:T(8,128)(2,1)}), bf16[32,40,576]{2,1,0:T(8,128)(2,1)S(1)}, u32[]{:S(2)}, u32[]{:S(2)}) async-start(bf16[32,40,576]{2,1,0:T(8,128)(2,1)} %bitcast.20), calls=%async_computation.3 | async-start | bytes 3276800 | tf_op jit(solution)/shard_map/all_to_all | solution.py:261
  130.3 1.4 convert_reduce_fusion.1
  131.8 16.5 %collective-permute-done.8 = bf16[256,1280]{1,0:T(8,128)(2,1)} collective-permute-done((bf16[256,1280]{1,0:T(8,128)(2,1)}, bf16[256,1280]{1,0:T(8,128)(2,1)}, u32[]{:S(2)}, u32[]{:S(2)}) %collective-permute-start.8) | collective-permute-done | bytes 655392 | tf_op jit(solution)/shard_map/ppermute | solution.py:276
  148.3 1.8 %fusion.16 = (f32[256]{0:T(256)S(1)}, f32[256]{0:T(256)S(1)}, f32[256,1280]{1,0:T(8,128)S(1)}) fusion(f32[256]{0:T(256)S(1)} %add_rsqrt_fusion, f32[256]{0:T(256)S(1)} %broadcast_multiply_fusion.2, bf16[256,1280]{1,0:T(8,128)(2,1)S(1)} %copy-done.13, f32[1280]{0:T(1024)S(1)} %copy-done.16, bf16[256,1280]{1,0:T(8,128)(2,1)} %collective-permute-done.8, ...), kind=kLoop, calls=%fused_computation.59 | loop fusion | flops 3603968 | bytes 4596736 | tf_op jit(solution)/shard_map/reduce_sum | solution.py:30
  150.2 1.3 fusion.10
  151.4 6.0 %all-to-all-done.3 = bf16[32,40,576]{2,1,0:T(8,128)(2,1)S(1)} async-done(((bf16[32,40,576]{2,1,0:T(8,128)(2,1)}), bf16[32,40,576]{2,1,0:T(8,128)(2,1)S(1)}, u32[]{:S(2)}, u32[]{:S(2)}) %all-to-all-start.3) | async-done | bytes 1474592 | tf_op jit(solution)/shard_map/all_to_all | solution.py:261
  (81 shorter events, 15.1 us)
Async XLA Ops:
  0.6 5.7 %copy-start.12 = (bf16[256,1280]{1,0:T(8,128)(2,1)S(1)}, bf16[256,1280]{1,0:T(8,128)(2,1)}, u32[]{:S(2)}) copy-start(bf16[256,1280]{1,0:T(8,128)(2,1)} %param.7) | copy-start | bytes 1966084
  0.6 6.2 %copy-start.16 = (f32[1280]{0:T(1024)S(1)}, f32[1280]{0:T(1024)}, u32[]{:S(2)}) copy-start(f32[1280]{0:T(1024)} %param.11) | copy-start | bytes 15364
  0.7 6.2 %copy-start.17 = (f32[1280]{0:T(1024)S(1)}, f32[1280]{0:T(1024)}, u32[]{:S(2)}) copy-start(f32[1280]{0:T(1024)} %param.12) | copy-start | bytes 15364
  2.6 6.6 %copy-start.15 = (bf16[40,3,320]{2,0,1:T(8,128)(2,1)S(1)}, bf16[40,3,320]{2,0,1:T(8,128)(2,1)}, u32[]{:S(2)}) copy-start(bf16[40,3,320]{2,0,1:T(8,128)(2,1)} %param.13) | copy-start | bytes 230404
  2.6 18.2 %collective-permute-start.4 = (bf16[384,640]{1,0:T(8,128)(2,1)}, bf16[384,640]{1,0:T(8,128)(2,1)S(1)}, u32[]{:S(2)}, u32[]{:S(2)}) collective-permute-start(bf16[384,640]{1,0:T(8,128)(2,1)} %constant_dynamic-slice_fusion.2), channel_id=1, source_target_pairs={{0,2},{1,3},{2,0},{3,1},{4,6},{5,7},{6,4},{7,5},{8,10},{9,11},{10,... | collective-permute-start | bytes 1474568 | tf_op jit(solution)/shard_map/ppermute | solution.py:276
  8.0 31.3 %collective-permute-start.1 = (bf16[256,1280]{1,0:T(8,128)(2,1)}, bf16[256,1280]{1,0:T(8,128)(2,1)}, u32[]{:S(2)}, u32[]{:S(2)}) collective-permute-start(bf16[256,1280]{1,0:T(8,128)(2,1)} %fusion.6.refs_2_), channel_id=1, source_target_pairs={{0,2},{1,3},{2,0},{3,1},{4,6},{5,7},{6,4},{7,5},{8,10},{9,11},{10,... | collective-permute-start | bytes 1966088 | tf_op jit(solution)/shard_map/ppermute | solution.py:276
  8.0 50.0 %collective-permute-start = (bf16[256,1280]{1,0:T(8,128)(2,1)}, bf16[256,1280]{1,0:T(8,128)(2,1)}, u32[]{:S(2)}, u32[]{:S(2)}) collective-permute-start(bf16[256,1280]{1,0:T(8,128)(2,1)} %fusion.6.refs_2_), channel_id=1, source_target_pairs={{0,1},{1,0},{2,3},{3,2},{4,5},{5,4},{6,7},{7,6},{8,9},{9,8},{10,11... | collective-permute-start | bytes 1966088 | tf_op jit(solution)/shard_map/ppermute | solution.py:280
  9.4 10.2 %copy-start.14 = (bf16[384,1280]{1,0:T(8,128)(2,1)S(1)}, bf16[384,1280]{1,0:T(8,128)(2,1)}, u32[]{:S(2)}) copy-start(bf16[384,1280]{1,0:T(8,128)(2,1)} %param.10) | copy-start | bytes 2949124
  10.5 36.4 %all-to-all-start = ((bf16[32,40,384]{2,1,0:T(8,128)(2,1)}), bf16[32,40,384]{2,1,0:T(8,128)(2,1)S(1)}, u32[]{:S(2)}, u32[]{:S(2)}) async-start(bf16[32,40,384]{2,1,0:T(8,128)(2,1)} %broadcast_in_dim.15), calls=%async_computation | async-start | bytes 1966080 | tf_op jit(solution)/shard_map/all_to_all | solution.py:255
  20.5 21.3 %collective-permute-start.3 = (bf16[384,320]{1,0:T(8,128)(2,1)}, bf16[384,320]{1,0:T(8,128)(2,1)}, u32[]{:S(2)}, u32[]{:S(2)}) collective-permute-start(bf16[384,320]{1,0:T(8,128)(2,1)} %get-tuple-element.28), channel_id=1, source_target_pairs={{0,1},{1,0},{2,3},{3,2},{4,5},{5,4},{6,7},{7,6},{8,9},{9,8},{10,11... | collective-permute-start | bytes 737288 | tf_op jit(solution)/shard_map/ppermute | solution.py:280
  21.1 20.7 %collective-permute-start.5 = (bf16[384,320]{1,0:T(8,128)(2,1)S(1)}, bf16[384,320]{1,0:T(8,128)(2,1)S(1)}, u32[]{:S(2)}, u32[]{:S(2)}) collective-permute-start(bf16[384,320]{1,0:T(8,128)(2,1)S(1)} %get-tuple-element.30), channel_id=1, source_target_pairs={{0,1},{1,0},{2,3},{3,2},{4,5},{5,4},{6,7},{7,6},{8,9},{9,8},{10,11... | collective-permute-start | bytes 737288 | tf_op jit(solution)/shard_map/ppermute | solution.py:280
  39.3 18.8 %collective-permute-start.2 = (bf16[256,1280]{1,0:T(8,128)(2,1)}, bf16[256,1280]{1,0:T(8,128)(2,1)}, u32[]{:S(2)}, u32[]{:S(2)}) collective-permute-start(bf16[256,1280]{1,0:T(8,128)(2,1)} %collective-permute-done.1.refs_4_), channel_id=1, source_target_pairs={{0,1},{1,0},{2,3},{3,2},{4,5},{5,4},{6,7},{7,6},{8,9},{9,8},{10,11... | collective-permute-start | bytes 1966088 | tf_op jit(solution)/shard_map/ppermute | solution.py:280
  46.9 11.2 %copy-start.2 = (bf16[32,40,384]{2,1,0:T(8,128)(2,1)}, bf16[32,40,384]{2,1,0:T(8,128)(2,1)S(1)}, u32[]{:S(2)}) copy-start(bf16[32,40,384]{2,1,0:T(8,128)(2,1)S(1)} %all-to-all-done) | copy-start | bytes 2949124
  48.3 32.5 %all-to-all-start.1 = ((bf16[32,40,576]{2,1,0:T(8,128)(2,1)}), bf16[32,40,576]{2,1,0:T(8,128)(2,1)S(1)}, u32[]{:S(2)}, u32[]{:S(2)}) async-start(bf16[32,40,576]{2,1,0:T(8,128)(2,1)} %broadcast_in_dim.39), calls=%async_computation.1 | async-start | bytes 3276800 | tf_op jit(solution)/shard_map/all_to_all | solution.py:255
  80.8 17.2 %copy-start.3 = (bf16[32,40,384]{2,1,0:T(8,128)(2,1)S(1)}, bf16[32,40,384]{2,1,0:T(8,128)(2,1)}, u32[]{:S(2)}) copy-start(bf16[32,40,384]{2,1,0:T(8,128)(2,1)} %copy-done.2) | copy-start | bytes 2949124
  80.8 17.2 %copy-start.10 = (bf16[1024,384]{1,0:T(8,128)(2,1)S(1)}, bf16[1024,384]{1,0:T(8,128)(2,1)}, u32[]{:S(2)}) copy-start(bf16[1024,384]{1,0:T(8,128)(2,1)} %copy-done.9) | copy-start | bytes 2359300
  100.2 15.6 %collective-permute-start.7 = (bf16[256,1280]{1,0:T(8,128)(2,1)}, bf16[256,1280]{1,0:T(8,128)(2,1)}, u32[]{:S(2)}, u32[]{:S(2)}) collective-permute-start(bf16[256,1280]{1,0:T(8,128)(2,1)} %get-tuple-element.19), channel_id=1, source_target_pairs={{0,1},{1,0},{2,3},{3,2},{4,5},{5,4},{6,7},{7,6},{8,9},{9,8},{10,11... | collective-permute-start | bytes 1966088 | tf_op jit(solution)/shard_map/ppermute | solution.py:280
  101.3 24.5 %all-to-all-start.2 = ((bf16[32,40,384]{2,1,0:T(8,128)(2,1)}), bf16[32,40,384]{2,1,0:T(8,128)(2,1)}, u32[]{:S(2)}, u32[]{:S(2)}) async-start(bf16[32,40,384]{2,1,0:T(8,128)(2,1)} %bitcast.46), calls=%async_computation.2 | async-start | bytes 1966080 | tf_op jit(solution)/shard_map/all_to_all | solution.py:261
  115.5 2.5 %copy-start = (f32[256,1280]{1,0:T(8,128)}, f32[256,1280]{1,0:T(8,128)S(1)}, u32[]{:S(2)}) copy-start(f32[256,1280]{1,0:T(8,128)S(1)} %get-tuple-element.16) | copy-start | bytes 3932164
  115.5 16.3 %collective-permute-start.6 = (bf16[256,1280]{1,0:T(8,128)(2,1)}, bf16[256,1280]{1,0:T(8,128)(2,1)}, u32[]{:S(2)}, u32[]{:S(2)}) collective-permute-start(bf16[256,1280]{1,0:T(8,128)(2,1)} %get-tuple-element.17), channel_id=1, source_target_pairs={{0,1},{1,0},{2,3},{3,2},{4,5},{5,4},{6,7},{7,6},{8,9},{9,8},{10,11... | collective-permute-start | bytes 1966088 | tf_op jit(solution)/shard_map/ppermute | solution.py:280
  118.0 30.3 %collective-permute-start.8 = (bf16[256,1280]{1,0:T(8,128)(2,1)}, bf16[256,1280]{1,0:T(8,128)(2,1)}, u32[]{:S(2)}, u32[]{:S(2)}) collective-permute-start(bf16[256,1280]{1,0:T(8,128)(2,1)} %add_convert_fusion), channel_id=1, source_target_pairs={{0,2},{1,3},{2,0},{3,1},{4,6},{5,7},{6,4},{7,5},{8,10},{9,11},{10,... | collective-permute-start | bytes 1966088 | tf_op jit(solution)/shard_map/ppermute | solution.py:276
  125.8 22.5 %copy-start.1 = (f32[256,1280]{1,0:T(8,128)S(1)}, f32[256,1280]{1,0:T(8,128)}, u32[]{:S(2)}) copy-start(f32[256,1280]{1,0:T(8,128)} %copy-done) | copy-start | bytes 3932164
  125.8 31.6 %all-to-all-start.3 = ((bf16[32,40,576]{2,1,0:T(8,128)(2,1)}), bf16[32,40,576]{2,1,0:T(8,128)(2,1)S(1)}, u32[]{:S(2)}, u32[]{:S(2)}) async-start(bf16[32,40,576]{2,1,0:T(8,128)(2,1)} %bitcast.20), calls=%async_computation.3 | async-start | bytes 3276800 | tf_op jit(solution)/shard_map/all_to_all | solution.py:261
  130.3 18.1 %copy-start.13 = (bf16[256,1280]{1,0:T(8,128)(2,1)S(1)}, bf16[256,1280]{1,0:T(8,128)(2,1)}, u32[]{:S(2)}) copy-start(bf16[256,1280]{1,0:T(8,128)(2,1)} %param.7) | copy-start | bytes 1966084
  (8 other events, 10.4 us)

commit v5 on v4

--- a/solution.py
+++ b/solution.py
@@ -250,17 +250,39 @@
     return jnp.stack(parts, axis=1)
 
 
-def gather_weight(shard):
+def plane_groups(groups):
+    return [list(range(first, groups, 2)) for first in range(2)]
+
+
+def swap_pair(block):
     groups = lax.axis_size("dp")
-    spread = lax.all_to_all(jnp.broadcast_to(shard[None], (groups,) + shard.shape), "dp", 0, 0, tiled=True)
-    return spread.reshape(groups * shard.shape[0], shard.shape[1])
+    return lax.ppermute(block, "dp", [(i, i ^ 1) for i in range(groups)])
+
+
+def gather_plane(block):
+    groups = lax.axis_size("dp")
+    spread = lax.all_to_all(
+        jnp.broadcast_to(block[None], (groups // 2,) + block.shape), "dp", 0, 0,
+        axis_index_groups=plane_groups(groups), tiled=True,
+    )
+    return spread.reshape(groups // 2 * block.shape[0], block.shape[1])
 
 
 def exchange_terms(term):
     groups = lax.axis_size("dp")
     return lax.all_to_all(
-        term.reshape(groups, term.shape[0] // groups, term.shape[1]), "dp", 0, 0, tiled=True
-    )
+        term.reshape(groups // 2, term.shape[0] * 2 // groups, term.shape[1]), "dp", 0, 0,
+        axis_index_groups=plane_groups(groups), tiled=True,
+    )
+
+
+def sum_terms(terms):
+    second = lax.axis_index("dp") % 2
+    total = jnp.sum(terms.astype(F32), axis=0)
+    halves = total.reshape(2, total.shape[0] // 2, total.shape[1])
+    keep = lax.dynamic_index_in_dim(halves, second, 0, keepdims=False)
+    give = lax.dynamic_index_in_dim(halves, 1 - second, 0, keepdims=False)
+    return keep + swap_pair(give.astype(BF16)).astype(F32)
 
 
 def grad_tiles(out_grad):
@@ -287,8 +309,12 @@
     think_rows = thinker_grad.shape[0]
     place = lax.axis_index("frame")
     side, core = place // 2, place % 2
-    shards = [pack_columns(qkv_weight, heads) for heads in CHUNKS]
-    weights = [gather_weight(shards[0])]
+    shard = jnp.concatenate([pack_columns(qkv_weight, heads) for heads in CHUNKS], axis=1)
+    other = swap_pair(shard)
+    both = jnp.where(lax.axis_index("dp") % 2 == 0, jnp.concatenate([shard, other]), jnp.concatenate([other, shard]))
+    cut = HD * len(chunk_blocks(CHUNKS[0]))
+    shards = [both[:, :cut], both[:, cut:]]
+    weights = [gather_plane(shards[0])]
     own, standard, inv_std = norm_forward(hidden_in, norm_gain, norm_bias)
     far = swap_side(own)
     near = swap_core(own)
@@ -299,7 +325,7 @@
     far_near = swap_core(far)
     far_near_think = swap_core(cols(far_think, 1 - core))
     shard, weights[0] = lax.optimization_barrier((shards[1], weights[0]))
-    weights.append(gather_weight(shard))
+    weights.append(gather_plane(shard))
     moved = jnp.concatenate([cols(sides[0], core), near_think, cols(far_think, core), far_near_think], axis=0)
     rows_at = ((token_positions // think_rows) ^ place) * think_rows + token_positions % think_rows
     out_grad = grad_tiles(jnp.take(moved, rows_at, axis=0))
@@ -316,7 +342,7 @@
     keep, give = norm_grad_blocks(0, 1, at, grads, weights)
     core_sum = swap_core(give)
     norm_grad = keep + core_sum.astype(F32) + side_sum.astype(F32)
-    weight_grad = unpack_columns([jnp.sum(term.astype(F32), axis=0) for term in terms])
+    weight_grad = unpack_columns([sum_terms(term) for term in terms])
     hidden_grad = norm_backward(norm_grad, standard, inv_std, norm_gain)
     return (hidden_grad, weight_grad)
 

time: 160 us -> 147 us (0.919)
  the two profiles are of different devices: /device:TPU:1 before, /device:TPU:24 now
where the time goes in v5:
time: 147 us
  waiting for transfers between devices  44.5 us (30%)
  Pallas kernels  42 us (29%)
  starting transfers between devices  30.3 us (21%)
  local copies, waits for them, and re-layouts  17.5 us (12%)
  other arithmetic  11.3 us (8%)
    pallas_call x2, Pallas kernels, attention(): pl.pallas_call(body, out_shape=(jax.ShapeDtypeStruct((rows, columns), BF1...  37.4 us
    ppermute x3, waiting for transfers between devices, swap_pair(): return lax.ppermute(block, 'dp', [(i, i ^ 1) for i in range(groups)])  23.5 us
    all_to_all x2, starting transfers between devices, gather_plane(): lax.all_to_all(jnp.broadcast_to(block[None], (groups // 2,) + block.shape...  12 us
    all_to_all x2, waiting for transfers between devices, gather_plane(): lax.all_to_all(jnp.broadcast_to(block[None], (groups // 2,) + block.shape...  11 us
    all_to_all x2, starting transfers between devices, exchange_terms(): lax.all_to_all(term.reshape(groups // 2, term.shape[0] * 2 // groups, ter...  10.9 us
    ppermute x3, waiting for transfers between devices, swap_side(): return lax.ppermute(block, 'frame', FRAME_SIDE)  7.25 us
    unnamed x38, local copies, waits for them, and re-layouts  7 us
    ppermute x3, starting transfers between devices, swap_side(): return lax.ppermute(block, 'frame', FRAME_SIDE)  5.12 us
  transfers between devices with their start and end apart: 16, of which 8 were waited for; matrix products, arithmetic and copies ran while one was open for 12% of the time, Pallas kernels for 29%

profile of v5, /device:TPU:24, one launch (start us, length us, event | category | flops | bytes accessed | tf_op | source)
XLA Modules:
  0.0 146.7 jit_solution(13643978385986254490)
XLA Ops:
  0.7 1.9 %constant_dynamic-slice_fusion.2 = bf16[384,640]{1,0:T(8,128)(2,1)} fusion(bf16[384,1280]{1,0:T(8,128)(2,1)} %param.10, s32[]{:T(128)S(6)} %select_n.90), kind=kLoop, calls=%fused_computation.58 | loop fusion | bytes 983044 | tf_op jit(solution)/shard_map/dynamic_slice | solution.py:321
  6.7 3.6 %collective-permute-start.1 = (bf16[256,1280]{1,0:T(8,128)(2,1)}, bf16[256,1280]{1,0:T(8,128)(2,1)}, u32[]{:S(2)}, u32[]{:S(2)}) collective-permute-start(bf16[256,1280]{1,0:T(8,128)(2,1)} %fusion.6.refs_2_), channel_id=1, source_target_pairs={{0,2},{1,3},{2,0},{3,1},{4,6},{5,7},{6,4},{7,5},{8,10},{9,11},{10,... | collective-permute-start | bytes 1966088 | tf_op jit(solution)/shard_map/ppermute | solution.py:298
  10.3 7.3 %collective-permute-done.3 = bf16[40,960]{1,0:T(8,128)(2,1)S(1)} collective-permute-done((bf16[40,960]{1,0:T(8,128)(2,1)S(1)}, bf16[40,960]{1,0:T(8,128)(2,1)S(1)}, u32[]{:S(2)}, u32[]{:S(2)}) %collective-permute-start.3) | collective-permute-done | bytes 76832 | tf_op jit(solution)/shard_map/ppermute | solution.py:259
  18.7 8.0 %all-to-all-start = ((bf16[16,80,384]{2,1,0:T(8,128)(2,1)}), bf16[16,80,384]{2,1,0:T(8,128)(2,1)S(1)}, u32[]{:S(2)}, u32[]{:S(2)}) async-start(bf16[16,80,384]{2,1,0:T(8,128)(2,1)} %broadcast_in_dim.15), calls=%async_computation | async-start | bytes 1966080 | tf_op jit(solution)/shard_map/all_to_all | solution.py:264
  28.1 5.1 %collective-permute-done.1.refs_4_ = bf16[256,1280]{1,0:T(8,128)(2,1)} collective-permute-done((bf16[256,1280]{1,0:T(8,128)(2,1)}, bf16[256,1280]{1,0:T(8,128)(2,1)}, u32[]{:S(2)}, u32[]{:S(2)}) %collective-permute-start.1) | collective-permute-done | bytes 655392 | tf_op jit(solution)/shard_map/ppermute | solution.py:298
  33.3 3.9 %gather_fusion = bf16[1024,320]{1,0:T(8,128)(2,1)S(1)} fusion(bf16[1536,320]{1,0:T(8,128)(2,1)S(1)} %pad_maximum_fusion, s32[1024]{0:T(1024)S(1)} %broadcast_clamp_fusion), kind=kCustom, calls=%fused_computation | custom fusion | bytes 1314816 | tf_op jit(solution)/shard_map/jit(_take)/gather | solution.py:331
  37.3 3.9 %all-to-all-done = bf16[16,80,384]{2,1,0:T(8,128)(2,1)S(1)} async-done(((bf16[16,80,384]{2,1,0:T(8,128)(2,1)}), bf16[16,80,384]{2,1,0:T(8,128)(2,1)S(1)}, u32[]{:S(2)}, u32[]{:S(2)}) %all-to-all-start) | async-done | bytes 983072 | tf_op jit(solution)/shard_map/all_to_all | solution.py:264
  41.2 1.4 broadcast_in_dim.39
  42.6 4.0 %all-to-all-start.1 = ((bf16[16,80,576]{2,1,0:T(8,128)(2,1)}), bf16[16,80,576]{2,1,0:T(8,128)(2,1)S(1)}, u32[]{:S(2)}, u32[]{:S(2)}) async-start(bf16[16,80,576]{2,1,0:T(8,128)(2,1)} %broadcast_in_dim.39), calls=%async_computation.1 | async-start | bytes 3276800 | tf_op jit(solution)/shard_map/all_to_all | solution.py:264
  47.5 16.1 %attention_backward.2 = (bf16[1024,384]{1,0:T(8,128)(2,1)S(1)}, bf16[1280,384]{1,0:T(8,128)(2,1)S(1)}) custom-call(s32[3]{0:T(128)S(1)} %bitcast.57, s32[1]{0:T(128)} %bitcast.refs_1_.refs_0_, bf16[256,1280]{1,0:T(8,128)(2,1)} %fusion.6.refs_2_, bf16[256,1280]{1,0:T(8,128)(2,1)} %collective-permute-done.refs_3_, ...), custom_call_target="tpu_custom_call" | custom-call | flops 10000000000 | bytes 8000000 | tf_op jit(solution)/shard_map/attention_backward/pallas_call | solution.py:196
  65.5 7.2 %all-to-all-done.1 = bf16[16,80,576]{2,1,0:T(8,128)(2,1)S(1)} async-done(((bf16[16,80,576]{2,1,0:T(8,128)(2,1)}), bf16[16,80,576]{2,1,0:T(8,128)(2,1)S(1)}, u32[]{:S(2)}, u32[]{:S(2)}) %all-to-all-start.1) | async-done | bytes 1474592 | tf_op jit(solution)/shard_map/all_to_all | solution.py:264
  72.7 4.5 %all-to-all-start.2 = ((bf16[16,80,384]{2,1,0:T(8,128)(2,1)}), bf16[16,80,384]{2,1,0:T(8,128)(2,1)}, u32[]{:S(2)}, u32[]{:S(2)}) async-start(bf16[16,80,384]{2,1,0:T(8,128)(2,1)} %bitcast.56), calls=%async_computation.2 | async-start | bytes 1966080 | tf_op jit(solution)/shard_map/all_to_all | solution.py:273
  77.2 21.3 %attention_backward.3 = (bf16[1024,576]{1,0:T(8,128)(2,1)S(1)}, bf16[1280,576]{1,0:T(8,128)(2,1)}) custom-call(s32[3]{0:T(128)S(1)} %bitcast.58, s32[1]{0:T(128)} %bitcast.refs_1_.refs_0_, bf16[256,1280]{1,0:T(8,128)(2,1)} %fusion.6.refs_2_, bf16[256,1280]{1,0:T(8,128)(2,1)} %collective-permute-done.refs_3_, ...), custom_call_target="tpu_custom_call" | custom-call | flops 15000000512 | bytes 8000000 | tf_op jit(solution)/shard_map/attention_backward/pallas_call | solution.py:196
  98.5 2.3 %norm_grad.3 = (f32[256,1280]{1,0:T(8,128)S(1)}, bf16[256,1280]{1,0:T(8,128)(2,1)}) custom-call(s32[1]{0:T(128)} %bitcast.refs_1_.refs_0_, bf16[1024,384]{1,0:T(8,128)(2,1)S(1)} %copy-done.10, bf16[1024,576]{1,0:T(8,128)(2,1)S(1)} %get-tuple-element.15.refs_2_, bf16[1280,384]{1,0:T(8,128)(2,1)S(1)} %bitcast.54, bf16[1280,576]{1,0:T(8,128)(2,1)S(1)} %bitcast.51), custom_call_target="tpu_custom_call" | custom-call | flops 1300000000 | bytes 6000000 | tf_op jit(solution)/shard_map/norm_grad/pallas_call | solution.py:226
  104.4 2.3 %norm_grad.2 = (f32[256,1280]{1,0:T(8,128)S(1)}, bf16[256,1280]{1,0:T(8,128)(2,1)}) custom-call(s32[1]{0:T(128)} %bitcast.refs_1_.refs_0_, bf16[1024,384]{1,0:T(8,128)(2,1)S(1)} %copy-done.11, bf16[1024,576]{1,0:T(8,128)(2,1)S(1)} %copy-done.8, bf16[1280,384]{1,0:T(8,128)(2,1)S(1)} %bitcast.55, bf16[1280,576]{1,0:T(8,128)(2,1)S(1)} %bitcast.52), custom_call_target="tpu_custom_call" | custom-call | flops 1300000000 | bytes 6000000 | tf_op jit(solution)/shard_map/norm_grad/pallas_call | solution.py:226
  108.3 6.4 %all-to-all-start.3 = ((bf16[16,80,576]{2,1,0:T(8,128)(2,1)}), bf16[16,80,576]{2,1,0:T(8,128)(2,1)}, u32[]{:S(2)}, u32[]{:S(2)}) async-start(bf16[16,80,576]{2,1,0:T(8,128)(2,1)} %bitcast.23), calls=%async_computation.3 | async-start | bytes 3276800 | tf_op jit(solution)/shard_map/all_to_all | solution.py:273
  114.7 2.0 %add_convert_fusion = bf16[256,1280]{1,0:T(8,128)(2,1)} fusion(f32[256,1280]{1,0:T(8,128)S(1)} %get-tuple-element.18, bf16[256,1280]{1,0:T(8,128)(2,1)} %collective-permute-done.8), kind=kLoop, calls=%fused_computation.18 | loop fusion | flops 983040 | bytes 2621440 | tf_op jit(solution)/shard_map/convert_element_type | solution.py:341
  117.0 1.5 convert_reduce_fusion.1
  119.1 13.8 %collective-permute-done.10 = bf16[40,384]{1,0:T(8,128)(2,1)S(1)} collective-permute-done((bf16[40,384]{1,0:T(8,128)(2,1)S(1)}, bf16[40,384]{1,0:T(8,128)(2,1)S(1)}, u32[]{:S(2)}, u32[]{:S(2)}) %collective-permute-start.10) | collective-permute-done | bytes 30752 | tf_op jit(solution)/shard_map/ppermute | solution.py:259
  133.0 2.1 %collective-permute-done.9 = bf16[256,1280]{1,0:T(8,128)(2,1)S(1)} collective-permute-done((bf16[256,1280]{1,0:T(8,128)(2,1)}, bf16[256,1280]{1,0:T(8,128)(2,1)S(1)}, u32[]{:S(2)}, u32[]{:S(2)}) %collective-permute-start.9) | collective-permute-done | bytes 655392 | tf_op jit(solution)/shard_map/ppermute | solution.py:298
  135.2 1.8 %fusion.18 = (f32[256]{0:T(256)S(1)}, f32[256]{0:T(256)S(1)}, f32[256,1280]{1,0:T(8,128)S(1)}) fusion(f32[256]{0:T(256)S(1)} %add_rsqrt_fusion, f32[256]{0:T(256)S(1)} %broadcast_multiply_fusion.2, bf16[256,1280]{1,0:T(8,128)(2,1)} %param.7, f32[1280]{0:T(1024)S(1)} %copy-done.16, bf16[256,1280]{1,0:T(8,128)(2,1)S(1)} %collective-permute-done.9, ...), kind=kLoop, calls=%fused_computation.66 | loop fusion | flops 3603968 | bytes 4596736 | tf_op jit(solution)/shard_map/reduce_sum | solution.py:30
  137.0 2.7 %all-to-all-done.3 = bf16[16,80,576]{2,1,0:T(8,128)(2,1)} async-done(((bf16[16,80,576]{2,1,0:T(8,128)(2,1)}), bf16[16,80,576]{2,1,0:T(8,128)(2,1)}, u32[]{:S(2)}, u32[]{:S(2)}) %all-to-all-start.3) | async-done | bytes 1474592 | tf_op jit(solution)/shard_map/all_to_all | solution.py:273
  139.7 1.7 %convert_reduce_fusion = f32[80,576]{1,0:T(8,128)S(1)} fusion(bf16[16,80,576]{2,1,0:T(8,128)(2,1)} %all-to-all-done.3), kind=kLoop, calls=%fused_computation.1 | loop fusion | flops 1428480 | bytes 1658880 | tf_op jit(solution)/shard_map/reduce_sum | solution.py:281
  143.2 2.5 %collective-permute-done.11 = bf16[40,576]{1,0:T(8,128)(2,1)S(1)} collective-permute-done((bf16[40,576]{1,0:T(8,128)(2,1)S(1)}, bf16[40,576]{1,0:T(8,128)(2,1)S(1)}, u32[]{:S(2)}, u32[]{:S(2)}) %collective-permute-start.11) | collective-permute-done | bytes 46112 | tf_op jit(solution)/shard_map/ppermute | solution.py:259
  (94 shorter events, 18.4 us)
Async XLA Ops:
  2.6 24.5 %collective-permute-start.5 = (bf16[384,640]{1,0:T(8,128)(2,1)}, bf16[384,640]{1,0:T(8,128)(2,1)S(1)}, u32[]{:S(2)}, u32[]{:S(2)}) collective-permute-start(bf16[384,640]{1,0:T(8,128)(2,1)} %constant_dynamic-slice_fusion.2), channel_id=1, source_target_pairs={{0,2},{1,3},{2,0},{3,1},{4,6},{5,7},{6,4},{7,5},{8,10},{9,11},{10,... | collective-permute-start | bytes 1474568 | tf_op jit(solution)/shard_map/ppermute | solution.py:298
  4.9 12.7 %collective-permute-start.3 = (bf16[40,960]{1,0:T(8,128)(2,1)S(1)}, bf16[40,960]{1,0:T(8,128)(2,1)S(1)}, u32[]{:S(2)}, u32[]{:S(2)}) collective-permute-start(bf16[40,960]{1,0:T(8,128)(2,1)S(1)} %concatenate.25), channel_id=1, source_target_pairs={{0,4},{4,0},{8,12},{12,8},{16,20},{20,16},{24,28},{28,24},{32,36},... | collective-permute-start | bytes 230408 | tf_op jit(solution)/shard_map/ppermute | solution.py:259
  6.7 26.5 %collective-permute-start.1 = (bf16[256,1280]{1,0:T(8,128)(2,1)}, bf16[256,1280]{1,0:T(8,128)(2,1)}, u32[]{:S(2)}, u32[]{:S(2)}) collective-permute-start(bf16[256,1280]{1,0:T(8,128)(2,1)} %fusion.6.refs_2_), channel_id=1, source_target_pairs={{0,2},{1,3},{2,0},{3,1},{4,6},{5,7},{6,4},{7,5},{8,10},{9,11},{10,... | collective-permute-start | bytes 1966088 | tf_op jit(solution)/shard_map/ppermute | solution.py:298
  10.3 36.8 %collective-permute-start = (bf16[256,1280]{1,0:T(8,128)(2,1)}, bf16[256,1280]{1,0:T(8,128)(2,1)}, u32[]{:S(2)}, u32[]{:S(2)}) collective-permute-start(bf16[256,1280]{1,0:T(8,128)(2,1)} %fusion.6.refs_2_), channel_id=1, source_target_pairs={{0,1},{1,0},{2,3},{3,2},{4,5},{5,4},{6,7},{7,6},{8,9},{9,8},{10,11... | collective-permute-start | bytes 1966088 | tf_op jit(solution)/shard_map/ppermute | solution.py:302
  17.6 10.4 %copy-start.15 = (bf16[80,960]{1,0:T(8,128)(2,1)}, bf16[80,960]{1,0:T(8,128)(2,1)S(1)}, u32[]{:S(2)}) copy-start(bf16[80,960]{1,0:T(8,128)(2,1)S(1)} %maximum_select_fusion) | copy-start | bytes 460804
  17.7 9.1 %copy-start.14 = (bf16[384,1280]{1,0:T(8,128)(2,1)S(1)}, bf16[384,1280]{1,0:T(8,128)(2,1)}, u32[]{:S(2)}) copy-start(bf16[384,1280]{1,0:T(8,128)(2,1)} %param.10) | copy-start | bytes 2949124
  18.7 22.4 %all-to-all-start = ((bf16[16,80,384]{2,1,0:T(8,128)(2,1)}), bf16[16,80,384]{2,1,0:T(8,128)(2,1)S(1)}, u32[]{:S(2)}, u32[]{:S(2)}) async-start(bf16[16,80,384]{2,1,0:T(8,128)(2,1)} %broadcast_in_dim.15), calls=%async_computation | async-start | bytes 1966080 | tf_op jit(solution)/shard_map/all_to_all | solution.py:264
  27.0 6.1 %collective-permute-start.4 = (bf16[384,320]{1,0:T(8,128)(2,1)S(1)}, bf16[384,320]{1,0:T(8,128)(2,1)S(1)}, u32[]{:S(2)}, u32[]{:S(2)}) collective-permute-start(bf16[384,320]{1,0:T(8,128)(2,1)S(1)} %get-tuple-element.28), channel_id=1, source_target_pairs={{0,1},{1,0},{2,3},{3,2},{4,5},{5,4},{6,7},{7,6},{8,9},{9,8},{10,11... | collective-permute-start | bytes 737288 | tf_op jit(solution)/shard_map/ppermute | solution.py:302
  27.4 5.7 %collective-permute-start.6 = (bf16[384,320]{1,0:T(8,128)(2,1)S(1)}, bf16[384,320]{1,0:T(8,128)(2,1)S(1)}, u32[]{:S(2)}, u32[]{:S(2)}) collective-permute-start(bf16[384,320]{1,0:T(8,128)(2,1)S(1)} %get-tuple-element.30), channel_id=1, source_target_pairs={{0,1},{1,0},{2,3},{3,2},{4,5},{5,4},{6,7},{7,6},{8,9},{9,8},{10,11... | collective-permute-start | bytes 737288 | tf_op jit(solution)/shard_map/ppermute | solution.py:302
  33.2 14.0 %collective-permute-start.2 = (bf16[256,1280]{1,0:T(8,128)(2,1)}, bf16[256,1280]{1,0:T(8,128)(2,1)}, u32[]{:S(2)}, u32[]{:S(2)}) collective-permute-start(bf16[256,1280]{1,0:T(8,128)(2,1)} %collective-permute-done.1.refs_4_), channel_id=1, source_target_pairs={{0,1},{1,0},{2,3},{3,2},{4,5},{5,4},{6,7},{7,6},{8,9},{9,8},{10,11... | collective-permute-start | bytes 1966088 | tf_op jit(solution)/shard_map/ppermute | solution.py:302
  33.3 7.8 %slice-start = ((bf16[80,960]{1,0:T(8,128)(2,1)}), bf16[80,576]{1,0:T(8,128)(2,1)S(1)}, s32[]{:S(2)}) async-start(bf16[80,960]{1,0:T(8,128)(2,1)} %copy-done.15), calls=%async_computation.4 | async-start | bytes 204800 | tf_op jit(solution)/shard_map/slice | solution.py:316
  41.2 6.0 %copy-start.2 = (bf16[16,80,384]{2,1,0:T(8,128)(2,1)}, bf16[16,80,384]{2,1,0:T(8,128)(2,1)S(1)}, u32[]{:S(2)}) copy-start(bf16[16,80,384]{2,1,0:T(8,128)(2,1)S(1)} %all-to-all-done) | copy-start | bytes 2949124
  42.6 30.1 %all-to-all-start.1 = ((bf16[16,80,576]{2,1,0:T(8,128)(2,1)}), bf16[16,80,576]{2,1,0:T(8,128)(2,1)S(1)}, u32[]{:S(2)}, u32[]{:S(2)}) async-start(bf16[16,80,576]{2,1,0:T(8,128)(2,1)} %broadcast_in_dim.39), calls=%async_computation.1 | async-start | bytes 3276800 | tf_op jit(solution)/shard_map/all_to_all | solution.py:264
  72.7 35.6 %all-to-all-start.2 = ((bf16[16,80,384]{2,1,0:T(8,128)(2,1)}), bf16[16,80,384]{2,1,0:T(8,128)(2,1)}, u32[]{:S(2)}, u32[]{:S(2)}) async-start(bf16[16,80,384]{2,1,0:T(8,128)(2,1)} %bitcast.56), calls=%async_computation.2 | async-start | bytes 1966080 | tf_op jit(solution)/shard_map/all_to_all | solution.py:273
  77.2 21.3 %copy-start.3 = (bf16[16,80,384]{2,1,0:T(8,128)(2,1)S(1)}, bf16[16,80,384]{2,1,0:T(8,128)(2,1)}, u32[]{:S(2)}) copy-start(bf16[16,80,384]{2,1,0:T(8,128)(2,1)} %copy-done.2) | copy-start | bytes 2949124
  77.2 21.3 %copy-start.10 = (bf16[1024,384]{1,0:T(8,128)(2,1)S(1)}, bf16[1024,384]{1,0:T(8,128)(2,1)}, u32[]{:S(2)}) copy-start(bf16[1024,384]{1,0:T(8,128)(2,1)} %copy-done.9) | copy-start | bytes 2359300
  100.8 13.9 %collective-permute-start.8 = (bf16[256,1280]{1,0:T(8,128)(2,1)}, bf16[256,1280]{1,0:T(8,128)(2,1)}, u32[]{:S(2)}, u32[]{:S(2)}) collective-permute-start(bf16[256,1280]{1,0:T(8,128)(2,1)} %get-tuple-element.19), channel_id=1, source_target_pairs={{0,1},{1,0},{2,3},{3,2},{4,5},{5,4},{6,7},{7,6},{8,9},{9,8},{10,11... | collective-permute-start | bytes 1966088 | tf_op jit(solution)/shard_map/ppermute | solution.py:302
  107.8 25.2 %collective-permute-start.7 = (bf16[256,1280]{1,0:T(8,128)(2,1)}, bf16[256,1280]{1,0:T(8,128)(2,1)}, u32[]{:S(2)}, u32[]{:S(2)}) collective-permute-start(bf16[256,1280]{1,0:T(8,128)(2,1)} %get-tuple-element.17), channel_id=1, source_target_pairs={{0,1},{1,0},{2,3},{3,2},{4,5},{5,4},{6,7},{7,6},{8,9},{9,8},{10,11... | collective-permute-start | bytes 1966088 | tf_op jit(solution)/shard_map/ppermute | solution.py:302
  108.3 31.4 %all-to-all-start.3 = ((bf16[16,80,576]{2,1,0:T(8,128)(2,1)}), bf16[16,80,576]{2,1,0:T(8,128)(2,1)}, u32[]{:S(2)}, u32[]{:S(2)}) async-start(bf16[16,80,576]{2,1,0:T(8,128)(2,1)} %bitcast.23), calls=%async_computation.3 | async-start | bytes 3276800 | tf_op jit(solution)/shard_map/all_to_all | solution.py:273
  116.7 18.4 %copy-start.1 = (f32[256,1280]{1,0:T(8,128)S(1)}, f32[256,1280]{1,0:T(8,128)}, u32[]{:S(2)}) copy-start(f32[256,1280]{1,0:T(8,128)} %copy-done) | copy-start | bytes 3932164
  116.7 18.4 %collective-permute-start.9 = (bf16[256,1280]{1,0:T(8,128)(2,1)}, bf16[256,1280]{1,0:T(8,128)(2,1)S(1)}, u32[]{:S(2)}, u32[]{:S(2)}) collective-permute-start(bf16[256,1280]{1,0:T(8,128)(2,1)} %add_convert_fusion), channel_id=1, source_target_pairs={{0,2},{1,3},{2,0},{3,1},{4,6},{5,7},{6,4},{7,5},{8,10},{9,11},{10,... | collective-permute-start | bytes 1966088 | tf_op jit(solution)/shard_map/ppermute | solution.py:298
  118.5 14.3 %collective-permute-start.10 = (bf16[40,384]{1,0:T(8,128)(2,1)S(1)}, bf16[40,384]{1,0:T(8,128)(2,1)S(1)}, u32[]{:S(2)}, u32[]{:S(2)}) collective-permute-start(bf16[40,384]{1,0:T(8,128)(2,1)S(1)} %fusion.13), channel_id=1, source_target_pairs={{0,4},{4,0},{8,12},{12,8},{16,20},{20,16},{24,28},{28,24},{32,36},... | collective-permute-start | bytes 92168 | tf_op jit(solution)/shard_map/ppermute | solution.py:259
  137.0 4.9 %copy-start.13 = (bf16[256,1280]{1,0:T(8,128)(2,1)S(1)}, bf16[256,1280]{1,0:T(8,128)(2,1)}, u32[]{:S(2)}) copy-start(bf16[256,1280]{1,0:T(8,128)(2,1)} %param.7) | copy-start | bytes 1966084
  141.4 4.2 %collective-permute-start.11 = (bf16[40,576]{1,0:T(8,128)(2,1)S(1)}, bf16[40,576]{1,0:T(8,128)(2,1)S(1)}, u32[]{:S(2)}, u32[]{:S(2)}) collective-permute-start(bf16[40,576]{1,0:T(8,128)(2,1)S(1)} %fusion.12), channel_id=1, source_target_pairs={{0,4},{4,0},{8,12},{12,8},{16,20},{20,16},{24,28},{28,24},{32,36},... | collective-permute-start | bytes 138248 | tf_op jit(solution)/shard_map/ppermute | solution.py:259
  (12 other events, 24.9 us)

commit v6 on v5

--- a/solution.py
+++ b/solution.py
@@ -204,7 +204,7 @@
         scratch_shapes=[pltpu.VMEM((rows, features), BF16)] + [tall] * 6 + [
             wide, wide, pltpu.VMEM((count, rows, 128), F32), pltpu.VMEM(((count + 1) // 2, QB, 128), F32)
         ],
-        compiler_params=pltpu.CompilerParams(vmem_limit_bytes=40 << 20),
+        compiler_params=pltpu.CompilerParams(vmem_limit_bytes=(12 + 5 * count) << 20),
         cost_estimate=pl.CostEstimate(
             flops=5_000_000_000 * count, bytes_accessed=8_000_000, transcendentals=1_000_000 * count
         ),
@@ -228,13 +228,13 @@
         out_shape=(jax.ShapeDtypeStruct(shape, F32), jax.ShapeDtypeStruct(shape, BF16)),
         in_specs=[SM] + [VM] * 4,
         out_specs=(VM, VM),
-        compiler_params=pltpu.CompilerParams(vmem_limit_bytes=24 << 20),
+        compiler_params=pltpu.CompilerParams(vmem_limit_bytes=10 << 20),
         cost_estimate=pl.CostEstimate(flops=1_300_000_000, bytes_accessed=6_000_000, transcendentals=0),
         name="norm_grad",
     )(place, *grads, *weights)
 
 
-CHUNKS = ((0, 1), (2, 3, 4))
+CHUNKS = ((2, 3, 4), (0, 1))
 
 
 def pack_columns(weight, heads):
@@ -282,7 +282,8 @@
     halves = total.reshape(2, total.shape[0] // 2, total.shape[1])
     keep = lax.dynamic_index_in_dim(halves, second, 0, keepdims=False)
     give = lax.dynamic_index_in_dim(halves, 1 - second, 0, keepdims=False)
-    return keep + swap_pair(give.astype(BF16)).astype(F32)
+    got = swap_pair(give.astype(BF16))
+    return keep + got.astype(F32)
 
 
 def grad_tiles(out_grad):

time: 147 us -> 149 us (1.014)
  the two profiles are of different devices: /device:TPU:24 before, /device:TPU:0 now
where the time goes in v6:
time: 149 us; the launch traced here: 148 us
  waiting for transfers between devices  46.6 us (31%)
  starting transfers between devices  37.8 us (25%)
  Pallas kernels  34.5 us (23%)
  local copies, waits for them, and re-layouts  17 us (11%)
  other arithmetic  11.1 us (7%)
    pallas_call x2, Pallas kernels, attention(): pl.pallas_call(body, out_shape=(jax.ShapeDtypeStruct((rows, columns), BF1...  29.7 us
    all_to_all x2, starting transfers between devices, exchange_terms(): lax.all_to_all(term.reshape(groups // 2, term.shape[0] * 2 // groups, ter...  15.9 us
    ppermute x3, waiting for transfers between devices, swap_side(): return lax.ppermute(block, 'frame', FRAME_SIDE)  14.2 us
    all_to_all x2, starting transfers between devices, gather_plane(): lax.all_to_all(jnp.broadcast_to(block[None], (groups // 2,) + block.shape...  12.2 us
    all_to_all x2, waiting for transfers between devices, gather_plane(): lax.all_to_all(jnp.broadcast_to(block[None], (groups // 2,) + block.shape...  12.1 us
    ppermute x3, waiting for transfers between devices, swap_pair(): return lax.ppermute(block, 'dp', [(i, i ^ 1) for i in range(groups)])  11.4 us
    all_to_all x2, waiting for transfers between devices, exchange_terms(): lax.all_to_all(term.reshape(groups // 2, term.shape[0] * 2 // groups, ter...  8.86 us
    ppermute x3, starting transfers between devices, swap_side(): return lax.ppermute(block, 'frame', FRAME_SIDE)  6.14 us
  transfers between devices with their start and end apart: 16, of which 8 were waited for; matrix products, arithmetic and copies ran while one was open for 12% of the time, Pallas kernels for 23%

profile of v6, /device:TPU:0, one launch (start us, length us, event | category | flops | bytes accessed | tf_op | source)
XLA Modules:
  0.0 148.0 jit_solution(17170033412950366413)
XLA Ops:
  0.7 1.9 %constant_dynamic-slice_fusion.2 = bf16[384,640]{1,0:T(8,128)(2,1)} fusion(bf16[384,1280]{1,0:T(8,128)(2,1)} %param.10, s32[]{:T(128)S(6)} %select_n.90), kind=kLoop, calls=%fused_computation.58 | loop fusion | bytes 983044 | tf_op jit(solution)/shard_map/dynamic_slice | solution.py:322
  2.6 3.3 %collective-permute-start.5 = (bf16[384,640]{1,0:T(8,128)(2,1)}, bf16[384,640]{1,0:T(8,128)(2,1)S(1)}, u32[]{:S(2)}, u32[]{:S(2)}) collective-permute-start(bf16[384,640]{1,0:T(8,128)(2,1)} %constant_dynamic-slice_fusion.2), channel_id=1, source_target_pairs={{0,2},{1,3},{2,0},{3,1},{4,6},{5,7},{6,4},{7,5},{8,10},{9,11},{10,... | collective-permute-start | bytes 1474568 | tf_op jit(solution)/shard_map/ppermute | solution.py:299
  9.4 1.8 %collective-permute-start.1 = (bf16[256,1280]{1,0:T(8,128)(2,1)}, bf16[256,1280]{1,0:T(8,128)(2,1)}, u32[]{:S(2)}, u32[]{:S(2)}) collective-permute-start(bf16[256,1280]{1,0:T(8,128)(2,1)} %fusion.6.refs_2_), channel_id=1, source_target_pairs={{0,2},{1,3},{2,0},{3,1},{4,6},{5,7},{6,4},{7,5},{8,10},{9,11},{10,... | collective-permute-start | bytes 1966088 | tf_op jit(solution)/shard_map/ppermute | solution.py:299
  11.3 9.4 %collective-permute-done.3 = bf16[40,960]{1,0:T(8,128)(2,1)S(1)} collective-permute-done((bf16[40,960]{1,0:T(8,128)(2,1)S(1)}, bf16[40,960]{1,0:T(8,128)(2,1)S(1)}, u32[]{:S(2)}, u32[]{:S(2)}) %collective-permute-start.3) | collective-permute-done | bytes 76832 | tf_op jit(solution)/shard_map/ppermute | solution.py:259
  20.7 1.3 broadcast_in_dim.15
  22.0 8.0 %all-to-all-start = ((bf16[16,80,576]{2,1,0:T(8,128)(2,1)}), bf16[16,80,576]{2,1,0:T(8,128)(2,1)S(1)}, u32[]{:S(2)}, u32[]{:S(2)}) async-start(bf16[16,80,576]{2,1,0:T(8,128)(2,1)} %broadcast_in_dim.15), calls=%async_computation | async-start | bytes 3276800 | tf_op jit(solution)/shard_map/all_to_all | solution.py:264
  31.4 1.8 %collective-permute-done.1.refs_4_ = bf16[256,1280]{1,0:T(8,128)(2,1)} collective-permute-done((bf16[256,1280]{1,0:T(8,128)(2,1)}, bf16[256,1280]{1,0:T(8,128)(2,1)}, u32[]{:S(2)}, u32[]{:S(2)}) %collective-permute-start.1) | collective-permute-done | bytes 655392 | tf_op jit(solution)/shard_map/ppermute | solution.py:299
  33.4 5.0 %gather_fusion = bf16[1024,320]{1,0:T(8,128)(2,1)} fusion(bf16[1536,320]{1,0:T(8,128)(2,1)S(1)} %pad_maximum_fusion, s32[1024]{0:T(1024)S(1)} %broadcast_clamp_fusion), kind=kCustom, calls=%fused_computation | custom fusion | bytes 1314816 | tf_op jit(solution)/shard_map/jit(_take)/gather | solution.py:332
  38.4 1.3 broadcast_select_fusion
  40.0 12.1 %all-to-all-done = bf16[16,80,576]{2,1,0:T(8,128)(2,1)S(1)} async-done(((bf16[16,80,576]{2,1,0:T(8,128)(2,1)}), bf16[16,80,576]{2,1,0:T(8,128)(2,1)S(1)}, u32[]{:S(2)}, u32[]{:S(2)}) %all-to-all-start) | async-done | bytes 1474592 | tf_op jit(solution)/shard_map/all_to_all | solution.py:264
  53.2 4.2 %all-to-all-start.1 = ((bf16[16,80,384]{2,1,0:T(8,128)(2,1)}), bf16[16,80,384]{2,1,0:T(8,128)(2,1)S(1)}, u32[]{:S(2)}, u32[]{:S(2)}) async-start(bf16[16,80,384]{2,1,0:T(8,128)(2,1)} %broadcast_in_dim.39), calls=%async_computation.1 | async-start | bytes 1966080 | tf_op jit(solution)/shard_map/all_to_all | solution.py:264
  57.5 17.0 %attention_backward.2 = (bf16[1024,576]{1,0:T(8,128)(2,1)S(1)}, bf16[1280,576]{1,0:T(8,128)(2,1)}) custom-call(s32[3]{0:T(128)S(1)} %bitcast.57, s32[1]{0:T(128)} %bitcast.refs_1_.refs_0_, bf16[256,1280]{1,0:T(8,128)(2,1)} %fusion.6.refs_2_, bf16[256,1280]{1,0:T(8,128)(2,1)} %collective-permute-done.refs_3_, ...), custom_call_target="tpu_custom_call" | custom-call | flops 15000000512 | bytes 8000000 | tf_op jit(solution)/shard_map/attention_backward/pallas_call | solution.py:196
  75.5 11.4 %all-to-all-start.3 = ((bf16[16,80,576]{2,1,0:T(8,128)(2,1)}), bf16[16,80,576]{2,1,0:T(8,128)(2,1)}, u32[]{:S(2)}, u32[]{:S(2)}) async-start(bf16[16,80,576]{2,1,0:T(8,128)(2,1)} %bitcast.23), calls=%async_computation.3 | async-start | bytes 3276800 | tf_op jit(solution)/shard_map/all_to_all | solution.py:273
  86.9 12.7 %attention_backward.3 = (bf16[1024,384]{1,0:T(8,128)(2,1)S(1)}, bf16[1280,384]{1,0:T(8,128)(2,1)S(1)}) custom-call(s32[3]{0:T(128)S(1)} %bitcast.58, s32[1]{0:T(128)} %bitcast.refs_1_.refs_0_, bf16[256,1280]{1,0:T(8,128)(2,1)} %fusion.6.refs_2_, bf16[256,1280]{1,0:T(8,128)(2,1)} %collective-permute-done.refs_3_, ...), custom_call_target="tpu_custom_call" | custom-call | flops 10000000000 | bytes 8000000 | tf_op jit(solution)/shard_map/attention_backward/pallas_call | solution.py:196
  101.6 6.2 %all-to-all-done.3 = bf16[16,80,576]{2,1,0:T(8,128)(2,1)} async-done(((bf16[16,80,576]{2,1,0:T(8,128)(2,1)}), bf16[16,80,576]{2,1,0:T(8,128)(2,1)}, u32[]{:S(2)}, u32[]{:S(2)}) %all-to-all-start.3) | async-done | bytes 1474592 | tf_op jit(solution)/shard_map/all_to_all | solution.py:273
  107.8 4.5 %all-to-all-start.2 = ((bf16[16,80,384]{2,1,0:T(8,128)(2,1)}), bf16[16,80,384]{2,1,0:T(8,128)(2,1)}, u32[]{:S(2)}, u32[]{:S(2)}) async-start(bf16[16,80,384]{2,1,0:T(8,128)(2,1)} %bitcast.56), calls=%async_computation.2 | async-start | bytes 1966080 | tf_op jit(solution)/shard_map/all_to_all | solution.py:273
  113.6 2.4 %norm_grad.2 = (f32[256,1280]{1,0:T(8,128)S(1)}, bf16[256,1280]{1,0:T(8,128)(2,1)}) custom-call(s32[1]{0:T(128)} %bitcast.refs_1_.refs_0_, bf16[1024,576]{1,0:T(8,128)(2,1)S(1)} %copy-done.7, bf16[1024,384]{1,0:T(8,128)(2,1)S(1)} %copy-done.10, bf16[1280,576]{1,0:T(8,128)(2,1)S(1)} %bitcast.51, bf16[1280,384]{1,0:T(8,128)(2,1)S(1)} %bitcast.54), custom_call_target="tpu_custom_call" | custom-call | flops 1300000000 | bytes 6000000 | tf_op jit(solution)/shard_map/norm_grad/pallas_call | solution.py:226
  117.1 1.8 %convert_reduce_fusion = f32[80,576]{1,0:T(8,128)S(1)} fusion(bf16[16,80,576]{2,1,0:T(8,128)(2,1)} %all-to-all-done.3), kind=kLoop, calls=%fused_computation.1 | loop fusion | flops 1428480 | bytes 1658880 | tf_op jit(solution)/shard_map/reduce_sum | solution.py:281
  119.7 2.3 %norm_grad.3 = (f32[256,1280]{1,0:T(8,128)S(1)}, bf16[256,1280]{1,0:T(8,128)(2,1)}) custom-call(s32[1]{0:T(128)} %bitcast.refs_1_.refs_0_, bf16[1024,576]{1,0:T(8,128)(2,1)S(1)} %copy-done.8, bf16[1024,384]{1,0:T(8,128)(2,1)S(1)} %copy-done.11, bf16[1280,576]{1,0:T(8,128)(2,1)S(1)} %bitcast.52, bf16[1280,384]{1,0:T(8,128)(2,1)S(1)} %bitcast.55), custom_call_target="tpu_custom_call" | custom-call | flops 1300000000 | bytes 6000000 | tf_op jit(solution)/shard_map/norm_grad/pallas_call | solution.py:226
  123.3 2.7 %all-to-all-done.2 = bf16[16,80,384]{2,1,0:T(8,128)(2,1)} async-done(((bf16[16,80,384]{2,1,0:T(8,128)(2,1)}), bf16[16,80,384]{2,1,0:T(8,128)(2,1)}, u32[]{:S(2)}, u32[]{:S(2)}) %all-to-all-start.2) | async-done | bytes 983072 | tf_op jit(solution)/shard_map/all_to_all | solution.py:273
  126.0 1.3 convert_reduce_fusion.1
  130.1 1.5 %collective-permute-done.10 = bf16[40,384]{1,0:T(8,128)(2,1)S(1)} collective-permute-done((bf16[40,384]{1,0:T(8,128)(2,1)S(1)}, bf16[40,384]{1,0:T(8,128)(2,1)S(1)}, u32[]{:S(2)}, u32[]{:S(2)}) %collective-permute-start.10) | collective-permute-done | bytes 30752 | tf_op jit(solution)/shard_map/ppermute | solution.py:259
  132.7 12.4 %collective-permute-done.9 = bf16[256,1280]{1,0:T(8,128)(2,1)S(1)} collective-permute-done((bf16[256,1280]{1,0:T(8,128)(2,1)}, bf16[256,1280]{1,0:T(8,128)(2,1)S(1)}, u32[]{:S(2)}, u32[]{:S(2)}) %collective-permute-start.9) | collective-permute-done | bytes 655392 | tf_op jit(solution)/shard_map/ppermute | solution.py:299
  145.1 1.7 %fusion.18 = (f32[256]{0:T(256)S(1)}, f32[256]{0:T(256)S(1)}, f32[256,1280]{1,0:T(8,128)S(1)}) fusion(f32[256]{0:T(256)S(1)} %add_rsqrt_fusion, f32[256]{0:T(256)S(1)} %broadcast_multiply_fusion.2, bf16[256,1280]{1,0:T(8,128)(2,1)S(1)} %copy-done.13, f32[1280]{0:T(1024)S(1)} %copy-done.15, bf16[256,1280]{1,0:T(8,128)(2,1)S(1)} %collective-permute-done.9, ...), kind=kLoop, calls=%fused_computation.66 | loop fusion | flops 3603968 | bytes 4596736 | tf_op jit(solution)/shard_map/reduce_sum | solution.py:30
  (91 shorter events, 18.9 us)
Async XLA Ops:
  0.6 7.1 %copy-start.12 = (bf16[256,1280]{1,0:T(8,128)(2,1)S(1)}, bf16[256,1280]{1,0:T(8,128)(2,1)}, u32[]{:S(2)}) copy-start(bf16[256,1280]{1,0:T(8,128)(2,1)} %param.7) | copy-start | bytes 1966084
  0.7 7.6 %copy-start.15 = (f32[1280]{0:T(1024)S(1)}, f32[1280]{0:T(1024)}, u32[]{:S(2)}) copy-start(f32[1280]{0:T(1024)} %param.11) | copy-start | bytes 15364
  0.7 7.6 %copy-start.16 = (f32[1280]{0:T(1024)S(1)}, f32[1280]{0:T(1024)}, u32[]{:S(2)}) copy-start(f32[1280]{0:T(1024)} %param.12) | copy-start | bytes 15364
  2.6 27.8 %collective-permute-start.5 = (bf16[384,640]{1,0:T(8,128)(2,1)}, bf16[384,640]{1,0:T(8,128)(2,1)S(1)}, u32[]{:S(2)}, u32[]{:S(2)}) collective-permute-start(bf16[384,640]{1,0:T(8,128)(2,1)} %constant_dynamic-slice_fusion.2), channel_id=1, source_target_pairs={{0,2},{1,3},{2,0},{3,1},{4,6},{5,7},{6,4},{7,5},{8,10},{9,11},{10,... | collective-permute-start | bytes 1474568 | tf_op jit(solution)/shard_map/ppermute | solution.py:299
  7.0 13.6 %collective-permute-start.3 = (bf16[40,960]{1,0:T(8,128)(2,1)S(1)}, bf16[40,960]{1,0:T(8,128)(2,1)S(1)}, u32[]{:S(2)}, u32[]{:S(2)}) collective-permute-start(bf16[40,960]{1,0:T(8,128)(2,1)S(1)} %concatenate.25), channel_id=1, source_target_pairs={{0,4},{4,0},{8,12},{12,8},{16,20},{20,16},{24,28},{28,24},{32,36},... | collective-permute-start | bytes 230408 | tf_op jit(solution)/shard_map/ppermute | solution.py:259
  9.4 23.8 %collective-permute-start.1 = (bf16[256,1280]{1,0:T(8,128)(2,1)}, bf16[256,1280]{1,0:T(8,128)(2,1)}, u32[]{:S(2)}, u32[]{:S(2)}) collective-permute-start(bf16[256,1280]{1,0:T(8,128)(2,1)} %fusion.6.refs_2_), channel_id=1, source_target_pairs={{0,2},{1,3},{2,0},{3,1},{4,6},{5,7},{6,4},{7,5},{8,10},{9,11},{10,... | collective-permute-start | bytes 1966088 | tf_op jit(solution)/shard_map/ppermute | solution.py:299
  11.3 46.2 %collective-permute-start = (bf16[256,1280]{1,0:T(8,128)(2,1)}, bf16[256,1280]{1,0:T(8,128)(2,1)}, u32[]{:S(2)}, u32[]{:S(2)}) collective-permute-start(bf16[256,1280]{1,0:T(8,128)(2,1)} %fusion.6.refs_2_), channel_id=1, source_target_pairs={{0,1},{1,0},{2,3},{3,2},{4,5},{5,4},{6,7},{7,6},{8,9},{9,8},{10,11... | collective-permute-start | bytes 1966088 | tf_op jit(solution)/shard_map/ppermute | solution.py:303
  22.0 8.0 %copy-start.14 = (bf16[384,1280]{1,0:T(8,128)(2,1)S(1)}, bf16[384,1280]{1,0:T(8,128)(2,1)}, u32[]{:S(2)}) copy-start(bf16[384,1280]{1,0:T(8,128)(2,1)} %param.10) | copy-start | bytes 2949124
  22.0 30.1 %all-to-all-start = ((bf16[16,80,576]{2,1,0:T(8,128)(2,1)}), bf16[16,80,576]{2,1,0:T(8,128)(2,1)S(1)}, u32[]{:S(2)}, u32[]{:S(2)}) async-start(bf16[16,80,576]{2,1,0:T(8,128)(2,1)} %broadcast_in_dim.15), calls=%async_computation | async-start | bytes 3276800 | tf_op jit(solution)/shard_map/all_to_all | solution.py:264
  30.3 2.9 %collective-permute-start.4 = (bf16[384,320]{1,0:T(8,128)(2,1)S(1)}, bf16[384,320]{1,0:T(8,128)(2,1)S(1)}, u32[]{:S(2)}, u32[]{:S(2)}) collective-permute-start(bf16[384,320]{1,0:T(8,128)(2,1)S(1)} %get-tuple-element.28), channel_id=1, source_target_pairs={{0,1},{1,0},{2,3},{3,2},{4,5},{5,4},{6,7},{7,6},{8,9},{9,8},{10,11... | collective-permute-start | bytes 737288 | tf_op jit(solution)/shard_map/ppermute | solution.py:303
  30.7 2.5 %collective-permute-start.6 = (bf16[384,320]{1,0:T(8,128)(2,1)S(1)}, bf16[384,320]{1,0:T(8,128)(2,1)S(1)}, u32[]{:S(2)}, u32[]{:S(2)}) collective-permute-start(bf16[384,320]{1,0:T(8,128)(2,1)S(1)} %get-tuple-element.30), channel_id=1, source_target_pairs={{0,1},{1,0},{2,3},{3,2},{4,5},{5,4},{6,7},{7,6},{8,9},{9,8},{10,11... | collective-permute-start | bytes 737288 | tf_op jit(solution)/shard_map/ppermute | solution.py:303
  33.2 24.2 %collective-permute-start.2 = (bf16[256,1280]{1,0:T(8,128)(2,1)}, bf16[256,1280]{1,0:T(8,128)(2,1)}, u32[]{:S(2)}, u32[]{:S(2)}) collective-permute-start(bf16[256,1280]{1,0:T(8,128)(2,1)} %collective-permute-done.1.refs_4_), channel_id=1, source_target_pairs={{0,1},{1,0},{2,3},{3,2},{4,5},{5,4},{6,7},{7,6},{8,9},{9,8},{10,11... | collective-permute-start | bytes 1966088 | tf_op jit(solution)/shard_map/ppermute | solution.py:303
  53.2 22.3 %all-to-all-start.1 = ((bf16[16,80,384]{2,1,0:T(8,128)(2,1)}), bf16[16,80,384]{2,1,0:T(8,128)(2,1)S(1)}, u32[]{:S(2)}, u32[]{:S(2)}) async-start(bf16[16,80,384]{2,1,0:T(8,128)(2,1)} %broadcast_in_dim.39), calls=%async_computation.1 | async-start | bytes 1966080 | tf_op jit(solution)/shard_map/all_to_all | solution.py:264
  75.5 36.8 %copy-start.2 = (bf16[16,80,384]{2,1,0:T(8,128)(2,1)}, bf16[16,80,384]{2,1,0:T(8,128)(2,1)S(1)}, u32[]{:S(2)}) copy-start(bf16[16,80,384]{2,1,0:T(8,128)(2,1)S(1)} %all-to-all-done.1) | copy-start | bytes 2949124
  75.5 32.3 %all-to-all-start.3 = ((bf16[16,80,576]{2,1,0:T(8,128)(2,1)}), bf16[16,80,576]{2,1,0:T(8,128)(2,1)}, u32[]{:S(2)}, u32[]{:S(2)}) async-start(bf16[16,80,576]{2,1,0:T(8,128)(2,1)} %bitcast.23), calls=%async_computation.3 | async-start | bytes 3276800 | tf_op jit(solution)/shard_map/all_to_all | solution.py:273
  107.8 18.2 %all-to-all-start.2 = ((bf16[16,80,384]{2,1,0:T(8,128)(2,1)}), bf16[16,80,384]{2,1,0:T(8,128)(2,1)}, u32[]{:S(2)}, u32[]{:S(2)}) async-start(bf16[16,80,384]{2,1,0:T(8,128)(2,1)} %bitcast.56), calls=%async_computation.2 | async-start | bytes 1966080 | tf_op jit(solution)/shard_map/all_to_all | solution.py:273
  113.6 6.1 %copy-start.8 = (bf16[1024,576]{1,0:T(8,128)(2,1)S(1)}, bf16[1024,576]{1,0:T(8,128)(2,1)}, u32[]{:S(2)}) copy-start(bf16[1024,576]{1,0:T(8,128)(2,1)} %copy-done.6) | copy-start | bytes 3538948
  118.9 4.2 %collective-permute-start.11 = (bf16[40,576]{1,0:T(8,128)(2,1)S(1)}, bf16[40,576]{1,0:T(8,128)(2,1)S(1)}, u32[]{:S(2)}, u32[]{:S(2)}) collective-permute-start(bf16[40,576]{1,0:T(8,128)(2,1)S(1)} %fusion.12), channel_id=1, source_target_pairs={{0,4},{4,0},{8,12},{12,8},{16,20},{20,16},{24,28},{28,24},{32,36},... | collective-permute-start | bytes 138248 | tf_op jit(solution)/shard_map/ppermute | solution.py:259
  122.1 10.6 %collective-permute-start.7 = (bf16[256,1280]{1,0:T(8,128)(2,1)}, bf16[256,1280]{1,0:T(8,128)(2,1)}, u32[]{:S(2)}, u32[]{:S(2)}) collective-permute-start(bf16[256,1280]{1,0:T(8,128)(2,1)} %get-tuple-element.17), channel_id=1, source_target_pairs={{0,1},{1,0},{2,3},{3,2},{4,5},{5,4},{6,7},{7,6},{8,9},{9,8},{10,11... | collective-permute-start | bytes 1966088 | tf_op jit(solution)/shard_map/ppermute | solution.py:303
  122.1 6.1 %collective-permute-start.8 = (bf16[256,1280]{1,0:T(8,128)(2,1)}, bf16[256,1280]{1,0:T(8,128)(2,1)S(1)}, u32[]{:S(2)}, u32[]{:S(2)}) collective-permute-start(bf16[256,1280]{1,0:T(8,128)(2,1)} %get-tuple-element.19), channel_id=1, source_target_pairs={{0,1},{1,0},{2,3},{3,2},{4,5},{5,4},{6,7},{7,6},{8,9},{9,8},{10,11... | collective-permute-start | bytes 1966088 | tf_op jit(solution)/shard_map/ppermute | solution.py:303
  127.3 4.3 %collective-permute-start.10 = (bf16[40,384]{1,0:T(8,128)(2,1)S(1)}, bf16[40,384]{1,0:T(8,128)(2,1)S(1)}, u32[]{:S(2)}, u32[]{:S(2)}) collective-permute-start(bf16[40,384]{1,0:T(8,128)(2,1)S(1)} %fusion.13), channel_id=1, source_target_pairs={{0,4},{4,0},{8,12},{12,8},{16,20},{20,16},{24,28},{28,24},{32,36},... | collective-permute-start | bytes 92168 | tf_op jit(solution)/shard_map/ppermute | solution.py:259
  128.2 16.9 %copy-start.1 = (f32[256,1280]{1,0:T(8,128)S(1)}, f32[256,1280]{1,0:T(8,128)}, u32[]{:S(2)}) copy-start(f32[256,1280]{1,0:T(8,128)} %copy-done) | copy-start | bytes 3932164
  129.1 15.9 %copy-start.13 = (bf16[256,1280]{1,0:T(8,128)(2,1)S(1)}, bf16[256,1280]{1,0:T(8,128)(2,1)}, u32[]{:S(2)}) copy-start(bf16[256,1280]{1,0:T(8,128)(2,1)} %param.7) | copy-start | bytes 1966084
  129.2 15.9 %collective-permute-start.9 = (bf16[256,1280]{1,0:T(8,128)(2,1)}, bf16[256,1280]{1,0:T(8,128)(2,1)S(1)}, u32[]{:S(2)}, u32[]{:S(2)}) collective-permute-start(bf16[256,1280]{1,0:T(8,128)(2,1)} %add_convert_fusion), channel_id=1, source_target_pairs={{0,2},{1,3},{2,0},{3,1},{4,6},{5,7},{6,4},{7,5},{8,10},{9,11},{10,... | collective-permute-start | bytes 1966088 | tf_op jit(solution)/shard_map/ppermute | solution.py:299
  (10 other events, 21.8 us)

commit v7 on v6

--- a/solution.py
+++ b/solution.py
@@ -259,13 +259,14 @@
     return lax.ppermute(block, "dp", [(i, i ^ 1) for i in range(groups)])
 
 
-def gather_plane(block):
+def spread_plane(block):
+    return jnp.broadcast_to(block[None], (lax.axis_size("dp") // 2,) + block.shape)
+
+
+def gather_plane(spread):
     groups = lax.axis_size("dp")
-    spread = lax.all_to_all(
-        jnp.broadcast_to(block[None], (groups // 2,) + block.shape), "dp", 0, 0,
-        axis_index_groups=plane_groups(groups), tiled=True,
-    )
-    return spread.reshape(groups // 2 * block.shape[0], block.shape[1])
+    got = lax.all_to_all(spread, "dp", 0, 0, axis_index_groups=plane_groups(groups), tiled=True)
+    return got.reshape(got.shape[0] * got.shape[1], got.shape[2])
 
 
 def exchange_terms(term):
@@ -314,7 +315,8 @@
     other = swap_pair(shard)
     both = jnp.where(lax.axis_index("dp") % 2 == 0, jnp.concatenate([shard, other]), jnp.concatenate([other, shard]))
     cut = HD * len(chunk_blocks(CHUNKS[0]))
-    shards = [both[:, :cut], both[:, cut:]]
+    shards = [spread_plane(both[:, :cut])]
+    shards.append(spread_plane(both[:, cut:]))
     weights = [gather_plane(shards[0])]
     own, standard, inv_std = norm_forward(hidden_in, norm_gain, norm_bias)
     far = swap_side(own)
@@ -322,14 +324,15 @@
     sides = [lax.dynamic_slice_in_dim(thinker_grad, 2 * head_cols * at, 2 * head_cols, 1) for at in (side, 1 - side)]
     far_think = swap_side(sides[1])
     cols = lambda block, at: lax.dynamic_slice_in_dim(block, head_cols * at, head_cols, 1)
-    near_think = swap_core(cols(sides[0], 1 - core))
+    near_half, own_half = cols(sides[0], 1 - core), cols(sides[0], core)
+    near_think = swap_core(near_half)
     far_near = swap_core(far)
     far_near_think = swap_core(cols(far_think, 1 - core))
     shard, weights[0] = lax.optimization_barrier((shards[1], weights[0]))
     weights.append(gather_plane(shard))
-    moved = jnp.concatenate([cols(sides[0], core), near_think, cols(far_think, core), far_near_think], axis=0)
+    moved = jnp.concatenate([own_half, near_think, cols(far_think, core), far_near_think], axis=0)
     rows_at = ((token_positions // think_rows) ^ place) * think_rows + token_positions % think_rows
-    out_grad = grad_tiles(jnp.take(moved, rows_at, axis=0))
+    out_grad = grad_tiles(jnp.take(moved, rows_at, axis=0, mode="clip"))
     pieces = (own, near, far, far_near)
     at = place.reshape(1)
     grads, terms = [], []

time: 149 us -> 147 us (0.987)
  the two profiles are of different devices: /device:TPU:0 before, /device:TPU:6 now
where the time goes in v7:
time: 147 us; the launch traced here: 146 us
  Pallas kernels  41.9 us (29%)
  starting transfers between devices  40.2 us (27%)
  waiting for transfers between devices  35.1 us (24%)
  local copies, waits for them, and re-layouts  16.9 us (11%)
  other arithmetic  10.9 us (7%)
    pallas_call x2, Pallas kernels, attention(): pl.pallas_call(body, out_shape=(jax.ShapeDtypeStruct((rows, columns), BF1...  37.2 us
    ppermute x3, waiting for transfers between devices, swap_side(): return lax.ppermute(block, 'frame', FRAME_SIDE)  27.8 us
    all_to_all x2, starting transfers between devices, gather_plane(): lax.all_to_all(spread, 'dp', 0, 0, axis_index_groups=plane_groups(groups)...  16.7 us
    all_to_all x2, starting transfers between devices, exchange_terms(): lax.all_to_all(term.reshape(groups // 2, term.shape[0] * 2 // groups, ter...  13.8 us
    ppermute x3, starting transfers between devices, swap_side(): return lax.ppermute(block, 'frame', FRAME_SIDE)  6.54 us
    unnamed x36, local copies, waits for them, and re-layouts  5.38 us
    all_to_all x2, waiting for transfers between devices, exchange_terms(): lax.all_to_all(term.reshape(groups // 2, term.shape[0] * 2 // groups, ter...  5.38 us
    gather x1, local copies, waits for them, and re-layouts, per_device(): out_grad = grad_tiles(jnp.take(moved, rows_at, axis=0, mode='clip'))  4.98 us
  transfers between devices with their start and end apart: 16, of which 6 were waited for; matrix products, arithmetic and copies ran while one was open for 12% of the time, Pallas kernels for 29%

profile of v7, /device:TPU:6, one launch (start us, length us, event | category | flops | bytes accessed | tf_op | source)
XLA Modules:
  0.0 146.0 jit_solution(18329432107529687869)
XLA Ops:
  1.8 1.7 %collective-permute-start.3 = (bf16[40,960]{1,0:T(8,128)(2,1)S(1)}, bf16[40,960]{1,0:T(8,128)(2,1)S(1)}, u32[]{:S(2)}, u32[]{:S(2)}) collective-permute-start(bf16[40,960]{1,0:T(8,128)(2,1)S(1)} %concatenate.25), channel_id=1, source_target_pairs={{0,4},{4,0},{8,12},{12,8},{16,20},{20,16},{24,28},{28,24},{32,36},... | collective-permute-start | bytes 230408 | tf_op jit(solution)/shard_map/ppermute | solution.py:259
  3.4 1.3 convert_reduce_fusion.2
  6.2 2.9 %collective-permute-start.1 = (bf16[256,1280]{1,0:T(8,128)(2,1)}, bf16[256,1280]{1,0:T(8,128)(2,1)}, u32[]{:S(2)}, u32[]{:S(2)}) collective-permute-start(bf16[256,1280]{1,0:T(8,128)(2,1)} %fusion.6.refs_2_), channel_id=1, source_target_pairs={{0,2},{1,3},{2,0},{3,1},{4,6},{5,7},{6,4},{7,5},{8,10},{9,11},{10,... | collective-permute-start | bytes 1966088 | tf_op jit(solution)/shard_map/ppermute | solution.py:300
  9.2 1.3 broadcast_in_dim.10
  10.5 8.4 %all-to-all-start = ((bf16[16,80,576]{2,1,0:T(8,128)(2,1)}), bf16[16,80,576]{2,1,0:T(8,128)(2,1)S(1)}, u32[]{:S(2)}, u32[]{:S(2)}) async-start(bf16[16,80,576]{2,1,0:T(8,128)(2,1)} %broadcast_in_dim.10), calls=%async_computation | async-start | bytes 3276800 | tf_op jit(solution)/shard_map/all_to_all | solution.py:268
  20.7 13.9 %collective-permute-done.5 = bf16[384,640]{1,0:T(8,128)(2,1)S(1)} collective-permute-done((bf16[384,640]{1,0:T(8,128)(2,1)}, bf16[384,640]{1,0:T(8,128)(2,1)S(1)}, u32[]{:S(2)}, u32[]{:S(2)}) %collective-permute-start.5) | collective-permute-done | bytes 491552 | tf_op jit(solution)/shard_map/ppermute | solution.py:300
  36.7 5.0 %gather_fusion = bf16[1024,320]{1,0:T(8,128)(2,1)} fusion(bf16[1536,320]{1,0:T(8,128)(2,1)S(1)} %pad_maximum_fusion, s32[1024]{0:T(1024)S(1)} %fusion.17), kind=kCustom, calls=%fused_computation | custom fusion | bytes 1314816 | tf_op jit(solution)/shard_map/jit(_take)/gather | solution.py:335
  44.1 8.3 %all-to-all-start.1 = ((bf16[16,80,384]{2,1,0:T(8,128)(2,1)}), bf16[16,80,384]{2,1,0:T(8,128)(2,1)S(1)}, u32[]{:S(2)}, u32[]{:S(2)}) async-start(bf16[16,80,384]{2,1,0:T(8,128)(2,1)} %broadcast_in_dim.9), calls=%async_computation.1 | async-start | bytes 1966080 | tf_op jit(solution)/shard_map/all_to_all | solution.py:268
  52.4 21.1 %attention_backward.2 = (bf16[1024,576]{1,0:T(8,128)(2,1)S(1)}, bf16[1280,576]{1,0:T(8,128)(2,1)}) custom-call(s32[3]{0:T(128)S(1)} %bitcast.57, s32[1]{0:T(128)} %bitcast.refs_1_.refs_0_, bf16[256,1280]{1,0:T(8,128)(2,1)} %fusion.6.refs_2_, bf16[256,1280]{1,0:T(8,128)(2,1)} %collective-permute-done.refs_3_, ...), custom_call_target="tpu_custom_call" | custom-call | flops 15000000512 | bytes 8000000 | tf_op jit(solution)/shard_map/attention_backward/pallas_call | solution.py:196
  74.6 7.2 %all-to-all-start.3 = ((bf16[16,80,576]{2,1,0:T(8,128)(2,1)}), bf16[16,80,576]{2,1,0:T(8,128)(2,1)}, u32[]{:S(2)}, u32[]{:S(2)}) async-start(bf16[16,80,576]{2,1,0:T(8,128)(2,1)} %bitcast.23), calls=%async_computation.3 | async-start | bytes 3276800 | tf_op jit(solution)/shard_map/all_to_all | solution.py:274
  81.8 16.1 %attention_backward.3 = (bf16[1024,384]{1,0:T(8,128)(2,1)S(1)}, bf16[1280,384]{1,0:T(8,128)(2,1)S(1)}) custom-call(s32[3]{0:T(128)S(1)} %bitcast.58, s32[1]{0:T(128)} %bitcast.refs_1_.refs_0_, bf16[256,1280]{1,0:T(8,128)(2,1)} %fusion.6.refs_2_, bf16[256,1280]{1,0:T(8,128)(2,1)} %collective-permute-done.refs_3_, ...), custom_call_target="tpu_custom_call" | custom-call | flops 10000000000 | bytes 8000000 | tf_op jit(solution)/shard_map/attention_backward/pallas_call | solution.py:196
  99.8 4.2 %all-to-all-done.3 = bf16[16,80,576]{2,1,0:T(8,128)(2,1)} async-done(((bf16[16,80,576]{2,1,0:T(8,128)(2,1)}), bf16[16,80,576]{2,1,0:T(8,128)(2,1)}, u32[]{:S(2)}, u32[]{:S(2)}) %all-to-all-start.3) | async-done | bytes 1474592 | tf_op jit(solution)/shard_map/all_to_all | solution.py:274
  104.0 6.6 %all-to-all-start.2 = ((bf16[16,80,384]{2,1,0:T(8,128)(2,1)}), bf16[16,80,384]{2,1,0:T(8,128)(2,1)}, u32[]{:S(2)}, u32[]{:S(2)}) async-start(bf16[16,80,384]{2,1,0:T(8,128)(2,1)} %bitcast.56), calls=%async_computation.2 | async-start | bytes 1966080 | tf_op jit(solution)/shard_map/all_to_all | solution.py:274
  110.5 1.3 copy-done.7
  111.9 2.4 %norm_grad.2 = (f32[256,1280]{1,0:T(8,128)S(1)}, bf16[256,1280]{1,0:T(8,128)(2,1)}) custom-call(s32[1]{0:T(128)} %bitcast.refs_1_.refs_0_, bf16[1024,576]{1,0:T(8,128)(2,1)S(1)} %copy-done.7, bf16[1024,384]{1,0:T(8,128)(2,1)S(1)} %copy-done.10, bf16[1280,576]{1,0:T(8,128)(2,1)S(1)} %bitcast.51, bf16[1280,384]{1,0:T(8,128)(2,1)S(1)} %bitcast.54), custom_call_target="tpu_custom_call" | custom-call | flops 1300000000 | bytes 6000000 | tf_op jit(solution)/shard_map/norm_grad/pallas_call | solution.py:226
  115.3 1.8 %convert_reduce_fusion = f32[80,576]{1,0:T(8,128)S(1)} fusion(bf16[16,80,576]{2,1,0:T(8,128)(2,1)} %all-to-all-done.3), kind=kLoop, calls=%fused_computation.1 | loop fusion | flops 1428480 | bytes 1658880 | tf_op jit(solution)/shard_map/reduce_sum | solution.py:282
  117.3 2.4 %norm_grad.3 = (f32[256,1280]{1,0:T(8,128)S(1)}, bf16[256,1280]{1,0:T(8,128)(2,1)}) custom-call(s32[1]{0:T(128)} %bitcast.refs_1_.refs_0_, bf16[1024,576]{1,0:T(8,128)(2,1)S(1)} %copy-done.8, bf16[1024,384]{1,0:T(8,128)(2,1)S(1)} %copy-done.11, bf16[1280,576]{1,0:T(8,128)(2,1)S(1)} %bitcast.52, bf16[1280,384]{1,0:T(8,128)(2,1)S(1)} %bitcast.55), custom_call_target="tpu_custom_call" | custom-call | flops 1300000000 | bytes 6000000 | tf_op jit(solution)/shard_map/norm_grad/pallas_call | solution.py:226
  120.1 1.2 collective-permute-done.11
  121.5 1.2 all-to-all-done.2
  122.7 1.3 convert_reduce_fusion.1
  125.2 3.0 %collective-permute-start.9 = (bf16[256,1280]{1,0:T(8,128)(2,1)}, bf16[256,1280]{1,0:T(8,128)(2,1)S(1)}, u32[]{:S(2)}, u32[]{:S(2)}) collective-permute-start(bf16[256,1280]{1,0:T(8,128)(2,1)} %add_convert_fusion), channel_id=1, source_target_pairs={{0,2},{1,3},{2,0},{3,1},{4,6},{5,7},{6,4},{7,5},{8,10},{9,11},{10,... | collective-permute-start | bytes 1966088 | tf_op jit(solution)/shard_map/ppermute | solution.py:300
  129.2 13.9 %collective-permute-done.9 = bf16[256,1280]{1,0:T(8,128)(2,1)S(1)} collective-permute-done((bf16[256,1280]{1,0:T(8,128)(2,1)}, bf16[256,1280]{1,0:T(8,128)(2,1)S(1)}, u32[]{:S(2)}, u32[]{:S(2)}) %collective-permute-start.9) | collective-permute-done | bytes 655392 | tf_op jit(solution)/shard_map/ppermute | solution.py:300
  143.1 1.7 %fusion.19 = (f32[256]{0:T(256)S(1)}, f32[256]{0:T(256)S(1)}, f32[256,1280]{1,0:T(8,128)S(1)}) fusion(f32[256]{0:T(256)S(1)} %add_rsqrt_fusion, f32[256]{0:T(256)S(1)} %broadcast_multiply_fusion.2, bf16[256,1280]{1,0:T(8,128)(2,1)S(1)} %copy-done.13, f32[1280]{0:T(1024)S(1)} %copy-done.15, bf16[256,1280]{1,0:T(8,128)(2,1)S(1)} %collective-permute-done.9, ...), kind=kLoop, calls=%fused_computation.63 | loop fusion | flops 3603968 | bytes 4596736 | tf_op jit(solution)/shard_map/reduce_sum | solution.py:30
  144.8 1.3 fusion.10
  (91 shorter events, 15.8 us)
Async XLA Ops:
  1.8 7.3 %collective-permute-start.3 = (bf16[40,960]{1,0:T(8,128)(2,1)S(1)}, bf16[40,960]{1,0:T(8,128)(2,1)S(1)}, u32[]{:S(2)}, u32[]{:S(2)}) collective-permute-start(bf16[40,960]{1,0:T(8,128)(2,1)S(1)} %concatenate.25), channel_id=1, source_target_pairs={{0,4},{4,0},{8,12},{12,8},{16,20},{20,16},{24,28},{28,24},{32,36},... | collective-permute-start | bytes 230408 | tf_op jit(solution)/shard_map/ppermute | solution.py:259
  6.2 29.3 %collective-permute-start.1 = (bf16[256,1280]{1,0:T(8,128)(2,1)}, bf16[256,1280]{1,0:T(8,128)(2,1)}, u32[]{:S(2)}, u32[]{:S(2)}) collective-permute-start(bf16[256,1280]{1,0:T(8,128)(2,1)} %fusion.6.refs_2_), channel_id=1, source_target_pairs={{0,2},{1,3},{2,0},{3,1},{4,6},{5,7},{6,4},{7,5},{8,10},{9,11},{10,... | collective-permute-start | bytes 1966088 | tf_op jit(solution)/shard_map/ppermute | solution.py:300
  10.5 8.4 %copy-start.14 = (bf16[384,1280]{1,0:T(8,128)(2,1)S(1)}, bf16[384,1280]{1,0:T(8,128)(2,1)}, u32[]{:S(2)}) copy-start(bf16[384,1280]{1,0:T(8,128)(2,1)} %param.10) | copy-start | bytes 2949124
  10.5 32.5 %all-to-all-start = ((bf16[16,80,576]{2,1,0:T(8,128)(2,1)}), bf16[16,80,576]{2,1,0:T(8,128)(2,1)S(1)}, u32[]{:S(2)}, u32[]{:S(2)}) async-start(bf16[16,80,576]{2,1,0:T(8,128)(2,1)} %broadcast_in_dim.10), calls=%async_computation | async-start | bytes 3276800 | tf_op jit(solution)/shard_map/all_to_all | solution.py:268
  19.7 16.0 %copy-start.17 = (s32[1024]{0:T(1024)S(1)}, s32[1024]{0:T(1024)}, u32[]{:S(2)}) copy-start(s32[1024]{0:T(1024)} %param.9) | copy-start | bytes 12292
  19.7 14.9 %collective-permute-start.5 = (bf16[384,640]{1,0:T(8,128)(2,1)}, bf16[384,640]{1,0:T(8,128)(2,1)S(1)}, u32[]{:S(2)}, u32[]{:S(2)}) collective-permute-start(bf16[384,640]{1,0:T(8,128)(2,1)} %constant_dynamic-slice_fusion.2), channel_id=1, source_target_pairs={{0,2},{1,3},{2,0},{3,1},{4,6},{5,7},{6,4},{7,5},{8,10},{9,11},{10,... | collective-permute-start | bytes 1474568 | tf_op jit(solution)/shard_map/ppermute | solution.py:300
  20.6 15.2 %collective-permute-start.4 = (bf16[384,320]{1,0:T(8,128)(2,1)S(1)}, bf16[384,320]{1,0:T(8,128)(2,1)S(1)}, u32[]{:S(2)}, u32[]{:S(2)}) collective-permute-start(bf16[384,320]{1,0:T(8,128)(2,1)S(1)} %get-tuple-element.26), channel_id=1, source_target_pairs={{0,1},{1,0},{2,3},{3,2},{4,5},{5,4},{6,7},{7,6},{8,9},{9,8},{10,11... | collective-permute-start | bytes 737288 | tf_op jit(solution)/shard_map/ppermute | solution.py:304
  34.9 1.7 %collective-permute-start.6 = (bf16[384,320]{1,0:T(8,128)(2,1)S(1)}, bf16[384,320]{1,0:T(8,128)(2,1)S(1)}, u32[]{:S(2)}, u32[]{:S(2)}) collective-permute-start(bf16[384,320]{1,0:T(8,128)(2,1)S(1)} %get-tuple-element.28), channel_id=1, source_target_pairs={{0,1},{1,0},{2,3},{3,2},{4,5},{5,4},{6,7},{7,6},{8,9},{9,8},{10,11... | collective-permute-start | bytes 737288 | tf_op jit(solution)/shard_map/ppermute | solution.py:304
  35.0 17.4 %collective-permute-start = (bf16[256,1280]{1,0:T(8,128)(2,1)}, bf16[256,1280]{1,0:T(8,128)(2,1)}, u32[]{:S(2)}, u32[]{:S(2)}) collective-permute-start(bf16[256,1280]{1,0:T(8,128)(2,1)} %fusion.6.refs_2_), channel_id=1, source_target_pairs={{0,1},{1,0},{2,3},{3,2},{4,5},{5,4},{6,7},{7,6},{8,9},{9,8},{10,11... | collective-permute-start | bytes 1966088 | tf_op jit(solution)/shard_map/ppermute | solution.py:304
  35.5 16.9 %collective-permute-start.2 = (bf16[256,1280]{1,0:T(8,128)(2,1)}, bf16[256,1280]{1,0:T(8,128)(2,1)}, u32[]{:S(2)}, u32[]{:S(2)}) collective-permute-start(bf16[256,1280]{1,0:T(8,128)(2,1)} %collective-permute-done.1.refs_4_), channel_id=1, source_target_pairs={{0,1},{1,0},{2,3},{3,2},{4,5},{5,4},{6,7},{7,6},{8,9},{9,8},{10,11... | collective-permute-start | bytes 1966088 | tf_op jit(solution)/shard_map/ppermute | solution.py:304
  43.0 9.3 %copy-start.5 = (s32[1,3]{1,0:T(1,128)S(1)}, s32[1,3]{1,0:T(1,128)}, u32[]{:S(2)}) copy-start(s32[1,3]{1,0:T(1,128)} %param.8) | copy-start | bytes 40
  44.1 30.5 %all-to-all-start.1 = ((bf16[16,80,384]{2,1,0:T(8,128)(2,1)}), bf16[16,80,384]{2,1,0:T(8,128)(2,1)S(1)}, u32[]{:S(2)}, u32[]{:S(2)}) async-start(bf16[16,80,384]{2,1,0:T(8,128)(2,1)} %broadcast_in_dim.9), calls=%async_computation.1 | async-start | bytes 1966080 | tf_op jit(solution)/shard_map/all_to_all | solution.py:268
  74.6 36.0 %copy-start.2 = (bf16[16,80,384]{2,1,0:T(8,128)(2,1)}, bf16[16,80,384]{2,1,0:T(8,128)(2,1)S(1)}, u32[]{:S(2)}) copy-start(bf16[16,80,384]{2,1,0:T(8,128)(2,1)S(1)} %all-to-all-done.1) | copy-start | bytes 2949124
  74.6 29.4 %all-to-all-start.3 = ((bf16[16,80,576]{2,1,0:T(8,128)(2,1)}), bf16[16,80,576]{2,1,0:T(8,128)(2,1)}, u32[]{:S(2)}, u32[]{:S(2)}) async-start(bf16[16,80,576]{2,1,0:T(8,128)(2,1)} %bitcast.23), calls=%async_computation.3 | async-start | bytes 3276800 | tf_op jit(solution)/shard_map/all_to_all | solution.py:274
  104.0 6.6 %copy-start.10 = (bf16[1024,384]{1,0:T(8,128)(2,1)S(1)}, bf16[1024,384]{1,0:T(8,128)(2,1)}, u32[]{:S(2)}) copy-start(bf16[1024,384]{1,0:T(8,128)(2,1)} %copy-done.9) | copy-start | bytes 2359300
  104.0 18.8 %all-to-all-start.2 = ((bf16[16,80,384]{2,1,0:T(8,128)(2,1)}), bf16[16,80,384]{2,1,0:T(8,128)(2,1)}, u32[]{:S(2)}, u32[]{:S(2)}) async-start(bf16[16,80,384]{2,1,0:T(8,128)(2,1)} %bitcast.56), calls=%async_computation.2 | async-start | bytes 1966080 | tf_op jit(solution)/shard_map/all_to_all | solution.py:274
  111.9 5.4 %copy-start.8 = (bf16[1024,576]{1,0:T(8,128)(2,1)S(1)}, bf16[1024,576]{1,0:T(8,128)(2,1)}, u32[]{:S(2)}) copy-start(bf16[1024,576]{1,0:T(8,128)(2,1)} %copy-done.6) | copy-start | bytes 3538948
  117.1 4.2 %collective-permute-start.11 = (bf16[40,576]{1,0:T(8,128)(2,1)S(1)}, bf16[40,576]{1,0:T(8,128)(2,1)S(1)}, u32[]{:S(2)}, u32[]{:S(2)}) collective-permute-start(bf16[40,576]{1,0:T(8,128)(2,1)S(1)} %fusion.12), channel_id=1, source_target_pairs={{0,4},{4,0},{8,12},{12,8},{16,20},{20,16},{24,28},{28,24},{32,36},... | collective-permute-start | bytes 138248 | tf_op jit(solution)/shard_map/ppermute | solution.py:259
  119.6 9.6 %collective-permute-start.7 = (bf16[256,1280]{1,0:T(8,128)(2,1)}, bf16[256,1280]{1,0:T(8,128)(2,1)}, u32[]{:S(2)}, u32[]{:S(2)}) collective-permute-start(bf16[256,1280]{1,0:T(8,128)(2,1)} %get-tuple-element.17), channel_id=1, source_target_pairs={{0,1},{1,0},{2,3},{3,2},{4,5},{5,4},{6,7},{7,6},{8,9},{9,8},{10,11... | collective-permute-start | bytes 1966088 | tf_op jit(solution)/shard_map/ppermute | solution.py:304
  119.6 4.6 %collective-permute-start.8 = (bf16[256,1280]{1,0:T(8,128)(2,1)}, bf16[256,1280]{1,0:T(8,128)(2,1)S(1)}, u32[]{:S(2)}, u32[]{:S(2)}) collective-permute-start(bf16[256,1280]{1,0:T(8,128)(2,1)} %get-tuple-element.19), channel_id=1, source_target_pairs={{0,1},{1,0},{2,3},{3,2},{4,5},{5,4},{6,7},{7,6},{8,9},{9,8},{10,11... | collective-permute-start | bytes 1966088 | tf_op jit(solution)/shard_map/ppermute | solution.py:304
  124.1 4.1 %collective-permute-start.10 = (bf16[40,384]{1,0:T(8,128)(2,1)S(1)}, bf16[40,384]{1,0:T(8,128)(2,1)S(1)}, u32[]{:S(2)}, u32[]{:S(2)}) collective-permute-start(bf16[40,384]{1,0:T(8,128)(2,1)S(1)} %fusion.13), channel_id=1, source_target_pairs={{0,4},{4,0},{8,12},{12,8},{16,20},{20,16},{24,28},{28,24},{32,36},... | collective-permute-start | bytes 92168 | tf_op jit(solution)/shard_map/ppermute | solution.py:259
  124.2 18.9 %copy-start.1 = (f32[256,1280]{1,0:T(8,128)S(1)}, f32[256,1280]{1,0:T(8,128)}, u32[]{:S(2)}) copy-start(f32[256,1280]{1,0:T(8,128)} %copy-done) | copy-start | bytes 3932164
  125.2 18.0 %copy-start.13 = (bf16[256,1280]{1,0:T(8,128)(2,1)S(1)}, bf16[256,1280]{1,0:T(8,128)(2,1)}, u32[]{:S(2)}) copy-start(bf16[256,1280]{1,0:T(8,128)(2,1)} %param.7) | copy-start | bytes 1966084
  125.2 18.0 %collective-permute-start.9 = (bf16[256,1280]{1,0:T(8,128)(2,1)}, bf16[256,1280]{1,0:T(8,128)(2,1)S(1)}, u32[]{:S(2)}, u32[]{:S(2)}) collective-permute-start(bf16[256,1280]{1,0:T(8,128)(2,1)} %add_convert_fusion), channel_id=1, source_target_pairs={{0,2},{1,3},{2,0},{3,1},{4,6},{5,7},{6,4},{7,5},{8,10},{9,11},{10,... | collective-permute-start | bytes 1966088 | tf_op jit(solution)/shard_map/ppermute | solution.py:300
  (12 other events, 24.2 us)

commit v8 on v7

--- a/solution.py
+++ b/solution.py
@@ -221,13 +221,18 @@
 
 
 def norm_grad_blocks(keep_at, give_at, place, grads, weights):
-    shape = (ROWS, weights[0].shape[0])
+    features = weights[0].shape[0]
+    shape = (ROWS, features)
     body = lambda *refs: norm_grad_kernel(keep_at, give_at, *refs)
+    out_block = pl.BlockSpec((ROWS, 256), lambda i: (0, i))
     return pl.pallas_call(
         body,
+        grid=(features // 256,),
         out_shape=(jax.ShapeDtypeStruct(shape, F32), jax.ShapeDtypeStruct(shape, BF16)),
-        in_specs=[SM] + [VM] * 4,
-        out_specs=(VM, VM),
+        in_specs=[SM] + [pl.BlockSpec(grad.shape, lambda i: (0, 0)) for grad in grads] + [
+            pl.BlockSpec((256, weight.shape[1]), lambda i: (i, 0)) for weight in weights
+        ],
+        out_specs=(out_block, out_block),
         compiler_params=pltpu.CompilerParams(vmem_limit_bytes=10 << 20),
         cost_estimate=pl.CostEstimate(flops=1_300_000_000, bytes_accessed=6_000_000, transcendentals=0),
         name="norm_grad",

time: 147 us -> 149 us (1.014)
  the two profiles are of different devices: /device:TPU:6 before, /device:TPU:1 now
where the time goes in v8:
time: 149 us; the launch traced here: 148 us
  starting transfers between devices  48.7 us (33%)
  Pallas kernels  37 us (25%)
  waiting for transfers between devices  33.2 us (22%)
  local copies, waits for them, and re-layouts  17 us (11%)
  other arithmetic  10.9 us (7%)
    pallas_call x2, Pallas kernels, attention(): pl.pallas_call(body, out_shape=(jax.ShapeDtypeStruct((rows, columns), BF1...  29.7 us
    ppermute x3, waiting for transfers between devices, swap_side(): return lax.ppermute(block, 'frame', FRAME_SIDE)  26 us
    all_to_all x2, starting transfers between devices, exchange_terms(): lax.all_to_all(term.reshape(groups // 2, term.shape[0] * 2 // groups, ter...  16 us
    all_to_all x2, starting transfers between devices, gather_plane(): lax.all_to_all(spread, 'dp', 0, 0, axis_index_groups=plane_groups(groups)...  15.3 us
    ppermute x6, starting transfers between devices, swap_core(): return lax.ppermute(block, 'frame', FRAME_CORE)  7.75 us
    pallas_call x2, Pallas kernels, norm_grad_blocks(): pl.pallas_call(body, grid=(features // 256,), out_shape=(jax.ShapeDtypeSt...  7.25 us
    all_to_all x2, waiting for transfers between devices, exchange_terms(): lax.all_to_all(term.reshape(groups // 2, term.shape[0] * 2 // groups, ter...  6.71 us
    ppermute x3, starting transfers between devices, swap_side(): return lax.ppermute(block, 'frame', FRAME_SIDE)  5.58 us
  transfers between devices with their start and end apart: 16, of which 4 were waited for; matrix products, arithmetic and copies ran while one was open for 12% of the time, Pallas kernels for 25%

profile of v8, /device:TPU:1, one launch (start us, length us, event | category | flops | bytes accessed | tf_op | source)
XLA Modules:
  0.0 147.8 jit_solution(773857836853384374)
XLA Ops:
  1.8 2.2 %collective-permute-start.3 = (bf16[40,960]{1,0:T(8,128)(2,1)S(1)}, bf16[40,960]{1,0:T(8,128)(2,1)S(1)}, u32[]{:S(2)}, u32[]{:S(2)}) collective-permute-start(bf16[40,960]{1,0:T(8,128)(2,1)S(1)} %concatenate.25), channel_id=1, source_target_pairs={{0,4},{4,0},{8,12},{12,8},{16,20},{20,16},{24,28},{28,24},{32,36},... | collective-permute-start | bytes 230408 | tf_op jit(solution)/shard_map/ppermute | solution.py:264
  6.7 2.6 %collective-permute-start.1 = (bf16[256,1280]{1,0:T(8,128)(2,1)}, bf16[256,1280]{1,0:T(8,128)(2,1)}, u32[]{:S(2)}, u32[]{:S(2)}) collective-permute-start(bf16[256,1280]{1,0:T(8,128)(2,1)} %fusion.6.refs_2_), channel_id=1, source_target_pairs={{0,2},{1,3},{2,0},{3,1},{4,6},{5,7},{6,4},{7,5},{8,10},{9,11},{10,... | collective-permute-start | bytes 1966088 | tf_op jit(solution)/shard_map/ppermute | solution.py:305
  9.4 1.3 broadcast_in_dim.10
  10.8 7.7 %all-to-all-start = ((bf16[16,80,576]{2,1,0:T(8,128)(2,1)}), bf16[16,80,576]{2,1,0:T(8,128)(2,1)S(1)}, u32[]{:S(2)}, u32[]{:S(2)}) async-start(bf16[16,80,576]{2,1,0:T(8,128)(2,1)} %broadcast_in_dim.10), calls=%async_computation | async-start | bytes 3276800 | tf_op jit(solution)/shard_map/all_to_all | solution.py:273
  20.0 1.9 %collective-permute-start.4 = (bf16[384,320]{1,0:T(8,128)(2,1)S(1)}, bf16[384,320]{1,0:T(8,128)(2,1)S(1)}, u32[]{:S(2)}, u32[]{:S(2)}) collective-permute-start(bf16[384,320]{1,0:T(8,128)(2,1)S(1)} %get-tuple-element.26), channel_id=1, source_target_pairs={{0,1},{1,0},{2,3},{3,2},{4,5},{5,4},{6,7},{7,6},{8,9},{9,8},{10,11... | collective-permute-start | bytes 737288 | tf_op jit(solution)/shard_map/ppermute | solution.py:309
  21.8 12.5 %collective-permute-done.5 = bf16[384,640]{1,0:T(8,128)(2,1)S(1)} collective-permute-done((bf16[384,640]{1,0:T(8,128)(2,1)}, bf16[384,640]{1,0:T(8,128)(2,1)S(1)}, u32[]{:S(2)}, u32[]{:S(2)}) %collective-permute-start.5) | collective-permute-done | bytes 491552 | tf_op jit(solution)/shard_map/ppermute | solution.py:305
  34.6 1.9 %collective-permute-start.6 = (bf16[384,320]{1,0:T(8,128)(2,1)S(1)}, bf16[384,320]{1,0:T(8,128)(2,1)S(1)}, u32[]{:S(2)}, u32[]{:S(2)}) collective-permute-start(bf16[384,320]{1,0:T(8,128)(2,1)S(1)} %get-tuple-element.28), channel_id=1, source_target_pairs={{0,1},{1,0},{2,3},{3,2},{4,5},{5,4},{6,7},{7,6},{8,9},{9,8},{10,11... | collective-permute-start | bytes 737288 | tf_op jit(solution)/shard_map/ppermute | solution.py:309
  37.8 5.0 %gather_fusion = bf16[1024,320]{1,0:T(8,128)(2,1)} fusion(bf16[1536,320]{1,0:T(8,128)(2,1)S(1)} %pad_maximum_fusion, s32[1024]{0:T(1024)S(1)} %fusion.17), kind=kCustom, calls=%fused_computation | custom fusion | bytes 1314816 | tf_op jit(solution)/shard_map/jit(_take)/gather | solution.py:340
  45.2 7.6 %all-to-all-start.1 = ((bf16[16,80,384]{2,1,0:T(8,128)(2,1)}), bf16[16,80,384]{2,1,0:T(8,128)(2,1)S(1)}, u32[]{:S(2)}, u32[]{:S(2)}) async-start(bf16[16,80,384]{2,1,0:T(8,128)(2,1)} %broadcast_in_dim.9), calls=%async_computation.1 | async-start | bytes 1966080 | tf_op jit(solution)/shard_map/all_to_all | solution.py:273
  52.9 17.0 %attention_backward.2 = (bf16[1024,576]{1,0:T(8,128)(2,1)S(1)}, bf16[1280,576]{1,0:T(8,128)(2,1)}) custom-call(s32[3]{0:T(128)S(1)} %bitcast.57, s32[1]{0:T(128)} %bitcast.refs_1_.refs_0_, bf16[256,1280]{1,0:T(8,128)(2,1)} %fusion.6.refs_2_, bf16[256,1280]{1,0:T(8,128)(2,1)} %collective-permute-done.refs_3_, ...), custom_call_target="tpu_custom_call" | custom-call | flops 15000000512 | bytes 8000000 | tf_op jit(solution)/shard_map/attention_backward/pallas_call | solution.py:196
  70.9 10.8 %all-to-all-start.3 = ((bf16[16,80,576]{2,1,0:T(8,128)(2,1)}), bf16[16,80,576]{2,1,0:T(8,128)(2,1)}, u32[]{:S(2)}, u32[]{:S(2)}) async-start(bf16[16,80,576]{2,1,0:T(8,128)(2,1)} %bitcast.23), calls=%async_computation.3 | async-start | bytes 3276800 | tf_op jit(solution)/shard_map/all_to_all | solution.py:279
  81.8 12.7 %attention_backward.3 = (bf16[1024,384]{1,0:T(8,128)(2,1)S(1)}, bf16[1280,384]{1,0:T(8,128)(2,1)S(1)}) custom-call(s32[3]{0:T(128)S(1)} %bitcast.58, s32[1]{0:T(128)} %bitcast.refs_1_.refs_0_, bf16[256,1280]{1,0:T(8,128)(2,1)} %fusion.6.refs_2_, bf16[256,1280]{1,0:T(8,128)(2,1)} %collective-permute-done.refs_3_, ...), custom_call_target="tpu_custom_call" | custom-call | flops 10000000000 | bytes 8000000 | tf_op jit(solution)/shard_map/attention_backward/pallas_call | solution.py:196
  96.4 6.7 %all-to-all-done.3 = bf16[16,80,576]{2,1,0:T(8,128)(2,1)} async-done(((bf16[16,80,576]{2,1,0:T(8,128)(2,1)}), bf16[16,80,576]{2,1,0:T(8,128)(2,1)}, u32[]{:S(2)}, u32[]{:S(2)}) %all-to-all-start.3) | async-done | bytes 1474592 | tf_op jit(solution)/shard_map/all_to_all | solution.py:279
  103.1 5.2 %all-to-all-start.2 = ((bf16[16,80,384]{2,1,0:T(8,128)(2,1)}), bf16[16,80,384]{2,1,0:T(8,128)(2,1)}, u32[]{:S(2)}, u32[]{:S(2)}) async-start(bf16[16,80,384]{2,1,0:T(8,128)(2,1)} %bitcast.56), calls=%async_computation.2 | async-start | bytes 1966080 | tf_op jit(solution)/shard_map/all_to_all | solution.py:279
  108.4 1.3 copy-done.7
  109.7 3.6 %norm_grad.2 = (f32[256,1280]{1,0:T(8,128)S(1)}, bf16[256,1280]{1,0:T(8,128)(2,1)}) custom-call(s32[1]{0:T(128)} %bitcast.refs_1_.refs_0_, bf16[1024,576]{1,0:T(8,128)(2,1)S(1)} %copy-done.7, bf16[1024,384]{1,0:T(8,128)(2,1)S(1)} %copy-done.10, bf16[1280,576]{1,0:T(8,128)(2,1)S(1)} %bitcast.51, bf16[1280,384]{1,0:T(8,128)(2,1)S(1)} %bitcast.54), custom_call_target="tpu_custom_call" | custom-call | flops 1300000000 | bytes 6000000 | tf_op jit(solution)/shard_map/norm_grad/pallas_call | solution.py:228
  114.4 1.8 %convert_reduce_fusion = f32[80,576]{1,0:T(8,128)S(1)} fusion(bf16[16,80,576]{2,1,0:T(8,128)(2,1)} %all-to-all-done.3), kind=kLoop, calls=%fused_computation.1 | loop fusion | flops 1428480 | bytes 1658880 | tf_op jit(solution)/shard_map/reduce_sum | solution.py:287
  116.3 3.6 %norm_grad.3 = (f32[256,1280]{1,0:T(8,128)S(1)}, bf16[256,1280]{1,0:T(8,128)(2,1)}) custom-call(s32[1]{0:T(128)} %bitcast.refs_1_.refs_0_, bf16[1024,576]{1,0:T(8,128)(2,1)S(1)} %copy-done.8, bf16[1024,384]{1,0:T(8,128)(2,1)S(1)} %copy-done.11, bf16[1280,576]{1,0:T(8,128)(2,1)S(1)} %bitcast.52, bf16[1280,384]{1,0:T(8,128)(2,1)S(1)} %bitcast.55), custom_call_target="tpu_custom_call" | custom-call | flops 1300000000 | bytes 6000000 | tf_op jit(solution)/shard_map/norm_grad/pallas_call | solution.py:228
  120.0 3.4 %collective-permute-start.7 = (bf16[256,1280]{1,0:T(8,128)(2,1)}, bf16[256,1280]{1,0:T(8,128)(2,1)}, u32[]{:S(2)}, u32[]{:S(2)}) collective-permute-start(bf16[256,1280]{1,0:T(8,128)(2,1)} %get-tuple-element.17), channel_id=1, source_target_pairs={{0,1},{1,0},{2,3},{3,2},{4,5},{5,4},{6,7},{7,6},{8,9},{9,8},{10,11... | collective-permute-start | bytes 1966088 | tf_op jit(solution)/shard_map/ppermute | solution.py:309
  123.5 1.3 convert_reduce_fusion.1
  124.9 1.8 %collective-permute-start.10 = (bf16[40,384]{1,0:T(8,128)(2,1)S(1)}, bf16[40,384]{1,0:T(8,128)(2,1)S(1)}, u32[]{:S(2)}, u32[]{:S(2)}) collective-permute-start(bf16[40,384]{1,0:T(8,128)(2,1)S(1)} %fusion.13), channel_id=1, source_target_pairs={{0,4},{4,0},{8,12},{12,8},{16,20},{20,16},{24,28},{28,24},{32,36},... | collective-permute-start | bytes 92168 | tf_op jit(solution)/shard_map/ppermute | solution.py:264
  127.7 2.6 %collective-permute-start.9 = (bf16[256,1280]{1,0:T(8,128)(2,1)}, bf16[256,1280]{1,0:T(8,128)(2,1)S(1)}, u32[]{:S(2)}, u32[]{:S(2)}) collective-permute-start(bf16[256,1280]{1,0:T(8,128)(2,1)} %add_convert_fusion), channel_id=1, source_target_pairs={{0,2},{1,3},{2,0},{3,1},{4,6},{5,7},{6,4},{7,5},{8,10},{9,11},{10,... | collective-permute-start | bytes 1966088 | tf_op jit(solution)/shard_map/ppermute | solution.py:305
  131.3 13.6 %collective-permute-done.9 = bf16[256,1280]{1,0:T(8,128)(2,1)S(1)} collective-permute-done((bf16[256,1280]{1,0:T(8,128)(2,1)}, bf16[256,1280]{1,0:T(8,128)(2,1)S(1)}, u32[]{:S(2)}, u32[]{:S(2)}) %collective-permute-start.9) | collective-permute-done | bytes 655392 | tf_op jit(solution)/shard_map/ppermute | solution.py:305
  144.9 1.7 %fusion.19 = (f32[256]{0:T(256)S(1)}, f32[256]{0:T(256)S(1)}, f32[256,1280]{1,0:T(8,128)S(1)}) fusion(f32[256]{0:T(256)S(1)} %add_rsqrt_fusion, f32[256]{0:T(256)S(1)} %broadcast_multiply_fusion.2, bf16[256,1280]{1,0:T(8,128)(2,1)S(1)} %copy-done.13, f32[1280]{0:T(1024)S(1)} %copy-done.15, bf16[256,1280]{1,0:T(8,128)(2,1)S(1)} %collective-permute-done.9, ...), kind=kLoop, calls=%fused_computation.63 | loop fusion | flops 3603968 | bytes 4596736 | tf_op jit(solution)/shard_map/reduce_sum | solution.py:30
  (91 shorter events, 16.9 us)
Async XLA Ops:
  1.8 7.6 %collective-permute-start.3 = (bf16[40,960]{1,0:T(8,128)(2,1)S(1)}, bf16[40,960]{1,0:T(8,128)(2,1)S(1)}, u32[]{:S(2)}, u32[]{:S(2)}) collective-permute-start(bf16[40,960]{1,0:T(8,128)(2,1)S(1)} %concatenate.25), channel_id=1, source_target_pairs={{0,4},{4,0},{8,12},{12,8},{16,20},{20,16},{24,28},{28,24},{32,36},... | collective-permute-start | bytes 230408 | tf_op jit(solution)/shard_map/ppermute | solution.py:264
  6.7 29.9 %collective-permute-start.1 = (bf16[256,1280]{1,0:T(8,128)(2,1)}, bf16[256,1280]{1,0:T(8,128)(2,1)}, u32[]{:S(2)}, u32[]{:S(2)}) collective-permute-start(bf16[256,1280]{1,0:T(8,128)(2,1)} %fusion.6.refs_2_), channel_id=1, source_target_pairs={{0,2},{1,3},{2,0},{3,1},{4,6},{5,7},{6,4},{7,5},{8,10},{9,11},{10,... | collective-permute-start | bytes 1966088 | tf_op jit(solution)/shard_map/ppermute | solution.py:305
  10.8 7.7 %copy-start.14 = (bf16[384,1280]{1,0:T(8,128)(2,1)S(1)}, bf16[384,1280]{1,0:T(8,128)(2,1)}, u32[]{:S(2)}) copy-start(bf16[384,1280]{1,0:T(8,128)(2,1)} %param.10) | copy-start | bytes 2949124
  10.8 33.4 %all-to-all-start = ((bf16[16,80,576]{2,1,0:T(8,128)(2,1)}), bf16[16,80,576]{2,1,0:T(8,128)(2,1)S(1)}, u32[]{:S(2)}, u32[]{:S(2)}) async-start(bf16[16,80,576]{2,1,0:T(8,128)(2,1)} %broadcast_in_dim.10), calls=%async_computation | async-start | bytes 3276800 | tf_op jit(solution)/shard_map/all_to_all | solution.py:273
  19.3 17.8 %copy-start.17 = (s32[1024]{0:T(1024)S(1)}, s32[1024]{0:T(1024)}, u32[]{:S(2)}) copy-start(s32[1024]{0:T(1024)} %param.9) | copy-start | bytes 12292
  19.3 15.0 %collective-permute-start.5 = (bf16[384,640]{1,0:T(8,128)(2,1)}, bf16[384,640]{1,0:T(8,128)(2,1)S(1)}, u32[]{:S(2)}, u32[]{:S(2)}) collective-permute-start(bf16[384,640]{1,0:T(8,128)(2,1)} %constant_dynamic-slice_fusion.2), channel_id=1, source_target_pairs={{0,2},{1,3},{2,0},{3,1},{4,6},{5,7},{6,4},{7,5},{8,10},{9,11},{10,... | collective-permute-start | bytes 1474568 | tf_op jit(solution)/shard_map/ppermute | solution.py:305
  20.0 17.2 %collective-permute-start.4 = (bf16[384,320]{1,0:T(8,128)(2,1)S(1)}, bf16[384,320]{1,0:T(8,128)(2,1)S(1)}, u32[]{:S(2)}, u32[]{:S(2)}) collective-permute-start(bf16[384,320]{1,0:T(8,128)(2,1)S(1)} %get-tuple-element.26), channel_id=1, source_target_pairs={{0,1},{1,0},{2,3},{3,2},{4,5},{5,4},{6,7},{7,6},{8,9},{9,8},{10,11... | collective-permute-start | bytes 737288 | tf_op jit(solution)/shard_map/ppermute | solution.py:309
  34.6 3.1 %collective-permute-start.6 = (bf16[384,320]{1,0:T(8,128)(2,1)S(1)}, bf16[384,320]{1,0:T(8,128)(2,1)S(1)}, u32[]{:S(2)}, u32[]{:S(2)}) collective-permute-start(bf16[384,320]{1,0:T(8,128)(2,1)S(1)} %get-tuple-element.28), channel_id=1, source_target_pairs={{0,1},{1,0},{2,3},{3,2},{4,5},{5,4},{6,7},{7,6},{8,9},{9,8},{10,11... | collective-permute-start | bytes 737288 | tf_op jit(solution)/shard_map/ppermute | solution.py:309
  36.5 16.3 %collective-permute-start = (bf16[256,1280]{1,0:T(8,128)(2,1)}, bf16[256,1280]{1,0:T(8,128)(2,1)}, u32[]{:S(2)}, u32[]{:S(2)}) collective-permute-start(bf16[256,1280]{1,0:T(8,128)(2,1)} %fusion.6.refs_2_), channel_id=1, source_target_pairs={{0,1},{1,0},{2,3},{3,2},{4,5},{5,4},{6,7},{7,6},{8,9},{9,8},{10,11... | collective-permute-start | bytes 1966088 | tf_op jit(solution)/shard_map/ppermute | solution.py:309
  36.6 16.2 %collective-permute-start.2 = (bf16[256,1280]{1,0:T(8,128)(2,1)}, bf16[256,1280]{1,0:T(8,128)(2,1)}, u32[]{:S(2)}, u32[]{:S(2)}) collective-permute-start(bf16[256,1280]{1,0:T(8,128)(2,1)} %collective-permute-done.1.refs_4_), channel_id=1, source_target_pairs={{0,1},{1,0},{2,3},{3,2},{4,5},{5,4},{6,7},{7,6},{8,9},{9,8},{10,11... | collective-permute-start | bytes 1966088 | tf_op jit(solution)/shard_map/ppermute | solution.py:309
  44.2 8.7 %copy-start.5 = (s32[1,3]{1,0:T(1,128)S(1)}, s32[1,3]{1,0:T(1,128)}, u32[]{:S(2)}) copy-start(s32[1,3]{1,0:T(1,128)} %param.8) | copy-start | bytes 40
  45.2 25.7 %all-to-all-start.1 = ((bf16[16,80,384]{2,1,0:T(8,128)(2,1)}), bf16[16,80,384]{2,1,0:T(8,128)(2,1)S(1)}, u32[]{:S(2)}, u32[]{:S(2)}) async-start(bf16[16,80,384]{2,1,0:T(8,128)(2,1)} %broadcast_in_dim.9), calls=%async_computation.1 | async-start | bytes 1966080 | tf_op jit(solution)/shard_map/all_to_all | solution.py:273
  70.9 37.4 %copy-start.2 = (bf16[16,80,384]{2,1,0:T(8,128)(2,1)}, bf16[16,80,384]{2,1,0:T(8,128)(2,1)S(1)}, u32[]{:S(2)}) copy-start(bf16[16,80,384]{2,1,0:T(8,128)(2,1)S(1)} %all-to-all-done.1) | copy-start | bytes 2949124
  70.9 32.2 %all-to-all-start.3 = ((bf16[16,80,576]{2,1,0:T(8,128)(2,1)}), bf16[16,80,576]{2,1,0:T(8,128)(2,1)}, u32[]{:S(2)}, u32[]{:S(2)}) async-start(bf16[16,80,576]{2,1,0:T(8,128)(2,1)} %bitcast.23), calls=%async_computation.3 | async-start | bytes 3276800 | tf_op jit(solution)/shard_map/all_to_all | solution.py:279
  103.1 5.2 %copy-start.10 = (bf16[1024,384]{1,0:T(8,128)(2,1)S(1)}, bf16[1024,384]{1,0:T(8,128)(2,1)}, u32[]{:S(2)}) copy-start(bf16[1024,384]{1,0:T(8,128)(2,1)} %copy-done.9) | copy-start | bytes 2359300
  103.1 20.4 %all-to-all-start.2 = ((bf16[16,80,384]{2,1,0:T(8,128)(2,1)}), bf16[16,80,384]{2,1,0:T(8,128)(2,1)}, u32[]{:S(2)}, u32[]{:S(2)}) async-start(bf16[16,80,384]{2,1,0:T(8,128)(2,1)} %bitcast.56), calls=%async_computation.2 | async-start | bytes 1966080 | tf_op jit(solution)/shard_map/all_to_all | solution.py:279
  109.7 6.6 %copy-start.8 = (bf16[1024,576]{1,0:T(8,128)(2,1)S(1)}, bf16[1024,576]{1,0:T(8,128)(2,1)}, u32[]{:S(2)}) copy-start(bf16[1024,576]{1,0:T(8,128)(2,1)} %copy-done.6) | copy-start | bytes 3538948
  116.2 7.1 %collective-permute-start.11 = (bf16[40,576]{1,0:T(8,128)(2,1)S(1)}, bf16[40,576]{1,0:T(8,128)(2,1)S(1)}, u32[]{:S(2)}, u32[]{:S(2)}) collective-permute-start(bf16[40,576]{1,0:T(8,128)(2,1)S(1)} %fusion.12), channel_id=1, source_target_pairs={{0,4},{4,0},{8,12},{12,8},{16,20},{20,16},{24,28},{28,24},{32,36},... | collective-permute-start | bytes 138248 | tf_op jit(solution)/shard_map/ppermute | solution.py:264
  120.0 11.4 %collective-permute-start.7 = (bf16[256,1280]{1,0:T(8,128)(2,1)}, bf16[256,1280]{1,0:T(8,128)(2,1)}, u32[]{:S(2)}, u32[]{:S(2)}) collective-permute-start(bf16[256,1280]{1,0:T(8,128)(2,1)} %get-tuple-element.17), channel_id=1, source_target_pairs={{0,1},{1,0},{2,3},{3,2},{4,5},{5,4},{6,7},{7,6},{8,9},{9,8},{10,11... | collective-permute-start | bytes 1966088 | tf_op jit(solution)/shard_map/ppermute | solution.py:309
  123.4 3.3 %collective-permute-start.8 = (bf16[256,1280]{1,0:T(8,128)(2,1)}, bf16[256,1280]{1,0:T(8,128)(2,1)S(1)}, u32[]{:S(2)}, u32[]{:S(2)}) collective-permute-start(bf16[256,1280]{1,0:T(8,128)(2,1)} %get-tuple-element.19), channel_id=1, source_target_pairs={{0,1},{1,0},{2,3},{3,2},{4,5},{5,4},{6,7},{7,6},{8,9},{9,8},{10,11... | collective-permute-start | bytes 1966088 | tf_op jit(solution)/shard_map/ppermute | solution.py:309
  124.9 5.4 %collective-permute-start.10 = (bf16[40,384]{1,0:T(8,128)(2,1)S(1)}, bf16[40,384]{1,0:T(8,128)(2,1)S(1)}, u32[]{:S(2)}, u32[]{:S(2)}) collective-permute-start(bf16[40,384]{1,0:T(8,128)(2,1)S(1)} %fusion.13), channel_id=1, source_target_pairs={{0,4},{4,0},{8,12},{12,8},{16,20},{20,16},{24,28},{28,24},{32,36},... | collective-permute-start | bytes 92168 | tf_op jit(solution)/shard_map/ppermute | solution.py:264
  126.7 18.2 %copy-start.1 = (f32[256,1280]{1,0:T(8,128)S(1)}, f32[256,1280]{1,0:T(8,128)}, u32[]{:S(2)}) copy-start(f32[256,1280]{1,0:T(8,128)} %copy-done) | copy-start | bytes 3932164
  127.7 17.2 %copy-start.13 = (bf16[256,1280]{1,0:T(8,128)(2,1)S(1)}, bf16[256,1280]{1,0:T(8,128)(2,1)}, u32[]{:S(2)}) copy-start(bf16[256,1280]{1,0:T(8,128)(2,1)} %param.7) | copy-start | bytes 1966084
  127.7 17.2 %collective-permute-start.9 = (bf16[256,1280]{1,0:T(8,128)(2,1)}, bf16[256,1280]{1,0:T(8,128)(2,1)S(1)}, u32[]{:S(2)}, u32[]{:S(2)}) collective-permute-start(bf16[256,1280]{1,0:T(8,128)(2,1)} %add_convert_fusion), channel_id=1, source_target_pairs={{0,2},{1,3},{2,0},{3,1},{4,6},{5,7},{6,4},{7,5},{8,10},{9,11},{10,... | collective-permute-start | bytes 1966088 | tf_op jit(solution)/shard_map/ppermute | solution.py:305
  (12 other events, 25.8 us)

commit v9 on v7

--- a/solution.py
+++ b/solution.py
@@ -186,30 +186,41 @@
 SM = pl.BlockSpec(memory_space=pltpu.SMEM)
 
 
-def attention(heads, lengths, place, pieces, weight, out_grad):
+def attention(heads, lengths, place, pieces, weight, out_grad, before=()):
     features, columns = weight.shape
     rows = out_grad.shape[0]
     count = len(heads)
     tall = pltpu.VMEM((count, rows, 128), BF16)
     wide = pltpu.VMEM((count, rows, QB), F32)
-    body = lambda *refs: attention_kernel(heads, *refs)
+    out_shape = [
+        jax.ShapeDtypeStruct((rows, columns), BF16),
+        jax.ShapeDtypeStruct((features, columns), BF16),
+    ]
+    if before:
+        out_shape += [jax.ShapeDtypeStruct((ROWS, features), F32), jax.ShapeDtypeStruct((ROWS, features), BF16)]
+
+    def body(*refs):
+        inputs, rest = refs[:8], refs[8:]
+        first, rest = rest[:len(before)], rest[len(before):]
+        outs, scratch = rest[:len(out_shape)], rest[len(out_shape):]
+        attention_kernel(heads, *inputs, *outs[:2], *scratch)
+        if before:
+            norm_grad_kernel(2, 3, inputs[1], first[0], outs[0], first[1], inputs[6], *outs[2:])
+
     return pl.pallas_call(
         body,
-        out_shape=(
-            jax.ShapeDtypeStruct((rows, columns), BF16),
-            jax.ShapeDtypeStruct((features, columns), BF16),
-        ),
-        in_specs=[SM, SM] + [VM] * 6,
-        out_specs=(VM, VM),
+        out_shape=tuple(out_shape),
+        in_specs=[SM, SM] + [VM] * (6 + len(before)),
+        out_specs=(VM,) * len(out_shape),
         scratch_shapes=[pltpu.VMEM((rows, features), BF16)] + [tall] * 6 + [
             wide, wide, pltpu.VMEM((count, rows, 128), F32), pltpu.VMEM(((count + 1) // 2, QB, 128), F32)
         ],
-        compiler_params=pltpu.CompilerParams(vmem_limit_bytes=(12 + 5 * count) << 20),
+        compiler_params=pltpu.CompilerParams(vmem_limit_bytes=(12 + 5 * count + 4 * len(before)) << 20),
         cost_estimate=pl.CostEstimate(
             flops=5_000_000_000 * count, bytes_accessed=8_000_000, transcendentals=1_000_000 * count
         ),
         name="attention_backward",
-    )(lengths, place, *pieces, weight, out_grad)
+    )(lengths, place, *pieces, weight, out_grad, *before)
 
 
 def norm_grad_kernel(keep_at, give_at, place, grad_0, grad_1, weight_0, weight_1, keep_ref, give_ref):
@@ -336,11 +347,12 @@
     pieces = (own, near, far, far_near)
     at = place.reshape(1)
     grads, terms = [], []
-    for heads, weight in zip(CHUNKS, weights):
-        grad, term = attention(heads, rec_lengths[0], at, pieces, weight, out_grad)
+    for n, (heads, weight) in enumerate(zip(CHUNKS, weights)):
+        before = (grads[0], weights[0]) if n else ()
+        grad, term, *far_sums = attention(heads, rec_lengths[0], at, pieces, weight, out_grad, before)
         grads.append(grad)
         terms.append(exchange_terms(term))
-    keep, give = norm_grad_blocks(2, 3, at, grads, weights)
+    keep, give = far_sums
     got = swap_core(give)
     side_sum = swap_side((keep + got.astype(F32)).astype(BF16))
     keep, give = norm_grad_blocks(0, 1, at, grads, weights)

time: 147 us -> 154 us (1.048)
  the two profiles are of different devices: /device:TPU:6 before, /device:TPU:24 now
where the time goes in v9:
time: 154 us; the launch traced here: 153 us
  Pallas kernels  41.8 us (27%)
  starting transfers between devices  40.6 us (26%)
  waiting for transfers between devices  34.8 us (23%)
  local copies, waits for them, and re-layouts  22.5 us (15%)
  other arithmetic  12.1 us (8%)
    pallas_call x2, Pallas kernels, attention(): pl.pallas_call(body, out_shape=tuple(out_shape), in_specs=[SM, SM] + [VM]...  39.4 us
    ppermute x3, waiting for transfers between devices, swap_side(): return lax.ppermute(block, 'frame', FRAME_SIDE)  27.7 us
    all_to_all x2, starting transfers between devices, gather_plane(): lax.all_to_all(spread, 'dp', 0, 0, axis_index_groups=plane_groups(groups)...  15.9 us
    all_to_all x2, starting transfers between devices, exchange_terms(): lax.all_to_all(term.reshape(groups // 2, term.shape[0] * 2 // groups, ter...  12.8 us
    unnamed x42, local copies, waits for them, and re-layouts  10.9 us
    all_to_all x2, waiting for transfers between devices, exchange_terms(): lax.all_to_all(term.reshape(groups // 2, term.shape[0] * 2 // groups, ter...  6.22 us
    ppermute x3, starting transfers between devices, swap_pair(): return lax.ppermute(block, 'dp', [(i, i ^ 1) for i in range(groups)])  5.85 us
    gather x1, local copies, waits for them, and re-layouts, per_device(): out_grad = grad_tiles(jnp.take(moved, rows_at, axis=0, mode='clip'))  4.98 us
  transfers between devices with their start and end apart: 16, of which 6 were waited for; matrix products, arithmetic and copies ran while one was open for 12% of the time, Pallas kernels for 27%

profile of v9, /device:TPU:24, one launch (start us, length us, event | category | flops | bytes accessed | tf_op | source)
XLA Modules:
  0.0 152.8 jit_solution(7454535058785887495)
XLA Ops:
  2.6 1.3 convert_reduce_fusion.2
  6.3 1.3 broadcast_in_dim.10
  7.7 8.0 %all-to-all-start = ((bf16[16,80,576]{2,1,0:T(8,128)(2,1)}), bf16[16,80,576]{2,1,0:T(8,128)(2,1)S(1)}, u32[]{:S(2)}, u32[]{:S(2)}) async-start(bf16[16,80,576]{2,1,0:T(8,128)(2,1)} %broadcast_in_dim.10), calls=%async_computation | async-start | bytes 3276800 | tf_op jit(solution)/shard_map/all_to_all | solution.py:279
  16.6 2.6 %collective-permute-start.5 = (bf16[384,640]{1,0:T(8,128)(2,1)}, bf16[384,640]{1,0:T(8,128)(2,1)S(1)}, u32[]{:S(2)}, u32[]{:S(2)}) collective-permute-start(bf16[384,640]{1,0:T(8,128)(2,1)} %constant_dynamic-slice_fusion.2), channel_id=1, source_target_pairs={{0,2},{1,3},{2,0},{3,1},{4,6},{5,7},{6,4},{7,5},{8,10},{9,11},{10,... | collective-permute-start | bytes 1474568 | tf_op jit(solution)/shard_map/ppermute | solution.py:311
  19.5 14.3 %collective-permute-done.5 = bf16[384,640]{1,0:T(8,128)(2,1)S(1)} collective-permute-done((bf16[384,640]{1,0:T(8,128)(2,1)}, bf16[384,640]{1,0:T(8,128)(2,1)S(1)}, u32[]{:S(2)}, u32[]{:S(2)}) %collective-permute-start.5) | collective-permute-done | bytes 491552 | tf_op jit(solution)/shard_map/ppermute | solution.py:311
  35.9 5.0 %gather_fusion = bf16[1024,320]{1,0:T(8,128)(2,1)} fusion(bf16[1536,320]{1,0:T(8,128)(2,1)S(1)} %pad_maximum_fusion, s32[1024]{0:T(1024)S(1)} %fusion.17), kind=kCustom, calls=%fused_computation | custom fusion | bytes 1314816 | tf_op jit(solution)/shard_map/jit(_take)/gather | solution.py:346
  43.4 7.9 %all-to-all-start.1 = ((bf16[16,80,384]{2,1,0:T(8,128)(2,1)}), bf16[16,80,384]{2,1,0:T(8,128)(2,1)S(1)}, u32[]{:S(2)}, u32[]{:S(2)}) async-start(bf16[16,80,384]{2,1,0:T(8,128)(2,1)} %broadcast_in_dim.9), calls=%async_computation.1 | async-start | bytes 1966080 | tf_op jit(solution)/shard_map/all_to_all | solution.py:279
  51.3 21.1 %attention_backward.2 = (bf16[1024,576]{1,0:T(8,128)(2,1)S(1)}, bf16[1280,576]{1,0:T(8,128)(2,1)}) custom-call(s32[3]{0:T(128)S(1)} %bitcast.56, s32[1]{0:T(128)} %bitcast.refs_1_.refs_0_, bf16[256,1280]{1,0:T(8,128)(2,1)} %fusion.6.refs_2_, bf16[256,1280]{1,0:T(8,128)(2,1)} %collective-permute-done.refs_3_, ...), custom_call_target="tpu_custom_call" | custom-call | flops 15000000512 | bytes 8000000 | tf_op jit(solution)/shard_map/attention_backward/pallas_call | solution.py:210
  74.5 6.7 %all-to-all-start.3 = ((bf16[16,80,576]{2,1,0:T(8,128)(2,1)}), bf16[16,80,576]{2,1,0:T(8,128)(2,1)}, u32[]{:S(2)}, u32[]{:S(2)}) async-start(bf16[16,80,576]{2,1,0:T(8,128)(2,1)} %bitcast.23), calls=%async_computation.3 | async-start | bytes 3276800 | tf_op jit(solution)/shard_map/all_to_all | solution.py:285
  83.5 1.3 copy-done.10
  84.8 18.3 %attention_backward.3 = (bf16[1024,384]{1,0:T(8,128)(2,1)S(1)}, bf16[1280,384]{1,0:T(8,128)(2,1)S(1)}, f32[256,1280]{1,0:T(8,128)S(1)}, bf16[256,1280]{1,0:T(8,128)(2,1)}) custom-call(s32[3]{0:T(128)S(1)} %bitcast.57, s32[1]{0:T(128)} %bitcast.refs_1_.refs_0_, bf16[256,1280]{1,0:T(8,128)(2,1)} %fusion.6.refs_2_, ...), custom_call_target="tpu_custom_call" | custom-call | flops 10000000000 | bytes 8000000 | tf_op jit(solution)/shard_map/attention_backward/pallas_call | solution.py:210
  105.5 6.2 %all-to-all-start.2 = ((bf16[16,80,384]{2,1,0:T(8,128)(2,1)}), bf16[16,80,384]{2,1,0:T(8,128)(2,1)}, u32[]{:S(2)}, u32[]{:S(2)}) async-start(bf16[16,80,384]{2,1,0:T(8,128)(2,1)} %bitcast.53), calls=%async_computation.2 | async-start | bytes 1966080 | tf_op jit(solution)/shard_map/all_to_all | solution.py:285
  111.7 1.8 %convert_reduce_fusion = f32[80,576]{1,0:T(8,128)S(1)} fusion(bf16[16,80,576]{2,1,0:T(8,128)(2,1)} %all-to-all-done.3), kind=kLoop, calls=%fused_computation.1 | loop fusion | flops 1428480 | bytes 1658880 | tf_op jit(solution)/shard_map/reduce_sum | solution.py:293
  113.5 2.5 %collective-permute-start.11 = (bf16[40,576]{1,0:T(8,128)(2,1)S(1)}, bf16[40,576]{1,0:T(8,128)(2,1)S(1)}, u32[]{:S(2)}, u32[]{:S(2)}) collective-permute-start(bf16[40,576]{1,0:T(8,128)(2,1)S(1)} %fusion.12), channel_id=1, source_target_pairs={{0,4},{4,0},{8,12},{12,8},{16,20},{20,16},{24,28},{28,24},{32,36},... | collective-permute-start | bytes 138248 | tf_op jit(solution)/shard_map/ppermute | solution.py:270
  116.0 1.3 copy-done.11
  117.4 2.4 %norm_grad.1 = (f32[256,1280]{1,0:T(8,128)S(1)}, bf16[256,1280]{1,0:T(8,128)(2,1)}) custom-call(s32[1]{0:T(128)} %bitcast.refs_1_.refs_0_, bf16[1024,576]{1,0:T(8,128)(2,1)S(1)} %copy-done.11, bf16[1024,384]{1,0:T(8,128)(2,1)S(1)} %copy-done.13, bf16[1280,576]{1,0:T(8,128)(2,1)S(1)} %bitcast.52, bf16[1280,384]{1,0:T(8,128)(2,1)S(1)} %bitcast.55), custom_call_target="tpu_custom_call" | custom-call | flops 1300000000 | bytes 6000000 | tf_op jit(solution)/shard_map/norm_grad/pallas_call | solution.py:237
  121.5 5.8 %all-to-all-done.2 = bf16[16,80,384]{2,1,0:T(8,128)(2,1)} async-done(((bf16[16,80,384]{2,1,0:T(8,128)(2,1)}), bf16[16,80,384]{2,1,0:T(8,128)(2,1)}, u32[]{:S(2)}, u32[]{:S(2)}) %all-to-all-start.2) | async-done | bytes 983072 | tf_op jit(solution)/shard_map/all_to_all | solution.py:285
  127.3 1.3 convert_reduce_fusion.1
  128.7 2.5 %collective-permute-start.10 = (bf16[40,384]{1,0:T(8,128)(2,1)S(1)}, bf16[40,384]{1,0:T(8,128)(2,1)S(1)}, u32[]{:S(2)}, u32[]{:S(2)}) collective-permute-start(bf16[40,384]{1,0:T(8,128)(2,1)S(1)} %fusion.13), channel_id=1, source_target_pairs={{0,4},{4,0},{8,12},{12,8},{16,20},{20,16},{24,28},{28,24},{32,36},... | collective-permute-start | bytes 92168 | tf_op jit(solution)/shard_map/ppermute | solution.py:270
  132.0 2.1 %add_convert_fusion = bf16[256,1280]{1,0:T(8,128)(2,1)} fusion(f32[256,1280]{1,0:T(8,128)S(1)} %get-tuple-element.18, bf16[256,1280]{1,0:T(8,128)(2,1)} %copy-done.17), kind=kLoop, calls=%fused_computation.18 | loop fusion | flops 983040 | bytes 2621440 | tf_op jit(solution)/shard_map/convert_element_type | solution.py:357
  134.1 1.2 collective-permute-start.9
  136.4 13.4 %collective-permute-done.9 = bf16[256,1280]{1,0:T(8,128)(2,1)S(1)} collective-permute-done((bf16[256,1280]{1,0:T(8,128)(2,1)}, bf16[256,1280]{1,0:T(8,128)(2,1)S(1)}, u32[]{:S(2)}, u32[]{:S(2)}) %collective-permute-start.9) | collective-permute-done | bytes 655392 | tf_op jit(solution)/shard_map/ppermute | solution.py:311
  149.9 1.7 %fusion.19 = (f32[256]{0:T(256)S(1)}, f32[256]{0:T(256)S(1)}, f32[256,1280]{1,0:T(8,128)S(1)}) fusion(f32[256]{0:T(256)S(1)} %add_rsqrt_fusion, f32[256]{0:T(256)S(1)} %broadcast_multiply_fusion.2, bf16[256,1280]{1,0:T(8,128)(2,1)S(1)} %copy-done.15, f32[1280]{0:T(1024)S(1)} %copy-done.18, bf16[256,1280]{1,0:T(8,128)(2,1)S(1)} %collective-permute-done.9, ...), kind=kLoop, calls=%fused_computation.63 | loop fusion | flops 3603968 | bytes 4596736 | tf_op jit(solution)/shard_map/reduce_sum | solution.py:30
  151.5 1.3 fusion.10
  (96 shorter events, 20.5 us)
Async XLA Ops:
  1.8 4.5 %collective-permute-start.3 = (bf16[40,960]{1,0:T(8,128)(2,1)S(1)}, bf16[40,960]{1,0:T(8,128)(2,1)S(1)}, u32[]{:S(2)}, u32[]{:S(2)}) collective-permute-start(bf16[40,960]{1,0:T(8,128)(2,1)S(1)} %concatenate.25), channel_id=1, source_target_pairs={{0,4},{4,0},{8,12},{12,8},{16,20},{20,16},{24,28},{28,24},{32,36},... | collective-permute-start | bytes 230408 | tf_op jit(solution)/shard_map/ppermute | solution.py:270
  5.4 29.3 %collective-permute-start.1 = (bf16[256,1280]{1,0:T(8,128)(2,1)}, bf16[256,1280]{1,0:T(8,128)(2,1)}, u32[]{:S(2)}, u32[]{:S(2)}) collective-permute-start(bf16[256,1280]{1,0:T(8,128)(2,1)} %fusion.6.refs_2_), channel_id=1, source_target_pairs={{0,2},{1,3},{2,0},{3,1},{4,6},{5,7},{6,4},{7,5},{8,10},{9,11},{10,... | collective-permute-start | bytes 1966088 | tf_op jit(solution)/shard_map/ppermute | solution.py:311
  7.7 8.0 %copy-start.16 = (bf16[384,1280]{1,0:T(8,128)(2,1)S(1)}, bf16[384,1280]{1,0:T(8,128)(2,1)}, u32[]{:S(2)}) copy-start(bf16[384,1280]{1,0:T(8,128)(2,1)} %param.10) | copy-start | bytes 2949124
  7.7 34.6 %all-to-all-start = ((bf16[16,80,576]{2,1,0:T(8,128)(2,1)}), bf16[16,80,576]{2,1,0:T(8,128)(2,1)S(1)}, u32[]{:S(2)}, u32[]{:S(2)}) async-start(bf16[16,80,576]{2,1,0:T(8,128)(2,1)} %broadcast_in_dim.10), calls=%async_computation | async-start | bytes 3276800 | tf_op jit(solution)/shard_map/all_to_all | solution.py:279
  16.6 18.3 %copy-start.20 = (s32[1024]{0:T(1024)S(1)}, s32[1024]{0:T(1024)}, u32[]{:S(2)}) copy-start(s32[1024]{0:T(1024)} %param.9) | copy-start | bytes 12292
  16.6 17.2 %collective-permute-start.5 = (bf16[384,640]{1,0:T(8,128)(2,1)}, bf16[384,640]{1,0:T(8,128)(2,1)S(1)}, u32[]{:S(2)}, u32[]{:S(2)}) collective-permute-start(bf16[384,640]{1,0:T(8,128)(2,1)} %constant_dynamic-slice_fusion.2), channel_id=1, source_target_pairs={{0,2},{1,3},{2,0},{3,1},{4,6},{5,7},{6,4},{7,5},{8,10},{9,11},{10,... | collective-permute-start | bytes 1474568 | tf_op jit(solution)/shard_map/ppermute | solution.py:311
  19.4 15.5 %collective-permute-start.4 = (bf16[384,320]{1,0:T(8,128)(2,1)S(1)}, bf16[384,320]{1,0:T(8,128)(2,1)S(1)}, u32[]{:S(2)}, u32[]{:S(2)}) collective-permute-start(bf16[384,320]{1,0:T(8,128)(2,1)S(1)} %get-tuple-element.26), channel_id=1, source_target_pairs={{0,1},{1,0},{2,3},{3,2},{4,5},{5,4},{6,7},{7,6},{8,9},{9,8},{10,11... | collective-permute-start | bytes 737288 | tf_op jit(solution)/shard_map/ppermute | solution.py:315
  34.1 1.7 %collective-permute-start.6 = (bf16[384,320]{1,0:T(8,128)(2,1)S(1)}, bf16[384,320]{1,0:T(8,128)(2,1)S(1)}, u32[]{:S(2)}, u32[]{:S(2)}) collective-permute-start(bf16[384,320]{1,0:T(8,128)(2,1)S(1)} %get-tuple-element.28), channel_id=1, source_target_pairs={{0,1},{1,0},{2,3},{3,2},{4,5},{5,4},{6,7},{7,6},{8,9},{9,8},{10,11... | collective-permute-start | bytes 737288 | tf_op jit(solution)/shard_map/ppermute | solution.py:315
  34.2 17.1 %collective-permute-start = (bf16[256,1280]{1,0:T(8,128)(2,1)}, bf16[256,1280]{1,0:T(8,128)(2,1)}, u32[]{:S(2)}, u32[]{:S(2)}) collective-permute-start(bf16[256,1280]{1,0:T(8,128)(2,1)} %fusion.6.refs_2_), channel_id=1, source_target_pairs={{0,1},{1,0},{2,3},{3,2},{4,5},{5,4},{6,7},{7,6},{8,9},{9,8},{10,11... | collective-permute-start | bytes 1966088 | tf_op jit(solution)/shard_map/ppermute | solution.py:315
  34.7 16.6 %collective-permute-start.2 = (bf16[256,1280]{1,0:T(8,128)(2,1)}, bf16[256,1280]{1,0:T(8,128)(2,1)}, u32[]{:S(2)}, u32[]{:S(2)}) collective-permute-start(bf16[256,1280]{1,0:T(8,128)(2,1)} %collective-permute-done.1.refs_4_), channel_id=1, source_target_pairs={{0,1},{1,0},{2,3},{3,2},{4,5},{5,4},{6,7},{7,6},{8,9},{9,8},{10,11... | collective-permute-start | bytes 1966088 | tf_op jit(solution)/shard_map/ppermute | solution.py:315
  42.2 9.1 %copy-start.6 = (bf16[1024,384]{1,0:T(8,128)(2,1)}, bf16[1024,384]{1,0:T(8,128)(2,1)S(1)}, u32[]{:S(2)}) copy-start(bf16[1024,384]{1,0:T(8,128)(2,1)S(1)} %pad_maximum_fusion.1.refs_7_) | copy-start | bytes 2359300
  42.2 9.1 %copy-start.8 = (s32[1,3]{1,0:T(1,128)S(1)}, s32[1,3]{1,0:T(1,128)}, u32[]{:S(2)}) copy-start(s32[1,3]{1,0:T(1,128)} %param.8) | copy-start | bytes 40
  43.4 30.1 %all-to-all-start.1 = ((bf16[16,80,384]{2,1,0:T(8,128)(2,1)}), bf16[16,80,384]{2,1,0:T(8,128)(2,1)S(1)}, u32[]{:S(2)}, u32[]{:S(2)}) async-start(bf16[16,80,384]{2,1,0:T(8,128)(2,1)} %broadcast_in_dim.9), calls=%async_computation.1 | async-start | bytes 1966080 | tf_op jit(solution)/shard_map/all_to_all | solution.py:279
  74.5 31.0 %all-to-all-start.3 = ((bf16[16,80,576]{2,1,0:T(8,128)(2,1)}), bf16[16,80,576]{2,1,0:T(8,128)(2,1)}, u32[]{:S(2)}, u32[]{:S(2)}) async-start(bf16[16,80,576]{2,1,0:T(8,128)(2,1)} %bitcast.23), calls=%async_computation.3 | async-start | bytes 3276800 | tf_op jit(solution)/shard_map/all_to_all | solution.py:285
  105.5 21.8 %all-to-all-start.2 = ((bf16[16,80,384]{2,1,0:T(8,128)(2,1)}), bf16[16,80,384]{2,1,0:T(8,128)(2,1)}, u32[]{:S(2)}, u32[]{:S(2)}) async-start(bf16[16,80,384]{2,1,0:T(8,128)(2,1)} %bitcast.53), calls=%async_computation.2 | async-start | bytes 1966080 | tf_op jit(solution)/shard_map/all_to_all | solution.py:285
  111.7 4.4 %copy-start.5 = (bf16[16,80,384]{2,1,0:T(8,128)(2,1)S(1)}, bf16[16,80,384]{2,1,0:T(8,128)(2,1)}, u32[]{:S(2)}) copy-start(bf16[16,80,384]{2,1,0:T(8,128)(2,1)} %copy-done.3) | copy-start | bytes 2949124
  111.7 4.4 %copy-start.13 = (bf16[1024,384]{1,0:T(8,128)(2,1)S(1)}, bf16[1024,384]{1,0:T(8,128)(2,1)}, u32[]{:S(2)}) copy-start(bf16[1024,384]{1,0:T(8,128)(2,1)} %copy-done.12) | copy-start | bytes 2359300
  113.5 7.8 %collective-permute-start.11 = (bf16[40,576]{1,0:T(8,128)(2,1)S(1)}, bf16[40,576]{1,0:T(8,128)(2,1)S(1)}, u32[]{:S(2)}, u32[]{:S(2)}) collective-permute-start(bf16[40,576]{1,0:T(8,128)(2,1)S(1)} %fusion.12), channel_id=1, source_target_pairs={{0,4},{4,0},{8,12},{12,8},{16,20},{20,16},{24,28},{28,24},{32,36},... | collective-permute-start | bytes 138248 | tf_op jit(solution)/shard_map/ppermute | solution.py:270
  120.8 15.6 %collective-permute-start.7 = (bf16[256,1280]{1,0:T(8,128)(2,1)}, bf16[256,1280]{1,0:T(8,128)(2,1)}, u32[]{:S(2)}, u32[]{:S(2)}) collective-permute-start(bf16[256,1280]{1,0:T(8,128)(2,1)} %get-tuple-element.17), channel_id=1, source_target_pairs={{0,1},{1,0},{2,3},{3,2},{4,5},{5,4},{6,7},{7,6},{8,9},{9,8},{10,11... | collective-permute-start | bytes 1966088 | tf_op jit(solution)/shard_map/ppermute | solution.py:315
  120.8 10.3 %collective-permute-start.8 = (bf16[256,1280]{1,0:T(8,128)(2,1)}, bf16[256,1280]{1,0:T(8,128)(2,1)S(1)}, u32[]{:S(2)}, u32[]{:S(2)}) collective-permute-start(bf16[256,1280]{1,0:T(8,128)(2,1)} %get-tuple-element.19), channel_id=1, source_target_pairs={{0,1},{1,0},{2,3},{3,2},{4,5},{5,4},{6,7},{7,6},{8,9},{9,8},{10,11... | collective-permute-start | bytes 1966088 | tf_op jit(solution)/shard_map/ppermute | solution.py:315
  128.7 6.7 %collective-permute-start.10 = (bf16[40,384]{1,0:T(8,128)(2,1)S(1)}, bf16[40,384]{1,0:T(8,128)(2,1)S(1)}, u32[]{:S(2)}, u32[]{:S(2)}) collective-permute-start(bf16[40,384]{1,0:T(8,128)(2,1)S(1)} %fusion.13), channel_id=1, source_target_pairs={{0,4},{4,0},{8,12},{12,8},{16,20},{20,16},{24,28},{28,24},{32,36},... | collective-permute-start | bytes 92168 | tf_op jit(solution)/shard_map/ppermute | solution.py:270
  132.0 17.9 %copy-start.1 = (f32[256,1280]{1,0:T(8,128)S(1)}, f32[256,1280]{1,0:T(8,128)}, u32[]{:S(2)}) copy-start(f32[256,1280]{1,0:T(8,128)} %copy-done) | copy-start | bytes 3932164
  134.1 15.7 %copy-start.15 = (bf16[256,1280]{1,0:T(8,128)(2,1)S(1)}, bf16[256,1280]{1,0:T(8,128)(2,1)}, u32[]{:S(2)}) copy-start(bf16[256,1280]{1,0:T(8,128)(2,1)} %param.7) | copy-start | bytes 1966084
  134.1 15.7 %collective-permute-start.9 = (bf16[256,1280]{1,0:T(8,128)(2,1)}, bf16[256,1280]{1,0:T(8,128)(2,1)S(1)}, u32[]{:S(2)}, u32[]{:S(2)}) collective-permute-start(bf16[256,1280]{1,0:T(8,128)(2,1)} %add_convert_fusion), channel_id=1, source_target_pairs={{0,2},{1,3},{2,0},{3,1},{4,6},{5,7},{6,4},{7,5},{8,10},{9,11},{10,... | collective-permute-start | bytes 1966088 | tf_op jit(solution)/shard_map/ppermute | solution.py:311
  (15 other events, 23.2 us)
